TPU v7x, 256 devices: a whole 4x4x8 slice. The times are simulated.
256 devices in a mesh: grp: 8 (over y, core), pan: 32 (over z, x).
Axes of the slice: x: 4, y: 4, z: 8, core: 2. Of those that a mesh axis runs over, the one named last changes fastest.
Arguments:
- anc_rows: bfloat16 [16384, 16384], P('grp', 'pan'), as said below
- row_home: int32 [128], replicated, may hold values from 0 to 127, as said below
- block_lists: int32 [8, 64], replicated, may hold values from 0 to 127, as said below
- front_blocks: int32 [8], replicated, may hold values from 32 to 64, as said below
- panel: bfloat16 [8, 8192, 768], P('grp', 'pan'), may hold values from -0.29882812 to 0.29882812
- pivot_inverse: bfloat16 [8, 768, 768], P('grp'), as said below
Outputs:
- cross_cov: bfloat16 [8, 8192, 768], P('grp', 'pan')
- pivot_cov: float32 [8, 768, 768], P('grp', 'pan')
Inputs may be any that keep to these rules, and one draw needn't show every extreme that they name: `row_home`: A permutation of 0 to 127; the 4 index blocks of each window [4 q, 4 q + 4) have their storage row blocks in one front group. `block_lists`: rising along each row; entries 2 * q to 2 * q + 1 lie in [4 * q, 4 * q + 4). `front_blocks`: some front has all 64 blocks. `anc_rows`: storage row block row_home[b] holds row block b of a symmetric matrix. `pivot_inverse`: lower triangular.
All inputs are finite; a program needn't handle non-finite values.
Results may differ from a plain program's by a relative error of at most 0.0095.
Values may be sent and summed in bfloat16 or wider, within the bound.
A program may use at most 128 MiB of HBM per device.

v0:
```python
import jax
import jax.numpy as jnp
from jax import lax
from jax.sharding import PartitionSpec as P

BLK = 128
P_SIZE = 768


def per_device(anc_rows, row_home, block_lists, front_blocks, panel, pivot_inverse):
    groups = lax.axis_size("grp")
    pan_count = lax.axis_size("pan")
    group_idx = lax.axis_index("grp")
    pan_idx = lax.axis_index("pan")
    block_count = row_home.shape[0]
    front_len = block_lists.shape[1]
    rb_local = front_len // pan_count
    cb_local = anc_rows.shape[1] // BLK
    stored_blocks = anc_rows.shape[0] // BLK
    contract = (((0,), (0,)), ((), ()))
    my_list = lax.dynamic_index_in_dim(block_lists, group_idx, 0, keepdims=False)
    column_table = block_lists.reshape(groups, pan_count, rb_local)
    column_pick = (
        lax.dynamic_index_in_dim(column_table, pan_idx, 1, keepdims=False) - cb_local * pan_idx
    )
    slot_block = jnp.argsort(row_home)
    owned_slots = lax.dynamic_slice_in_dim(slot_block, group_idx * stored_blocks, stored_blocks)
    wanted = jnp.any(owned_slots[None, :, None] == block_lists[:, None, :], axis=2)
    layered = anc_rows.reshape(stored_blocks, BLK, cb_local, BLK)[:, :, column_pick, :]
    layered = jnp.transpose(layered, (2, 0, 1, 3, 4))
    layered = jnp.where(wanted[:, :, None, None, None], layered, jnp.zeros_like(layered))
    outgoing = layered.reshape(groups, stored_blocks * BLK, rb_local * BLK)
    received = lax.all_to_all(outgoing, "grp", split_axis=0, concat_axis=0, tiled=True)
    picked = received.reshape(block_count, BLK, rb_local * BLK)
    sigma_cols = picked[row_home[my_list]].reshape(front_len * BLK, rb_local * BLK)
    my_blocks = pan_idx * rb_local + jnp.arange(rb_local, dtype=jnp.int32)
    front_live = lax.dynamic_index_in_dim(front_blocks, group_idx, 0, keepdims=False)
    alive_rows = jnp.repeat(my_blocks < front_live, BLK)
    inverse_pivot = pivot_inverse[0]
    scaled = jnp.dot(panel[0], inverse_pivot, preferred_element_type=jnp.float32)
    scaled = jnp.where(alive_rows[:, None], scaled, jnp.zeros_like(scaled)).astype(jnp.bfloat16)
    product = lax.dot_general(
        sigma_cols,
        lax.all_gather(scaled, "pan", axis=0, tiled=True),
        contract,
        preferred_element_type=jnp.float32,
    )
    cross = jnp.where(alive_rows[:, None], -product, jnp.zeros_like(product)).astype(jnp.bfloat16)
    pivot_rows = P_SIZE // pan_count
    summed = lax.psum(
        (-lax.dot_general(scaled, cross, contract, preferred_element_type=jnp.float32)).astype(
            jnp.bfloat16
        ),
        "pan",
    ).astype(jnp.float32)
    shared = lax.dynamic_slice_in_dim(summed, pan_idx * pivot_rows, pivot_rows, 0)
    own_columns = lax.dynamic_slice_in_dim(inverse_pivot, pan_idx * pivot_rows, pivot_rows, 1)
    triangle = lax.dot_general(
        own_columns, inverse_pivot, contract, preferred_element_type=jnp.float32
    )
    pivot = triangle + shared
    return (cross[None], pivot[None])


def solution(mesh):
    placed = (P("grp", "pan"), P(), P(), P(), P("grp", "pan", None), P("grp", None, None))
    return jax.shard_map(
        per_device,
        mesh=mesh,
        in_specs=placed,
        out_specs=(P("grp", "pan", None), P("grp", "pan", None)),
        check_vma=False,
    )
```

profile of v0, /device:TPU:70, one launch (start us, length us, event | category | flops | bytes accessed | tf_op | source)
XLA Modules:
  0.0 337.3 jit_solution(7931357291125570440)
XLA Ops:
  7.2 0.0 copy-start
  7.2 0.0 all-gather.2.cloned.1.call-start
  7.2 1.3 dynamic_slice.23
  8.6 0.7 add_compare_fusion
  9.2 0.1 broadcast_bitcast_fusion
  9.3 2.2 fusion.1
  11.5 0.0 all-gather.2.cloned.1.call-update
  11.5 0.8 copy.19
  12.3 0.1 copy.20
  12.4 0.1 reshape.93
  12.5 4.0 %reshape.116 = bf16[16,128,4,128]{3,2,1,0:T(4,128)(2,1)} reshape(bf16[2048,512]{1,0:T(8,128)(2,1)} %param.6) | data formatting | bytes 4194304 | tf_op jit(solution)/shard_map/reshape | solution.py:29
  16.5 2.1 copy.21
  18.6 0.0 copy-start.1
  18.7 0.0 copy-start.4
  18.7 4.7 %gather_fusion = bf16[16,16,128,128]{3,2,1,0:T(8,128)(2,1)} fusion(bf16[16,128,4,128]{3,1,2,0:T(8,128)(2,1)S(1)} %copy.21, s32[1024]{0:T(1024)S(1)} %pad_clamp_fusion.2), kind=kCustom, calls=%fused_computation | custom fusion | bytes 16777280 | tf_op jit(solution)/shard_map/gather | solution.py:29
  23.4 2.5 sort.17
  25.9 0.1 dynamic_slice.24
  26.0 0.3 compare_reduce_fusion
  26.2 7.5 %select_bitcast_fusion = bf16[8,16,128,2,128]{4,2,1,3,0:T(8,128)(2,1)} fusion(bf16[8,2,16,128,128]{4,3,2,1,0:T(8,128)(2,1)} %bitcast.47, pred[8,16]{1,0:T(8,128)(4,1)S(1)} %compare_reduce_fusion), kind=kLoop, calls=%fused_computation.3 | loop fusion | flops 4194304 | bytes 16777344 | tf_op jit(solution)/shard_map/jit(_where)/select_n | solution.py:31
  33.7 16.4 %copy.22 = bf16[8,16,128,2,128]{4,3,2,1,0:T(2,128)(2,1)} copy(bf16[8,16,128,2,128]{4,2,1,3,0:T(8,128)(2,1)} %select_bitcast_fusion) | data formatting | bytes 16777216 | tf_op jit(solution)/shard_map/jit(_where)/select_n | solution.py:31
  50.2 14.1 %reshape.88 = bf16[8,2048,256]{2,1,0:T(8,128)(2,1)} reshape(bf16[8,16,128,2,128]{4,3,2,1,0:T(2,128)(2,1)} %copy.22) | data formatting | bytes 16777216 | tf_op jit(solution)/shard_map/reshape | solution.py:32
  64.3 5.0 %all-to-all-start = ((bf16[8,2048,256]{2,1,0:T(8,128)(2,1)}), bf16[8,2048,256]{2,1,0:T(8,128)(2,1)}, u32[]{:S(2)}, u32[]{:S(2)}) async-start(bf16[8,2048,256]{2,1,0:T(8,128)(2,1)} %reshape.88), calls=%async_computation | async-start | bytes 16777216 | tf_op jit(solution)/shard_map/all_to_all | solution.py:33
  69.3 0.0 all-reduce.2.cloned.1.call-start
  69.4 0.8 gather_fusion.1
  70.2 93.7 %all-to-all-done = bf16[8,2048,256]{2,1,0:T(8,128)(2,1)} async-done(((bf16[8,2048,256]{2,1,0:T(8,128)(2,1)}), bf16[8,2048,256]{2,1,0:T(8,128)(2,1)}, u32[]{:S(2)}, u32[]{:S(2)}) %all-to-all-start) | async-done | bytes 8388640 | tf_op jit(solution)/shard_map/all_to_all | solution.py:33
  163.9 6.2 %gather_fusion.2 = bf16[64,128,256]{2,1,0:T(8,128)(2,1)} fusion(bf16[128,128,256]{2,1,0:T(8,128)(2,1)} %bitcast.6, s32[1024]{0:T(1024)S(1)} %pad_clamp_fusion), kind=kCustom, calls=%fused_computation.2 | custom fusion | bytes 8388864 | tf_op jit(solution)/shard_map/gather | solution.py:35
  170.1 9.3 %fusion.2 = bf16[256,768]{1,0:T(8,128)(2,1)S(1)} fusion(bf16[8192,256]{1,0:T(8,128)(2,1)} %bitcast.48, bf16[8192,768]{1,0:T(8,128)(2,1)} %all-gather.2.cloned.1.call-done, pred[256]{0:T(512)(128)(4,1)S(1)} %broadcast_bitcast_fusion), kind=kOutput, calls=%fused_computation.9 | convolution fusion | flops 3221815296 | bytes 17170688 | tf_op jit(solution)/shard_map/dot_general | solution.py:42
  179.4 0.0 copy-start.3
  179.4 1.6 negate_convert_fusion
  181.0 0.0 all-reduce.2.cloned.1.call-update
  181.0 147.6 %all-reduce.2.cloned.1.call-done = bf16[768,768]{1,0:T(8,128)(2,1)} async-done(((bf16[768,768]{1,0:T(8,128)(2,1)}), bf16[768,768]{1,0:T(8,128)(2,1)}) %all-reduce.2.cloned.1.call-update) | async-done | bytes 1179664 | tf_op jit(solution)/shard_map/psum | solution.py:50
  328.6 1.8 fusion.9
  (14 shorter events, 0.1 us)
Async XLA Ops:
  7.2 2.1 copy-start
  7.2 162.9 %all-gather.2.cloned.1.call-start = ((), (), s32[]{:S(2)}) async-start(), calls=%async_computation.1 | async-start | bytes 12976128 | tf_op jit(solution)/shard_map/all_gather | solution.py:44
  18.6 4.7 %copy-start.1 = (s32[128]{0:T(128)S(1)}, s32[128]{0:T(128)}, u32[]{:S(2)}) copy-start(s32[128]{0:T(128)} %param.7) | copy-start | bytes 1540
  18.7 7.3 %copy-start.4 = (s32[8,64]{1,0:T(8,128)S(1)}, s32[8,64]{1,0:T(8,128)}, u32[]{:S(2)}) copy-start(s32[8,64]{1,0:T(8,128)} %param.8) | copy-start | bytes 6148
  64.3 99.6 %all-to-all-start = ((bf16[8,2048,256]{2,1,0:T(8,128)(2,1)}), bf16[8,2048,256]{2,1,0:T(8,128)(2,1)}, u32[]{:S(2)}, u32[]{:S(2)}) async-start(bf16[8,2048,256]{2,1,0:T(8,128)(2,1)} %reshape.88), calls=%async_computation | async-start | bytes 16777216 | tf_op jit(solution)/shard_map/all_to_all | solution.py:33
  69.3 259.3 %all-reduce.2.cloned.1.call-start = ((), (), s32[]{:S(2)}) async-start(), calls=%async_computation.2 | async-start | bytes 2359296 | tf_op jit(solution)/shard_map/psum | solution.py:50
  170.1 9.3 %copy-start.2 = (bf16[256,768]{1,0:T(8,128)(2,1)S(1)}, bf16[256,768]{1,0:T(8,128)(2,1)}, u32[]{:S(2)}) copy-start(bf16[256,768]{1,0:T(8,128)(2,1)} %fusion.1) | copy-start | bytes 1179652
  179.4 151.0 %copy-start.3 = (bf16[256,768]{1,0:T(8,128)(2,1)}, bf16[256,768]{1,0:T(8,128)(2,1)S(1)}, u32[]{:S(2)}) copy-start(bf16[256,768]{1,0:T(8,128)(2,1)S(1)} %fusion.2) | copy-start | bytes 1179652
Sparse Core Ops, SparseCore 0:
  11.7 119.3 all-gather.1
  181.2 147.4 all-reduce.1
where the time goes:
time: 341 us; the launch traced here: 337 us
  waiting for transfers between devices  241 us (71%)
  local copies, waits for them, and re-layouts  50.7 us (15%)
  matrix products  14.9 us (4%)
  between operations  14.2 us (4%)
  other arithmetic  11 us (3%)
  starting transfers between devices  5.1 us (1%)
    psum x1, waiting for transfers between devices, per_device(): lax.psum((-lax.dot_general(scaled, cross, contract, preferred_element_typ...  148 us
    all_to_all x1, waiting for transfers between devices, per_device(): lax.all_to_all(outgoing, 'grp', split_axis=0, concat_axis=0, tiled=True)  93.7 us
    select_n x1, local copies, waits for them, and re-layouts, per_device(): jnp.where(wanted[:, :, None, None, None], layered, jnp.zeros_like(layered))  16.4 us
    reshape x1, local copies, waits for them, and re-layouts, per_device(): outgoing = layered.reshape(groups, stored_blocks * BLK, rb_local * BLK)  14.1 us
    dot_general x1, matrix products, per_device(): lax.dot_general(sigma_cols, lax.all_gather(scaled, 'pan', axis=0, tiled=T...  9.33 us
    select_n x1, other arithmetic, per_device(): jnp.where(wanted[:, :, None, None, None], layered, jnp.zeros_like(layered))  7.5 us
  transfers between devices with their start and end apart: 3, of which 2 were waited for; matrix products, arithmetic and copies ran while one was open for 18% of the time, Pallas kernels for 0%

commit v1 on v0

v1 whole, which is shorter than its diff:
```python
import jax
import jax.numpy as jnp
from jax import lax
from jax.sharding import PartitionSpec as P

BLK = 128
P_SIZE = 768


def per_device(anc_rows, row_home, block_lists, front_blocks, panel, pivot_inverse):
    groups = lax.axis_size("grp")
    pan_count = lax.axis_size("pan")
    group_idx = lax.axis_index("grp")
    pan_idx = lax.axis_index("pan")
    block_count = row_home.shape[0]
    front_len = block_lists.shape[1]
    rb_local = front_len // pan_count
    cb_local = anc_rows.shape[1] // BLK
    stored_blocks = anc_rows.shape[0] // BLK
    windows = block_count // cb_local
    win_per_group = windows // groups
    per_src = win_per_group * rb_local
    contract = (((0,), (0,)), ((), ()))

    home_of_window = row_home[cb_local * jnp.arange(windows, dtype=jnp.int32)] // stored_blocks
    win = jnp.argsort(home_of_window * windows + jnp.arange(windows, dtype=jnp.int32))
    win = win.reshape(groups, win_per_group).astype(jnp.int32)
    pos = (rb_local * win[:, :, None] + jnp.arange(rb_local, dtype=jnp.int32)).reshape(
        groups, per_src
    )

    my_pos = lax.dynamic_index_in_dim(pos, group_idx, 0, keepdims=False)
    row_blocks = jnp.take(block_lists, my_pos, axis=1)
    slots = jnp.take(row_home, row_blocks) - stored_blocks * group_idx
    cols = lax.dynamic_slice_in_dim(block_lists, rb_local * pan_idx, rb_local, axis=1) - (
        cb_local * pan_idx
    )
    local = anc_rows.reshape(stored_blocks, BLK, cb_local, BLK)
    outgoing = local[slots[:, :, None], :, cols[:, None, :], :]
    received = lax.all_to_all(outgoing, "grp", split_axis=0, concat_axis=0, tiled=True)
    order = jnp.argsort(pos.reshape(groups * per_src)).astype(jnp.int32)
    sigma = jnp.take(received.reshape(groups * per_src, rb_local, BLK, BLK), order, axis=0)

    my_blocks = pan_idx * rb_local + jnp.arange(rb_local, dtype=jnp.int32)
    front_live = lax.dynamic_index_in_dim(front_blocks, group_idx, 0, keepdims=False)
    alive_rows = jnp.repeat(my_blocks < front_live, BLK)
    inverse_pivot = pivot_inverse[0]
    scaled = jnp.dot(panel[0], inverse_pivot, preferred_element_type=jnp.float32)
    scaled = jnp.where(alive_rows[:, None], scaled, jnp.zeros_like(scaled)).astype(jnp.bfloat16)
    full = lax.all_gather(scaled, "pan", axis=0, tiled=True)
    product = lax.dot_general(
        sigma,
        full.reshape(front_len, BLK, P_SIZE),
        (((0, 2), (0, 1)), ((), ())),
        preferred_element_type=jnp.float32,
    ).reshape(rb_local * BLK, P_SIZE)
    cross = jnp.where(alive_rows[:, None], -product, jnp.zeros_like(product)).astype(jnp.bfloat16)
    pivot_rows = P_SIZE // pan_count
    shared = lax.psum_scatter(
        (-lax.dot_general(scaled, cross, contract, preferred_element_type=jnp.float32)).astype(
            jnp.bfloat16
        ),
        "pan",
        scatter_dimension=0,
        tiled=True,
    ).astype(jnp.float32)
    own_columns = lax.dynamic_slice_in_dim(inverse_pivot, pan_idx * pivot_rows, pivot_rows, 1)
    triangle = lax.dot_general(
        own_columns, inverse_pivot, contract, preferred_element_type=jnp.float32
    )
    pivot = triangle + shared
    return (cross[None], pivot[None])


def solution(mesh):
    placed = (P("grp", "pan"), P(), P(), P(), P("grp", "pan", None), P("grp", None, None))
    return jax.shard_map(
        per_device,
        mesh=mesh,
        in_specs=placed,
        out_specs=(P("grp", "pan", None), P("grp", "pan", None)),
        check_vma=False,
    )
```

time: 341 us -> 353 us (1.035)
  waiting for transfers between devices: 241 us -> 282 us
  local copies, waits for them, and re-layouts: 50.7 us -> 25.1 us
    reduce_scatter x0 -> x1, waiting for transfers between devices: none -> 201 us  [per_device(): lax.psum_scatter((-lax.dot_general(scaled, cross, contract, preferred_ele...]
    psum x1 -> x0, waiting for transfers between devices: 148 us -> none  [per_device(): lax.psum((-lax.dot_general(scaled, cross, contract, preferred_element_typ...]
    all_to_all x1, waiting for transfers between devices: 93.7 us -> 47.3 us  [per_device(): lax.all_to_all(outgoing, 'grp', split_axis=0, concat_axis=0, tiled=True)]
    all_gather x1, waiting for transfers between devices: 0.01 us -> 33.7 us  [per_device(): full = lax.all_gather(scaled, 'pan', axis=0, tiled=True)]
    select_n x3 -> x1, local copies, waits for them, and re-layouts: 16.6 us -> 0.08 us  [per_device(): slots = jnp.take(row_home, row_blocks) - stored_blocks * group_idx]
    reshape x3 -> x2, local copies, waits for them, and re-layouts: 20.2 us -> 4.26 us  [per_device(): local = anc_rows.reshape(stored_blocks, BLK, cb_local, BLK)]
    dot_general x0 -> x1, local copies, waits for them, and re-layouts: none -> 6.42 us  [per_device(): lax.dot_general(sigma, full.reshape(front_len, BLK, P_SIZE), (((0, 2), (0...]
    select_n x4 -> x5, other arithmetic: 7.52 us -> 4.93 us  [the longest x2 4.92 us: per_device(): jnp.take(received.reshape(groups * per_src, rb_local, BLK, BLK), order, a...]
  transfers between devices with their start and end apart: 3 -> 3, of which waited for: 2 -> 3; matrix products, arithmetic and copies ran while one was open for 18% -> 9% of each run, Pallas kernels for 0% -> 0%
where the time goes in v1:
time: 353 us; the launch traced here: 350 us
  waiting for transfers between devices  282 us (80%)
  local copies, waits for them, and re-layouts  25.1 us (7%)
  matrix products  14.3 us (4%)
  between operations  14.2 us (4%)
  other arithmetic  9.6 us (3%)
  starting transfers between devices  4.69 us (1%)
    reduce_scatter x1, waiting for transfers between devices, per_device(): lax.psum_scatter((-lax.dot_general(scaled, cross, contract, preferred_ele...  201 us
    all_to_all x1, waiting for transfers between devices, per_device(): lax.all_to_all(outgoing, 'grp', split_axis=0, concat_axis=0, tiled=True)  47.3 us
    all_gather x1, waiting for transfers between devices, per_device(): full = lax.all_gather(scaled, 'pan', axis=0, tiled=True)  33.7 us
    dot_general x1, matrix products, per_device(): lax.dot_general(sigma, full.reshape(front_len, BLK, P_SIZE), (((0, 2), (0...  8.79 us
  transfers between devices with their start and end apart: 3, of which 3 were waited for; matrix products, arithmetic and copies ran while one was open for 9% of the time, Pallas kernels for 0%

profile of v1, /device:TPU:70, one launch (start us, length us, event | category | flops | bytes accessed | tf_op | source)
XLA Modules:
  0.0 350.0 jit_solution(3056510419691765363)
XLA Ops:
  7.3 1.4 dynamic_slice.16
  8.7 0.7 add_compare_fusion
  9.4 2.2 fusion.3
  11.7 1.4 gather_fusion
  13.0 1.6 sort.34
  14.7 0.1 mul.53
  14.7 0.1 copy.20
  14.8 0.1 add.144
  15.0 0.2 dynamic-slice_reduce_fusion
  15.2 0.8 copy.23
  16.0 0.6 gather_fusion.1
  16.6 0.1 reshape.182
  16.7 0.8 gather_fusion.2
  17.5 0.1 reshape.181
  17.6 0.1 fusion.17
  18.0 0.1 reshape.188
  18.1 2.1 reshape.205
  20.2 2.1 copy.27
  22.4 3.1 gather_fusion.3
  25.4 4.6 %all-to-all-start = ((bf16[8,8,2,128,128]{4,3,2,1,0:T(8,128)(2,1)}), bf16[8,8,2,128,128]{4,3,2,1,0:T(8,128)(2,1)}, u32[]{:S(2)}, u32[]{:S(2)}) async-start(bf16[8,8,2,128,128]{4,3,2,1,0:T(8,128)(2,1)} %bitcast.59), calls=%async_computation | async-start | bytes 8388608 | tf_op jit(solution)/shard_map/all_to_all | solution.py:40
  30.1 0.1 copy.21
  30.2 0.1 add.139
  30.3 2.0 sort.35
  32.4 47.3 %all-to-all-done = bf16[8,8,2,128,128]{4,3,2,1,0:T(8,128)(2,1)} async-done(((bf16[8,8,2,128,128]{4,3,2,1,0:T(8,128)(2,1)}), bf16[8,8,2,128,128]{4,3,2,1,0:T(8,128)(2,1)}, u32[]{:S(2)}, u32[]{:S(2)}) %all-to-all-start) | async-done | bytes 4194336 | tf_op jit(solution)/shard_map/all_to_all | solution.py:40
  79.7 5.2 %gather_fusion.4 = bf16[64,2,128,128]{3,2,1,0:T(8,128)(2,1)} fusion(bf16[64,2,128,128]{3,2,1,0:T(8,128)(2,1)} %bitcast.8, s32[1024]{0:T(1024)S(1)} %pad_clamp_fusion), kind=kCustom, calls=%fused_computation.4 | custom fusion | bytes 8388864 | tf_op jit(solution)/shard_map/jit(_take)/gather | solution.py:42
  84.9 4.9 %select_bitcast_fusion = bf16[2,128,64,128]{1,3,0,2:T(8,128)(2,1)} fusion(bf16[64,2,128,128]{3,2,1,0:T(8,128)(2,1)} %gather_fusion.4, pred[64]{0:T(512)(128)(4,1)S(1)} %compare_and_fusion.1), kind=kLoop, calls=%fused_computation.5 | loop fusion | flops 2097152 | bytes 8388672 | tf_op jit(solution)/shard_map/jit(_take)/select_n | solution.py:42
  89.9 6.4 %copy.32 = bf16[2,128,64,128]{3,1,0,2:T(8,128)(2,1)} copy(bf16[2,128,64,128]{1,3,0,2:T(8,128)(2,1)} %select_bitcast_fusion) | data formatting | bytes 8388608 | tf_op jit(solution)/shard_map/dot_general | solution.py:51
  96.3 33.7 %all-gather.2.cloned.1.call-done = bf16[8192,768]{1,0:T(8,128)(2,1)} async-done(((bf16[256,768]{1,0:T(8,128)(2,1)}), bf16[8192,768]{1,0:T(8,128)(2,1)}) %all-gather.2.cloned.1.call-update) | async-done | bytes 12582928 | tf_op jit(solution)/shard_map/all_gather | solution.py:50
  130.0 8.8 %fusion.2 = bf16[256,768]{1,0:T(8,128)(2,1)S(1)} fusion(bf16[256,64,128]{2,0,1:T(8,128)(2,1)} %bitcast.60, bf16[64,128,768]{2,1,0:T(8,128)(2,1)} %bitcast.63, pred[256]{0:T(512)(128)(4,1)S(1)} %broadcast_bitcast_fusion), kind=kOutput, calls=%fused_computation.11 | convolution fusion | flops 3221815296 | bytes 17170688 | tf_op jit(solution)/shard_map/dot_general | solution.py:51
  138.8 1.5 negate_convert_fusion
  140.4 200.9 %reduce-scatter.2.cloned.1.call-done = bf16[24,768]{1,0:T(8,128)(2,1)} async-done(((bf16[768,768]{1,0:T(8,128)(2,1)}), bf16[24,768]{1,0:T(8,128)(2,1)}) %reduce-scatter.2.cloned.1.call-update) | async-done | bytes 36880 | tf_op jit(solution)/shard_map/reduce_scatter | solution.py:59
  341.3 1.8 fusion.10
  (40 shorter events, 0.8 us)
Async XLA Ops:
  7.2 2.2 copy-start
  7.2 9.5 %copy-start.1 = (s32[128]{0:T(128)S(1)}, s32[128]{0:T(128)}, u32[]{:S(2)}) copy-start(s32[128]{0:T(128)} %param.7) | copy-start | bytes 1540
  7.2 10.6 %copy-start.4 = (s32[8,64]{1,0:T(8,128)S(1)}, s32[8,64]{1,0:T(8,128)}, u32[]{:S(2)}) copy-start(s32[8,64]{1,0:T(8,128)} %param.8) | copy-start | bytes 6148
  7.2 10.9 %copy-start.2 = (bf16[2048,512]{1,0:T(8,128)(2,1)S(1)}, bf16[2048,512]{1,0:T(8,128)(2,1)}, u32[]{:S(2)}) copy-start(bf16[2048,512]{1,0:T(8,128)(2,1)} %param.6) | copy-start | bytes 6291460
  7.2 122.8 %all-gather.2.cloned.1.call-start = ((), (), s32[]{:S(2)}) async-start(), calls=%async_computation.2 | async-start | bytes 12976128 | tf_op jit(solution)/shard_map/all_gather | solution.py:50
  25.4 54.3 %all-to-all-start = ((bf16[8,8,2,128,128]{4,3,2,1,0:T(8,128)(2,1)}), bf16[8,8,2,128,128]{4,3,2,1,0:T(8,128)(2,1)}, u32[]{:S(2)}, u32[]{:S(2)}) async-start(bf16[8,8,2,128,128]{4,3,2,1,0:T(8,128)(2,1)} %bitcast.59), calls=%async_computation | async-start | bytes 8388608 | tf_op jit(solution)/shard_map/all_to_all | solution.py:40
  30.1 311.3 %reduce-scatter.2.cloned.1.call-start = ((), (), s32[]{:S(2)}) async-start(), calls=%async_computation.3 | async-start | bytes 1216512 | tf_op jit(solution)/shard_map/reduce_scatter | solution.py:59
  130.0 8.8 %copy-start.3 = (bf16[256,768]{1,0:T(8,128)(2,1)S(1)}, bf16[256,768]{1,0:T(8,128)(2,1)}, u32[]{:S(2)}) copy-start(bf16[256,768]{1,0:T(8,128)(2,1)} %fusion.3) | copy-start | bytes 1179652
  138.8 204.3 %copy-start.5 = (bf16[256,768]{1,0:T(8,128)(2,1)}, bf16[256,768]{1,0:T(8,128)(2,1)S(1)}, u32[]{:S(2)}) copy-start(bf16[256,768]{1,0:T(8,128)(2,1)S(1)} %fusion.2) | copy-start | bytes 1179652
Sparse Core Ops, SparseCore 0:
  11.8 118.2 all-gather.1
  140.5 200.7 reduce-scatter.1

commit v2 on v1

--- a/solution.py
+++ b/solution.py
@@ -2,9 +2,78 @@
 import jax.numpy as jnp
 from jax import lax
 from jax.sharding import PartitionSpec as P
+from jax.experimental import pallas as pl
+from jax.experimental.pallas import tpu as pltpu
 
 BLK = 128
 P_SIZE = 768
+
+
+def _scatter_sum_kernel(n, part_ref, out_ref, buf, send_sem, recv_sem, local_sem):
+    me = lax.axis_index("pan")
+    grp = lax.axis_index("grp")
+    mesh_ids = pl.DeviceIdType.MESH
+
+    barrier = pltpu.get_barrier_semaphore()
+
+    def greet(k, carry):
+        peer = lax.rem(me + k, n)
+        pl.semaphore_signal(barrier, 1, device_id=(grp, peer), device_id_type=mesh_ids)
+        return carry
+
+    lax.fori_loop(1, n, greet, 0)
+    pl.semaphore_wait(barrier, n - 1)
+
+    own = pltpu.make_async_copy(part_ref.at[me], buf.at[0], local_sem)
+    own.start()
+
+    def send(k):
+        peer = lax.rem(me + k, n)
+        return pltpu.make_async_remote_copy(
+            src_ref=part_ref.at[peer],
+            dst_ref=buf.at[k],
+            send_sem=send_sem.at[k],
+            recv_sem=recv_sem.at[k],
+            device_id=(grp, peer),
+            device_id_type=mesh_ids,
+        )
+
+    def start(k, carry):
+        send(k).start()
+        return carry
+
+    def finish(k, carry):
+        send(k).wait()
+        return carry
+
+    lax.fori_loop(1, n, start, 0)
+    own.wait()
+    lax.fori_loop(1, n, finish, 0)
+
+    out_ref[...] = buf[0].astype(jnp.float32)
+
+    def accumulate(k, carry):
+        out_ref[...] += buf[k].astype(jnp.float32)
+        return carry
+
+    lax.fori_loop(1, n, accumulate, 0)
+
+
+def scatter_sum(part, n):
+    _, rows, cols = part.shape
+    return pl.pallas_call(
+        lambda *refs: _scatter_sum_kernel(n, *refs),
+        out_shape=jax.ShapeDtypeStruct((rows, cols), jnp.float32),
+        in_specs=[pl.BlockSpec(memory_space=pl.ANY)],
+        out_specs=pl.BlockSpec(memory_space=pltpu.VMEM),
+        scratch_shapes=[
+            pltpu.VMEM((n, rows, cols), part.dtype),
+            pltpu.SemaphoreType.DMA((n,)),
+            pltpu.SemaphoreType.DMA((n,)),
+            pltpu.SemaphoreType.DMA,
+        ],
+        compiler_params=pltpu.CompilerParams(collective_id=0, has_side_effects=True),
+    )(part)
 
 
 def per_device(anc_rows, row_home, block_lists, front_blocks, panel, pivot_inverse):
@@ -56,14 +125,10 @@
     ).reshape(rb_local * BLK, P_SIZE)
     cross = jnp.where(alive_rows[:, None], -product, jnp.zeros_like(product)).astype(jnp.bfloat16)
     pivot_rows = P_SIZE // pan_count
-    shared = lax.psum_scatter(
-        (-lax.dot_general(scaled, cross, contract, preferred_element_type=jnp.float32)).astype(
-            jnp.bfloat16
-        ),
-        "pan",
-        scatter_dimension=0,
-        tiled=True,
-    ).astype(jnp.float32)
+    part = (-lax.dot_general(scaled, cross, contract, preferred_element_type=jnp.float32)).astype(
+        jnp.bfloat16
+    )
+    shared = scatter_sum(part.reshape(pan_count, pivot_rows, P_SIZE), pan_count)
     own_columns = lax.dynamic_slice_in_dim(inverse_pivot, pan_idx * pivot_rows, pivot_rows, 1)
     triangle = lax.dot_general(
         own_columns, inverse_pivot, contract, preferred_element_type=jnp.float32

time: 353 us -> 188 us (0.53)
  waiting for transfers between devices: 282 us -> 81.3 us
  Pallas kernels: 0 us -> 37.5 us
    reduce_scatter x1 -> x0, waiting for transfers between devices: 201 us -> none  [per_device(): lax.psum_scatter((-lax.dot_general(scaled, cross, contract, preferred_ele...]
    pallas_call x0 -> x1, Pallas kernels: none -> 37.5 us  [scatter_sum(): pl.pallas_call(lambda *refs: _scatter_sum_kernel(n, *refs), out_shape=jax...]
  transfers between devices with their start and end apart: 3 -> 2, of which waited for: 3 -> 2; matrix products, arithmetic and copies ran while one was open for 9% -> 17% of each run, Pallas kernels for 0% -> 0%
where the time goes in v2:
time: 188 us; the launch traced here: 187 us
  waiting for transfers between devices  81.3 us (43%)
  Pallas kernels  37.5 us (20%)
  local copies, waits for them, and re-layouts  25.1 us (13%)
  matrix products  14.5 us (8%)
  between operations  14.2 us (8%)
  other arithmetic  9.59 us (5%)
  starting transfers between devices  4.64 us (2%)
    all_to_all x1, waiting for transfers between devices, per_device(): lax.all_to_all(outgoing, 'grp', split_axis=0, concat_axis=0, tiled=True)  47.4 us
    pallas_call x1, Pallas kernels, scatter_sum(): pl.pallas_call(lambda *refs: _scatter_sum_kernel(n, *refs), out_shape=jax...  37.5 us
    all_gather x1, waiting for transfers between devices, per_device(): full = lax.all_gather(scaled, 'pan', axis=0, tiled=True)  33.9 us
    dot_general x1, matrix products, per_device(): lax.dot_general(sigma, full.reshape(front_len, BLK, P_SIZE), (((0, 2), (0...  8.79 us
    dot_general x1, local copies, waits for them, and re-layouts, per_device(): lax.dot_general(sigma, full.reshape(front_len, BLK, P_SIZE), (((0, 2), (0...  6.42 us
    gather x1, local copies, waits for them, and re-layouts, per_device(): jnp.take(received.reshape(groups * per_src, rb_local, BLK, BLK), order, a...  5.2 us
    select_n x2, other arithmetic, per_device(): jnp.take(received.reshape(groups * per_src, rb_local, BLK, BLK), order, a...  4.9 us
    all_to_all x1, starting transfers between devices, per_device(): lax.all_to_all(outgoing, 'grp', split_axis=0, concat_axis=0, tiled=True)  4.61 us
  transfers between devices with their start and end apart: 2, of which 2 were waited for; matrix products, arithmetic and copies ran while one was open for 17% of the time, Pallas kernels for 0%

profile of v2, /device:TPU:70, one launch (start us, length us, event | category | flops | bytes accessed | tf_op | source)
XLA Modules:
  0.0 186.8 jit_solution(16307687126332310253)
XLA Ops:
  7.3 1.4 dynamic_slice.16
  8.7 0.7 add_compare_fusion
  9.4 2.2 %fusion.3 = bf16[256,768]{1,0:T(8,128)(2,1)} fusion(bf16[1,768,768]{2,1,0:T(8,128)(2,1)S(1)} %copy-done, bf16[1,256,768]{2,1,0:T(8,128)(2,1)} %param.10, pred[256]{0:T(512)(128)(4,1)S(1)} %broadcast_bitcast_fusion), kind=kOutput, calls=%fused_computation.12 | convolution fusion | flops 302383104 | bytes 1966336 | tf_op jit(solution)/shard_map/dot_general | solution.py:117
  11.7 1.4 gather_fusion
  13.0 1.6 sort.34
  14.7 0.1 mul.53
  14.7 0.1 copy.20
  14.8 0.1 add.142
  15.0 0.2 dynamic-slice_reduce_fusion
  15.2 0.8 copy.23
  16.0 0.6 gather_fusion.1
  16.6 0.1 reshape.186
  16.7 0.8 gather_fusion.2
  17.5 0.1 reshape.185
  17.6 0.1 fusion.17
  18.0 0.1 reshape.192
  18.1 2.1 %reshape.209 = bf16[16,128,4,128]{3,2,1,0:T(4,128)(2,1)} reshape(bf16[2048,512]{1,0:T(8,128)(2,1)S(1)} %copy-done.2) | data formatting | bytes 4194304 | tf_op jit(solution)/shard_map/reshape | solution.py:107
  20.2 2.1 %copy.27 = bf16[16,128,4,128]{3,1,2,0:T(8,128)(2,1)S(1)} copy(bf16[16,128,4,128]{3,2,1,0:T(4,128)(2,1)} %reshape.209) | data formatting | bytes 4194304 | tf_op jit(solution)/shard_map/reshape | solution.py:107
  22.4 3.1 %gather_fusion.3 = bf16[128,128,128]{2,1,0:T(8,128)(2,1)} fusion(bf16[16,128,4,128]{3,1,2,0:T(8,128)(2,1)S(1)} %copy.27, s32[128]{0:T(128)S(1)} %reshape.192), kind=kCustom, calls=%fused_computation.3 | custom fusion | bytes 8389632 | tf_op jit(solution)/shard_map/gather | solution.py:108
  25.4 4.6 %all-to-all-start = ((bf16[8,8,2,128,128]{4,3,2,1,0:T(8,128)(2,1)}), bf16[8,8,2,128,128]{4,3,2,1,0:T(8,128)(2,1)}, u32[]{:S(2)}, u32[]{:S(2)}) async-start(bf16[8,8,2,128,128]{4,3,2,1,0:T(8,128)(2,1)} %bitcast.60), calls=%async_computation | async-start | bytes 8388608 | tf_op jit(solution)/shard_map/all_to_all | solution.py:109
  30.1 0.1 copy.21
  30.2 0.1 add.137
  30.3 2.0 %sort.35 = (s32[64]{0:T(128)}, s32[64]{0:T(128)S(1)}) sort(s32[64]{0:T(128)S(1)} %add.137, s32[64]{0:T(128)S(1)} %iota.27), dimensions={0}, to_apply=%region_1.2 | sort | flops 384 | bytes 1024 | tf_op jit(solution)/shard_map/jit(argsort)/sort | solution.py:110
  32.4 47.4 %all-to-all-done = bf16[8,8,2,128,128]{4,3,2,1,0:T(8,128)(2,1)} async-done(((bf16[8,8,2,128,128]{4,3,2,1,0:T(8,128)(2,1)}), bf16[8,8,2,128,128]{4,3,2,1,0:T(8,128)(2,1)}, u32[]{:S(2)}, u32[]{:S(2)}) %all-to-all-start) | async-done | bytes 4194336 | tf_op jit(solution)/shard_map/all_to_all | solution.py:109
  79.7 5.2 %gather_fusion.4 = bf16[64,2,128,128]{3,2,1,0:T(8,128)(2,1)} fusion(bf16[64,2,128,128]{3,2,1,0:T(8,128)(2,1)} %bitcast.8, s32[1024]{0:T(1024)S(1)} %pad_clamp_fusion), kind=kCustom, calls=%fused_computation.4 | custom fusion | bytes 8388864 | tf_op jit(solution)/shard_map/jit(_take)/gather | solution.py:111
  84.9 4.9 %select_bitcast_fusion = bf16[2,128,64,128]{1,3,0,2:T(8,128)(2,1)} fusion(bf16[64,2,128,128]{3,2,1,0:T(8,128)(2,1)} %gather_fusion.4, pred[64]{0:T(512)(128)(4,1)S(1)} %compare_and_fusion.1), kind=kLoop, calls=%fused_computation.5 | loop fusion | flops 2097152 | bytes 8388672 | tf_op jit(solution)/shard_map/jit(_take)/select_n | solution.py:111
  89.8 6.4 %copy.32 = bf16[2,128,64,128]{3,1,0,2:T(8,128)(2,1)} copy(bf16[2,128,64,128]{1,3,0,2:T(8,128)(2,1)} %select_bitcast_fusion) | data formatting | bytes 8388608 | tf_op jit(solution)/shard_map/dot_general | solution.py:120
  96.2 33.9 %all-gather.2.cloned.1.call-done = bf16[8192,768]{1,0:T(8,128)(2,1)} async-done(((bf16[256,768]{1,0:T(8,128)(2,1)}), bf16[8192,768]{1,0:T(8,128)(2,1)}) %all-gather.2.cloned.1.call-update) | async-done | bytes 12582928 | tf_op jit(solution)/shard_map/all_gather | solution.py:119
  130.1 8.8 %fusion.2 = bf16[256,768]{1,0:T(8,128)(2,1)S(1)} fusion(bf16[256,64,128]{2,0,1:T(8,128)(2,1)} %bitcast.61, bf16[64,128,768]{2,1,0:T(8,128)(2,1)} %bitcast.65, pred[256]{0:T(512)(128)(4,1)S(1)} %broadcast_bitcast_fusion), kind=kOutput, calls=%fused_computation.11 | convolution fusion | flops 3221815296 | bytes 17170688 | tf_op jit(solution)/shard_map/dot_general | solution.py:120
  139.0 1.5 negate_convert_fusion
  140.5 37.5 %shard_map.77 = f32[24,768]{1,0:T(8,128)} custom-call(bf16[32,24,768]{2,1,0:T(8,128)(2,1)} %bitcast.62), custom_call_target="tpu_custom_call" | custom-call | tf_op jit(solution)/shard_map/pallas_call | solution.py:64
  178.0 1.9 %fusion.10 = f32[1,24,768]{2,1,0:T(8,128)} fusion(f32[24,768]{1,0:T(8,128)} %shard_map.77, bf16[1,768,768]{2,1,0:T(8,128)(2,1)S(1)} %copy-done, s32[]{:T(128)S(6)} %select_n.138), kind=kOutput, calls=%fused_computation.17 | convolution fusion | flops 28329984 | bytes 1523716 | tf_op jit(solution)/shard_map/dot_general | solution.py:133
  (38 shorter events, 0.7 us)
Async XLA Ops:
  7.2 2.2 %copy-start = (bf16[1,768,768]{2,1,0:T(8,128)(2,1)S(1)}, bf16[1,768,768]{2,1,0:T(8,128)(2,1)}, u32[]{:S(2)}) copy-start(bf16[1,768,768]{2,1,0:T(8,128)(2,1)} %param.11) | copy-start | bytes 3538948
  7.2 9.5 %copy-start.1 = (s32[128]{0:T(128)S(1)}, s32[128]{0:T(128)}, u32[]{:S(2)}) copy-start(s32[128]{0:T(128)} %param.7) | copy-start | bytes 1540
  7.2 10.6 %copy-start.4 = (s32[8,64]{1,0:T(8,128)S(1)}, s32[8,64]{1,0:T(8,128)}, u32[]{:S(2)}) copy-start(s32[8,64]{1,0:T(8,128)} %param.8) | copy-start | bytes 6148
  7.2 10.9 %copy-start.2 = (bf16[2048,512]{1,0:T(8,128)(2,1)S(1)}, bf16[2048,512]{1,0:T(8,128)(2,1)}, u32[]{:S(2)}) copy-start(bf16[2048,512]{1,0:T(8,128)(2,1)} %param.6) | copy-start | bytes 6291460
  7.2 122.9 %all-gather.2.cloned.1.call-start = ((), (), s32[]{:S(2)}) async-start(), calls=%async_computation.1 | async-start | bytes 12976128 | tf_op jit(solution)/shard_map/all_gather | solution.py:119
  25.4 54.3 %all-to-all-start = ((bf16[8,8,2,128,128]{4,3,2,1,0:T(8,128)(2,1)}), bf16[8,8,2,128,128]{4,3,2,1,0:T(8,128)(2,1)}, u32[]{:S(2)}, u32[]{:S(2)}) async-start(bf16[8,8,2,128,128]{4,3,2,1,0:T(8,128)(2,1)} %bitcast.60), calls=%async_computation | async-start | bytes 8388608 | tf_op jit(solution)/shard_map/all_to_all | solution.py:109
  130.1 8.8 %copy-start.3 = (bf16[256,768]{1,0:T(8,128)(2,1)S(1)}, bf16[256,768]{1,0:T(8,128)(2,1)}, u32[]{:S(2)}) copy-start(bf16[256,768]{1,0:T(8,128)(2,1)} %fusion.3) | copy-start | bytes 1179652
  138.9 41.0 %copy-start.5 = (bf16[256,768]{1,0:T(8,128)(2,1)}, bf16[256,768]{1,0:T(8,128)(2,1)S(1)}, u32[]{:S(2)}) copy-start(bf16[256,768]{1,0:T(8,128)(2,1)S(1)} %fusion.2) | copy-start | bytes 1179652
Sparse Core Ops, SparseCore 0:
  11.8 118.3 all-gather.1

commit v3 on v2

--- a/solution.py
+++ b/solution.py
@@ -59,7 +59,7 @@
     lax.fori_loop(1, n, accumulate, 0)
 
 
-def scatter_sum(part, n):
+def scatter_sum(part, n, kernel_id):
     _, rows, cols = part.shape
     return pl.pallas_call(
         lambda *refs: _scatter_sum_kernel(n, *refs),
@@ -72,7 +72,12 @@
             pltpu.SemaphoreType.DMA((n,)),
             pltpu.SemaphoreType.DMA,
         ],
-        compiler_params=pltpu.CompilerParams(collective_id=0, has_side_effects=True),
+        compiler_params=pltpu.CompilerParams(collective_id=kernel_id, has_side_effects=True),
+        cost_estimate=pl.CostEstimate(
+            flops=n * rows * cols,
+            bytes_accessed=2 * n * rows * cols * part.dtype.itemsize,
+            transcendentals=0,
+        ),
     )(part)
 
 
@@ -116,19 +121,31 @@
     inverse_pivot = pivot_inverse[0]
     scaled = jnp.dot(panel[0], inverse_pivot, preferred_element_type=jnp.float32)
     scaled = jnp.where(alive_rows[:, None], scaled, jnp.zeros_like(scaled)).astype(jnp.bfloat16)
-    full = lax.all_gather(scaled, "pan", axis=0, tiled=True)
-    product = lax.dot_general(
-        sigma,
-        full.reshape(front_len, BLK, P_SIZE),
-        (((0, 2), (0, 1)), ((), ())),
-        preferred_element_type=jnp.float32,
-    ).reshape(rb_local * BLK, P_SIZE)
-    cross = jnp.where(alive_rows[:, None], -product, jnp.zeros_like(product)).astype(jnp.bfloat16)
     pivot_rows = P_SIZE // pan_count
-    part = (-lax.dot_general(scaled, cross, contract, preferred_element_type=jnp.float32)).astype(
-        jnp.bfloat16
-    )
-    shared = scatter_sum(part.reshape(pan_count, pivot_rows, P_SIZE), pan_count)
+    cross_pieces = []
+    shared_pieces = []
+    first = 0
+    for piece, width in enumerate((P_SIZE // 3, 2 * P_SIZE // 3)):
+        full = lax.all_gather(scaled[:, first : first + width], "pan", axis=0, tiled=True)
+        product = lax.dot_general(
+            sigma,
+            full.reshape(front_len, BLK, width),
+            (((0, 2), (0, 1)), ((), ())),
+            preferred_element_type=jnp.float32,
+        ).reshape(rb_local * BLK, width)
+        cross_piece = jnp.where(
+            alive_rows[:, None], -product, jnp.zeros_like(product)
+        ).astype(jnp.bfloat16)
+        part = (
+            -lax.dot_general(scaled, cross_piece, contract, preferred_element_type=jnp.float32)
+        ).astype(jnp.bfloat16)
+        slabs = part.reshape(pan_count, pivot_rows * width // BLK, BLK)
+        summed = scatter_sum(slabs, pan_count, piece)
+        cross_pieces.append(cross_piece)
+        shared_pieces.append(summed.reshape(pivot_rows, width))
+        first += width
+    cross = jnp.concatenate(cross_pieces, axis=1)
+    shared = jnp.concatenate(shared_pieces, axis=1)
     own_columns = lax.dynamic_slice_in_dim(inverse_pivot, pan_idx * pivot_rows, pivot_rows, 1)
     triangle = lax.dot_general(
         own_columns, inverse_pivot, contract, preferred_element_type=jnp.float32

time: 188 us -> 243 us (1.29)
  waiting for transfers between devices: 81.3 us -> 114 us
  Pallas kernels: 37.5 us -> 52.3 us
  local copies, waits for them, and re-layouts: 25.1 us -> 31.4 us
    all_gather x1 -> x2, waiting for transfers between devices: 33.9 us -> 66.2 us  [per_device(): lax.all_gather(scaled[:, first:first + width], 'pan', axis=0, tiled=True)]
    pallas_call x1 -> x2, Pallas kernels: 37.5 us -> 52.3 us  [scatter_sum(): pl.pallas_call(lambda *refs: _scatter_sum_kernel(n, *refs), out_shape=jax...]
    reshape x0 -> x4, local copies, waits for them, and re-layouts: none -> 3.04 us  [the longest x2 2.22 us: per_device(): slabs = part.reshape(pan_count, pivot_rows * width // BLK, BLK)]
    dot_general x2 -> x4, matrix products: 10.3 us -> 12.9 us  [the longest x2 12.2 us: per_device(): lax.dot_general(sigma, full.reshape(front_len, BLK, width), (((0, 2), (0,...]
  transfers between devices with their start and end apart: 2 -> 3, of which waited for: 2 -> 2; matrix products, arithmetic and copies ran while one was open for 17% -> 17% of each run, Pallas kernels for 0% -> 10%
where the time goes in v3:
time: 243 us; the launch traced here: 242 us
  waiting for transfers between devices  114 us (47%)
  Pallas kernels  52.3 us (22%)
  local copies, waits for them, and re-layouts  31.4 us (13%)
  matrix products  15.4 us (6%)
  between operations  14.3 us (6%)
  other arithmetic  10 us (4%)
  starting transfers between devices  4.66 us (2%)
    all_gather x2, waiting for transfers between devices, per_device(): lax.all_gather(scaled[:, first:first + width], 'pan', axis=0, tiled=True)  66.2 us
    pallas_call x2, Pallas kernels, scatter_sum(): pl.pallas_call(lambda *refs: _scatter_sum_kernel(n, *refs), out_shape=jax...  52.3 us
    all_to_all x1, waiting for transfers between devices, per_device(): lax.all_to_all(outgoing, 'grp', split_axis=0, concat_axis=0, tiled=True)  47.4 us
    dot_general x2, matrix products, per_device(): lax.dot_general(sigma, full.reshape(front_len, BLK, width), (((0, 2), (0,...  12.2 us
    dot_general x1, local copies, waits for them, and re-layouts, per_device(): lax.dot_general(sigma, full.reshape(front_len, BLK, width), (((0, 2), (0,...  6.38 us
    reshape x2, local copies, waits for them, and re-layouts, per_device(): local = anc_rows.reshape(stored_blocks, BLK, cb_local, BLK)  6.14 us
    gather x1, local copies, waits for them, and re-layouts, per_device(): jnp.take(received.reshape(groups * per_src, rb_local, BLK, BLK), order, a...  5.24 us
  transfers between devices with their start and end apart: 3, of which 2 were waited for; matrix products, arithmetic and copies ran while one was open for 17% of the time, Pallas kernels for 10%

profile of v3, /device:TPU:70, one launch (start us, length us, event | category | flops | bytes accessed | tf_op | source)
XLA Modules:
  0.0 241.7 jit_solution(4747077722715548028)
XLA Ops:
  7.3 1.3 dynamic_slice.16
  8.6 0.7 add_compare_fusion
  9.3 1.5 fusion
  10.8 0.7 slice.18
  11.6 0.7 slice.19
  12.3 1.4 gather_fusion
  13.7 1.6 sort.34
  15.7 0.2 dynamic-slice_reduce_fusion
  15.9 0.8 copy.27
  16.7 0.6 gather_fusion.1
  17.4 0.8 gather_fusion.2
  18.8 4.0 %reshape.228 = bf16[16,128,4,128]{3,2,1,0:T(4,128)(2,1)} reshape(bf16[2048,512]{1,0:T(8,128)(2,1)} %param.6) | data formatting | bytes 4194304 | tf_op jit(solution)/shard_map/reshape | solution.py:112
  22.8 2.1 copy.31
  24.9 3.1 %gather_fusion.3 = bf16[128,128,128]{2,1,0:T(8,128)(2,1)} fusion(bf16[16,128,4,128]{3,1,2,0:T(8,128)(2,1)S(1)} %copy.31, s32[128]{0:T(128)S(1)} %reshape.210), kind=kCustom, calls=%fused_computation.3 | custom fusion | bytes 8389632 | tf_op jit(solution)/shard_map/gather | solution.py:113
  28.0 4.6 %all-to-all-start = ((bf16[8,8,2,128,128]{4,3,2,1,0:T(8,128)(2,1)}), bf16[8,8,2,128,128]{4,3,2,1,0:T(8,128)(2,1)}, u32[]{:S(2)}, u32[]{:S(2)}) async-start(bf16[8,8,2,128,128]{4,3,2,1,0:T(8,128)(2,1)} %bitcast.74), calls=%async_computation | async-start | bytes 8388608 | tf_op jit(solution)/shard_map/all_to_all | solution.py:114
  32.8 2.0 sort.35
  34.9 47.4 %all-to-all-done = bf16[8,8,2,128,128]{4,3,2,1,0:T(8,128)(2,1)} async-done(((bf16[8,8,2,128,128]{4,3,2,1,0:T(8,128)(2,1)}), bf16[8,8,2,128,128]{4,3,2,1,0:T(8,128)(2,1)}, u32[]{:S(2)}, u32[]{:S(2)}) %all-to-all-start) | async-done | bytes 4194336 | tf_op jit(solution)/shard_map/all_to_all | solution.py:114
  82.3 5.2 %gather_fusion.4 = bf16[64,2,128,128]{3,2,1,0:T(8,128)(2,1)} fusion(bf16[64,2,128,128]{3,2,1,0:T(8,128)(2,1)} %bitcast.8, s32[1024]{0:T(1024)S(1)} %pad_clamp_fusion), kind=kCustom, calls=%fused_computation.4 | custom fusion | bytes 8388864 | tf_op jit(solution)/shard_map/jit(_take)/gather | solution.py:116
  87.5 4.6 %select_bitcast_fusion = bf16[2,128,64,128]{1,3,0,2:T(8,128)(2,1)} fusion(bf16[64,2,128,128]{3,2,1,0:T(8,128)(2,1)} %gather_fusion.4, pred[64]{0:T(512)(128)(4,1)S(1)} %compare_and_fusion.1), kind=kLoop, calls=%fused_computation.5 | loop fusion | flops 2097152 | bytes 8388672 | tf_op jit(solution)/shard_map/jit(_take)/select_n | solution.py:116
  92.1 6.4 %copy.40 = bf16[2,128,64,128]{3,1,0,2:T(8,128)(2,1)} copy(bf16[2,128,64,128]{1,3,0,2:T(8,128)(2,1)} %select_bitcast_fusion) | data formatting | bytes 8388608 | tf_op jit(solution)/shard_map/dot_general | solution.py:130
  98.5 5.2 %fusion.10 = bf16[256,256]{0,1:T(8,128)(2,1)S(1)} fusion(bf16[256,64,128]{2,0,1:T(8,128)(2,1)} %bitcast.75, bf16[64,128,256]{2,1,0:T(8,128)(2,1)} %bitcast.77, pred[256]{0:T(512)(128)(4,1)S(1)} %broadcast_bitcast_fusion), kind=kOutput, calls=%fused_computation.21 | convolution fusion | flops 1073938432 | bytes 8519936 | tf_op jit(solution)/shard_map/dot_general | solution.py:130
  103.7 0.3 fusion.1
  104.0 0.9 reshape.182.refs_0_
  104.9 23.6 %shard_map.77 = f32[48,128]{1,0:T(8,128)} custom-call(bf16[32,48,128]{2,1,0:T(8,128)(2,1)} %reshape.182.refs_0_), custom_call_target="tpu_custom_call" | custom-call | flops 196608 | bytes 786432 | tf_op jit(solution)/shard_map/pallas_call | solution.py:64
  128.6 66.2 %all-gather.5.cloned.1.call-done = bf16[8192,512]{1,0:T(8,128)(2,1)} async-done(((bf16[256,512]{1,0:T(8,128)(2,1)}), bf16[8192,512]{1,0:T(8,128)(2,1)}) %all-gather.5.cloned.1.call-update) | async-done | bytes 8388624 | tf_op jit(solution)/shard_map/all_gather | solution.py:129
  194.8 7.0 %fusion.4 = bf16[256,512]{1,0:T(8,128)(2,1)S(1)} fusion(bf16[256,64,128]{2,0,1:T(8,128)(2,1)} %bitcast.76, bf16[64,128,512]{2,1,0:T(8,128)(2,1)} %bitcast.80, pred[256]{0:T(512)(128)(4,1)S(1)} %broadcast_bitcast_fusion), kind=kOutput, calls=%fused_computation.14 | convolution fusion | flops 2147876864 | bytes 12845312 | tf_op jit(solution)/shard_map/dot_general | solution.py:130
  201.8 0.4 negate_convert_fusion
  202.2 1.3 reshape.184.refs_0_
  203.5 28.7 %shard_map.78 = f32[96,128]{1,0:T(8,128)} custom-call(bf16[32,96,128]{2,1,0:T(8,128)(2,1)} %reshape.184.refs_0_), custom_call_target="tpu_custom_call" | custom-call | flops 393216 | bytes 1572864 | tf_op jit(solution)/shard_map/pallas_call | solution.py:64
  232.2 0.8 reshape.185
  233.0 0.8 maximum_bitcast_fusion
  233.8 1.0 fusion.14
  (52 shorter events, 1.7 us)
Async XLA Ops:
  7.2 2.1 copy-start
  7.2 10.2 %copy-start.1 = (s32[128]{0:T(128)S(1)}, s32[128]{0:T(128)}, u32[]{:S(2)}) copy-start(s32[128]{0:T(128)} %param.7) | copy-start | bytes 1540
  7.2 91.3 %all-gather.3.cloned.1.call-start = ((), (), s32[]{:S(2)}) async-start(), calls=%async_computation.1 | async-start | bytes 4325376 | tf_op jit(solution)/shard_map/all_gather | solution.py:129
  7.2 11.2 %copy-start.5 = (s32[8,64]{1,0:T(8,128)S(1)}, s32[8,64]{1,0:T(8,128)}, u32[]{:S(2)}) copy-start(s32[8,64]{1,0:T(8,128)} %param.8) | copy-start | bytes 6148
  10.8 8.0 %copy-start.2 = (bf16[256,768]{1,0:T(8,128)(2,1)}, bf16[256,768]{1,0:T(8,128)(2,1)S(1)}, u32[]{:S(2)}) copy-start(bf16[256,768]{1,0:T(8,128)(2,1)S(1)} %fusion) | copy-start | bytes 1179652
  11.5 183.2 %all-gather.5.cloned.1.call-start = ((), (), s32[]{:S(2)}) async-start(), calls=%async_computation.2 | async-start | bytes 8650752 | tf_op jit(solution)/shard_map/all_gather | solution.py:129
  28.0 54.3 %all-to-all-start = ((bf16[8,8,2,128,128]{4,3,2,1,0:T(8,128)(2,1)}), bf16[8,8,2,128,128]{4,3,2,1,0:T(8,128)(2,1)}, u32[]{:S(2)}, u32[]{:S(2)}) async-start(bf16[8,8,2,128,128]{4,3,2,1,0:T(8,128)(2,1)} %bitcast.74), calls=%async_computation | async-start | bytes 8388608 | tf_op jit(solution)/shard_map/all_to_all | solution.py:114
  98.4 5.3 %copy-start.3 = (bf16[256,768]{1,0:T(8,128)(2,1)S(1)}, bf16[256,768]{1,0:T(8,128)(2,1)}, u32[]{:S(2)}) copy-start(bf16[256,768]{1,0:T(8,128)(2,1)} %copy-done.2) | copy-start | bytes 1179652
  194.8 8.7 %copy-start.4 = (f32[48,128]{1,0:T(8,128)S(1)}, f32[48,128]{1,0:T(8,128)}, u32[]{:S(2)}) copy-start(f32[48,128]{1,0:T(8,128)} %shard_map.77) | copy-start | bytes 73732
Sparse Core Ops, SparseCore 0:
  11.7 81.9 all-gather.2
  96.2 98.5 all-gather.4

commit v4 on v2

--- a/solution.py
+++ b/solution.py
@@ -9,7 +9,7 @@
 P_SIZE = 768
 
 
-def _scatter_sum_kernel(n, part_ref, out_ref, buf, send_sem, recv_sem, local_sem):
+def _scatter_sum_kernel(n, part_ref, base_ref, out_ref, buf, send_sem, recv_sem, local_sem):
     me = lax.axis_index("pan")
     grp = lax.axis_index("grp")
     mesh_ids = pl.DeviceIdType.MESH
@@ -50,7 +50,7 @@
     own.wait()
     lax.fori_loop(1, n, finish, 0)
 
-    out_ref[...] = buf[0].astype(jnp.float32)
+    out_ref[...] = base_ref[...] + buf[0].astype(jnp.float32)
 
     def accumulate(k, carry):
         out_ref[...] += buf[k].astype(jnp.float32)
@@ -59,12 +59,12 @@
     lax.fori_loop(1, n, accumulate, 0)
 
 
-def scatter_sum(part, n):
+def scatter_sum(part, base, n):
     _, rows, cols = part.shape
     return pl.pallas_call(
         lambda *refs: _scatter_sum_kernel(n, *refs),
         out_shape=jax.ShapeDtypeStruct((rows, cols), jnp.float32),
-        in_specs=[pl.BlockSpec(memory_space=pl.ANY)],
+        in_specs=[pl.BlockSpec(memory_space=pl.ANY), pl.BlockSpec(memory_space=pltpu.VMEM)],
         out_specs=pl.BlockSpec(memory_space=pltpu.VMEM),
         scratch_shapes=[
             pltpu.VMEM((n, rows, cols), part.dtype),
@@ -73,7 +73,7 @@
             pltpu.SemaphoreType.DMA,
         ],
         compiler_params=pltpu.CompilerParams(collective_id=0, has_side_effects=True),
-    )(part)
+    )(part, base)
 
 
 def per_device(anc_rows, row_home, block_lists, front_blocks, panel, pivot_inverse):
@@ -109,6 +109,7 @@
     received = lax.all_to_all(outgoing, "grp", split_axis=0, concat_axis=0, tiled=True)
     order = jnp.argsort(pos.reshape(groups * per_src)).astype(jnp.int32)
     sigma = jnp.take(received.reshape(groups * per_src, rb_local, BLK, BLK), order, axis=0)
+    sigma_t = jnp.transpose(sigma, (1, 3, 0, 2)).reshape(rb_local * BLK, front_len * BLK)
 
     my_blocks = pan_idx * rb_local + jnp.arange(rb_local, dtype=jnp.int32)
     front_live = lax.dynamic_index_in_dim(front_blocks, group_idx, 0, keepdims=False)
@@ -117,23 +118,17 @@
     scaled = jnp.dot(panel[0], inverse_pivot, preferred_element_type=jnp.float32)
     scaled = jnp.where(alive_rows[:, None], scaled, jnp.zeros_like(scaled)).astype(jnp.bfloat16)
     full = lax.all_gather(scaled, "pan", axis=0, tiled=True)
-    product = lax.dot_general(
-        sigma,
-        full.reshape(front_len, BLK, P_SIZE),
-        (((0, 2), (0, 1)), ((), ())),
-        preferred_element_type=jnp.float32,
-    ).reshape(rb_local * BLK, P_SIZE)
+    product = jnp.dot(sigma_t, full, preferred_element_type=jnp.float32)
     cross = jnp.where(alive_rows[:, None], -product, jnp.zeros_like(product)).astype(jnp.bfloat16)
     pivot_rows = P_SIZE // pan_count
     part = (-lax.dot_general(scaled, cross, contract, preferred_element_type=jnp.float32)).astype(
         jnp.bfloat16
     )
-    shared = scatter_sum(part.reshape(pan_count, pivot_rows, P_SIZE), pan_count)
     own_columns = lax.dynamic_slice_in_dim(inverse_pivot, pan_idx * pivot_rows, pivot_rows, 1)
     triangle = lax.dot_general(
         own_columns, inverse_pivot, contract, preferred_element_type=jnp.float32
     )
-    pivot = triangle + shared
+    pivot = scatter_sum(part.reshape(pan_count, pivot_rows, P_SIZE), triangle, pan_count)
     return (cross[None], pivot[None])
 
 

time: 188 us -> 190 us (1.011)
    select_n x0 -> x1, local copies, waits for them, and re-layouts: none -> 6.58 us  [per_device(): jnp.take(received.reshape(groups * per_src, rb_local, BLK, BLK), order, a...]
    dot_general x1 -> x0, local copies, waits for them, and re-layouts: 6.42 us -> none  [per_device(): lax.dot_general(sigma, full.reshape(front_len, BLK, P_SIZE), (((0, 2), (0...]
    dot_general x1, matrix products: 8.79 us -> 10.8 us  [per_device(): product = jnp.dot(sigma_t, full, preferred_element_type=jnp.float32)]
  transfers between devices with their start and end apart: 2 -> 2, of which waited for: 2 -> 2; matrix products, arithmetic and copies ran while one was open for 17% -> 18% of each run, Pallas kernels for 0% -> 0%
where the time goes in v4:
time: 190 us; the launch traced here: 189 us
  waiting for transfers between devices  80.1 us (42%)
  Pallas kernels  38.4 us (20%)
  local copies, waits for them, and re-layouts  26.8 us (14%)
  matrix products  15.5 us (8%)
  between operations  14.2 us (7%)
  other arithmetic  9.59 us (5%)
  starting transfers between devices  4.64 us (2%)
    all_to_all x1, waiting for transfers between devices, per_device(): lax.all_to_all(outgoing, 'grp', split_axis=0, concat_axis=0, tiled=True)  46.3 us
    pallas_call x1, Pallas kernels, scatter_sum(): pl.pallas_call(lambda *refs: _scatter_sum_kernel(n, *refs), out_shape=jax...  38.4 us
    all_gather x1, waiting for transfers between devices, per_device(): full = lax.all_gather(scaled, 'pan', axis=0, tiled=True)  33.7 us
    dot_general x1, matrix products, per_device(): product = jnp.dot(sigma_t, full, preferred_element_type=jnp.float32)  10.8 us
    select_n x1, local copies, waits for them, and re-layouts, per_device(): jnp.take(received.reshape(groups * per_src, rb_local, BLK, BLK), order, a...  6.58 us
    gather x1, local copies, waits for them, and re-layouts, per_device(): jnp.take(received.reshape(groups * per_src, rb_local, BLK, BLK), order, a...  5.2 us
    select_n x2, other arithmetic, per_device(): jnp.take(received.reshape(groups * per_src, rb_local, BLK, BLK), order, a...  4.9 us
    all_to_all x1, starting transfers between devices, per_device(): lax.all_to_all(outgoing, 'grp', split_axis=0, concat_axis=0, tiled=True)  4.61 us
  transfers between devices with their start and end apart: 2, of which 2 were waited for; matrix products, arithmetic and copies ran while one was open for 18% of the time, Pallas kernels for 0%

profile of v4, /device:TPU:70, one launch (start us, length us, event | category | flops | bytes accessed | tf_op | source)
XLA Modules:
  0.0 189.2 jit_solution(2795596537568755544)
XLA Ops:
  7.3 1.4 dynamic_slice.16
  8.7 0.7 add_compare_fusion
  9.4 2.2 %fusion.12 = bf16[256,768]{1,0:T(8,128)(2,1)} fusion(bf16[1,768,768]{2,1,0:T(8,128)(2,1)S(1)} %copy-done, bf16[1,256,768]{2,1,0:T(8,128)(2,1)} %param.10, pred[256]{0:T(512)(128)(4,1)S(1)} %broadcast_bitcast_fusion), kind=kOutput, calls=%fused_computation.14 | convolution fusion | flops 302383104 | bytes 1966336 | tf_op jit(solution)/shard_map/dot_general | solution.py:118
  11.7 1.4 gather_fusion
  13.0 1.6 sort.34
  14.7 0.1 mul.53
  14.7 0.1 copy.28
  14.8 0.1 add.139
  15.0 0.2 dynamic-slice_reduce_fusion
  15.2 0.8 copy.31
  16.0 0.6 gather_fusion.1
  16.6 0.1 reshape.184
  16.7 0.8 gather_fusion.2
  17.6 0.1 fusion.20
  18.0 0.1 reshape.190
  18.1 2.1 %reshape.206 = bf16[16,128,4,128]{3,2,1,0:T(4,128)(2,1)} reshape(bf16[2048,512]{1,0:T(8,128)(2,1)S(1)} %copy-done.2) | data formatting | bytes 4194304 | tf_op jit(solution)/shard_map/reshape | solution.py:107
  20.2 2.1 %copy.35 = bf16[16,128,4,128]{3,1,2,0:T(8,128)(2,1)S(1)} copy(bf16[16,128,4,128]{3,2,1,0:T(4,128)(2,1)} %reshape.206) | data formatting | bytes 4194304 | tf_op jit(solution)/shard_map/reshape | solution.py:107
  22.4 3.1 %gather_fusion.3 = bf16[128,128,128]{2,1,0:T(8,128)(2,1)} fusion(bf16[16,128,4,128]{3,1,2,0:T(8,128)(2,1)S(1)} %copy.35, s32[128]{0:T(128)S(1)} %reshape.190), kind=kCustom, calls=%fused_computation.3 | custom fusion | bytes 8389632 | tf_op jit(solution)/shard_map/gather | solution.py:108
  25.4 4.6 %all-to-all-start = ((bf16[8,8,2,128,128]{4,3,2,1,0:T(8,128)(2,1)}), bf16[8,8,2,128,128]{4,3,2,1,0:T(8,128)(2,1)}, u32[]{:S(2)}, u32[]{:S(2)}) async-start(bf16[8,8,2,128,128]{4,3,2,1,0:T(8,128)(2,1)} %bitcast.54), calls=%async_computation | async-start | bytes 8388608 | tf_op jit(solution)/shard_map/all_to_all | solution.py:109
  30.1 0.1 copy.29
  30.2 0.1 add.134
  30.3 2.0 %sort.35 = (s32[64]{0:T(128)}, s32[64]{0:T(128)S(1)}) sort(s32[64]{0:T(128)S(1)} %add.134, s32[64]{0:T(128)S(1)} %iota.27), dimensions={0}, to_apply=%region_1.2 | sort | flops 384 | bytes 1024 | tf_op jit(solution)/shard_map/jit(argsort)/sort | solution.py:110
  32.4 1.0 fusion.13.refs_1_
  33.4 46.3 %all-to-all-done = bf16[8,8,2,128,128]{4,3,2,1,0:T(8,128)(2,1)} async-done(((bf16[8,8,2,128,128]{4,3,2,1,0:T(8,128)(2,1)}), bf16[8,8,2,128,128]{4,3,2,1,0:T(8,128)(2,1)}, u32[]{:S(2)}, u32[]{:S(2)}) %all-to-all-start) | async-done | bytes 4194336 | tf_op jit(solution)/shard_map/all_to_all | solution.py:109
  79.7 5.2 %gather_fusion.4 = bf16[64,2,128,128]{3,2,1,0:T(8,128)(2,1)} fusion(bf16[64,2,128,128]{3,2,1,0:T(8,128)(2,1)} %bitcast.8, s32[1024]{0:T(1024)S(1)} %pad_clamp_fusion), kind=kCustom, calls=%fused_computation.4 | custom fusion | bytes 8388864 | tf_op jit(solution)/shard_map/jit(_take)/gather | solution.py:111
  84.9 4.9 %select_bitcast_fusion = bf16[2,128,64,128]{1,3,0,2:T(8,128)(2,1)} fusion(bf16[64,2,128,128]{3,2,1,0:T(8,128)(2,1)} %gather_fusion.4, pred[64]{0:T(512)(128)(4,1)S(1)} %compare_and_fusion.1), kind=kLoop, calls=%fused_computation.8 | loop fusion | flops 2097152 | bytes 8388672 | tf_op jit(solution)/shard_map/jit(_take)/select_n | solution.py:111
  89.8 6.6 %copy.36 = bf16[2,128,64,128]{3,2,1,0:T(8,128)(2,1)} copy(bf16[2,128,64,128]{1,3,0,2:T(8,128)(2,1)} %select_bitcast_fusion) | data formatting | bytes 8388608 | tf_op jit(solution)/shard_map/jit(_take)/select_n | solution.py:111
  96.4 33.7 %all-gather.2.cloned.1.call-done = bf16[8192,768]{1,0:T(8,128)(2,1)} async-done(((bf16[256,768]{1,0:T(8,128)(2,1)}), bf16[8192,768]{1,0:T(8,128)(2,1)}) %all-gather.2.cloned.1.call-update) | async-done | bytes 12582928 | tf_op jit(solution)/shard_map/all_gather | solution.py:120
  130.1 10.8 %fusion.9 = bf16[256,768]{1,0:T(8,128)(2,1)S(1)} fusion(bf16[8192,768]{1,0:T(8,128)(2,1)} %all-gather.2.cloned.1.call-done, bf16[32,8,64,128]{3,2,1,0:T(8,128)(2,1)} %bitcast.55, pred[256]{0:T(512)(128)(4,1)S(1)} %broadcast_bitcast_fusion), kind=kOutput, calls=%fused_computation.13 | convolution fusion | flops 3221815296 | bytes 17170688 | tf_op jit(solution)/shard_map/dot_general | solution.py:121
  140.9 1.5 negate_convert_fusion
  142.5 38.4 %shard_map.77 = f32[24,768]{1,0:T(8,128)} custom-call(bf16[32,24,768]{2,1,0:T(8,128)(2,1)} %bitcast.56, f32[24,768]{1,0:T(8,128)} %fusion.13.refs_1_), custom_call_target="tpu_custom_call" | custom-call | tf_op jit(solution)/shard_map/pallas_call | solution.py:64
  180.8 1.5 copy.51
  (39 shorter events, 0.8 us)
Async XLA Ops:
  7.2 2.2 %copy-start = (bf16[1,768,768]{2,1,0:T(8,128)(2,1)S(1)}, bf16[1,768,768]{2,1,0:T(8,128)(2,1)}, u32[]{:S(2)}) copy-start(bf16[1,768,768]{2,1,0:T(8,128)(2,1)} %param.11) | copy-start | bytes 3538948
  7.2 9.5 %copy-start.1 = (s32[128]{0:T(128)S(1)}, s32[128]{0:T(128)}, u32[]{:S(2)}) copy-start(s32[128]{0:T(128)} %param.7) | copy-start | bytes 1540
  7.2 10.6 %copy-start.4 = (s32[8,64]{1,0:T(8,128)S(1)}, s32[8,64]{1,0:T(8,128)}, u32[]{:S(2)}) copy-start(s32[8,64]{1,0:T(8,128)} %param.8) | copy-start | bytes 6148
  7.2 10.9 %copy-start.2 = (bf16[2048,512]{1,0:T(8,128)(2,1)S(1)}, bf16[2048,512]{1,0:T(8,128)(2,1)}, u32[]{:S(2)}) copy-start(bf16[2048,512]{1,0:T(8,128)(2,1)} %param.6) | copy-start | bytes 6291460
  7.2 122.9 %all-gather.2.cloned.1.call-start = ((), (), s32[]{:S(2)}) async-start(), calls=%async_computation.1 | async-start | bytes 12976128 | tf_op jit(solution)/shard_map/all_gather | solution.py:120
  25.4 54.3 %all-to-all-start = ((bf16[8,8,2,128,128]{4,3,2,1,0:T(8,128)(2,1)}), bf16[8,8,2,128,128]{4,3,2,1,0:T(8,128)(2,1)}, u32[]{:S(2)}, u32[]{:S(2)}) async-start(bf16[8,8,2,128,128]{4,3,2,1,0:T(8,128)(2,1)} %bitcast.54), calls=%async_computation | async-start | bytes 8388608 | tf_op jit(solution)/shard_map/all_to_all | solution.py:109
  130.1 10.8 %copy-start.3 = (bf16[256,768]{1,0:T(8,128)(2,1)S(1)}, bf16[256,768]{1,0:T(8,128)(2,1)}, u32[]{:S(2)}) copy-start(bf16[256,768]{1,0:T(8,128)(2,1)} %fusion.12) | copy-start | bytes 1179652
  140.9 41.4 %copy-start.5 = (bf16[256,768]{1,0:T(8,128)(2,1)}, bf16[256,768]{1,0:T(8,128)(2,1)S(1)}, u32[]{:S(2)}) copy-start(bf16[256,768]{1,0:T(8,128)(2,1)S(1)} %fusion.9) | copy-start | bytes 1179652
Sparse Core Ops, SparseCore 0:
  11.8 118.3 all-gather.1

commit v5 on v2

--- a/solution.py
+++ b/solution.py
@@ -128,7 +128,10 @@
     part = (-lax.dot_general(scaled, cross, contract, preferred_element_type=jnp.float32)).astype(
         jnp.bfloat16
     )
-    shared = scatter_sum(part.reshape(pan_count, pivot_rows, P_SIZE), pan_count)
+    slab_rows = pivot_rows * P_SIZE // BLK
+    shared = scatter_sum(part.reshape(pan_count, slab_rows, BLK), pan_count).reshape(
+        pivot_rows, P_SIZE
+    )
     own_columns = lax.dynamic_slice_in_dim(inverse_pivot, pan_idx * pivot_rows, pivot_rows, 1)
     triangle = lax.dot_general(
         own_columns, inverse_pivot, contract, preferred_element_type=jnp.float32

time: 188 us -> 189 us (level)
  local copies, waits for them, and re-layouts: 25.1 us -> 27.8 us
  matrix products: 14.5 us -> 12.6 us
    reshape x0 -> x2, local copies, waits for them, and re-layouts: none -> 2.76 us  [the longest x1 1.86 us: per_device(): part.reshape(pan_count, slab_rows, BLK)]
where the time goes in v5:
time: 189 us; the launch traced here: 188 us
  waiting for transfers between devices  81.3 us (43%)
  Pallas kernels  37.6 us (20%)
  local copies, waits for them, and re-layouts  27.8 us (15%)
  between operations  14.2 us (8%)
  matrix products  12.6 us (7%)
  other arithmetic  9.59 us (5%)
  starting transfers between devices  4.64 us (2%)
    all_to_all x1, waiting for transfers between devices, per_device(): lax.all_to_all(outgoing, 'grp', split_axis=0, concat_axis=0, tiled=True)  47.4 us
    pallas_call x1, Pallas kernels, scatter_sum(): pl.pallas_call(lambda *refs: _scatter_sum_kernel(n, *refs), out_shape=jax...  37.6 us
    all_gather x1, waiting for transfers between devices, per_device(): full = lax.all_gather(scaled, 'pan', axis=0, tiled=True)  33.9 us
    dot_general x1, matrix products, per_device(): lax.dot_general(sigma, full.reshape(front_len, BLK, P_SIZE), (((0, 2), (0...  8.79 us
    dot_general x1, local copies, waits for them, and re-layouts, per_device(): lax.dot_general(sigma, full.reshape(front_len, BLK, P_SIZE), (((0, 2), (0...  6.42 us
    gather x1, local copies, waits for them, and re-layouts, per_device(): jnp.take(received.reshape(groups * per_src, rb_local, BLK, BLK), order, a...  5.2 us
    select_n x2, other arithmetic, per_device(): jnp.take(received.reshape(groups * per_src, rb_local, BLK, BLK), order, a...  4.9 us
    all_to_all x1, starting transfers between devices, per_device(): lax.all_to_all(outgoing, 'grp', split_axis=0, concat_axis=0, tiled=True)  4.61 us
  transfers between devices with their start and end apart: 2, of which 2 were waited for; matrix products, arithmetic and copies ran while one was open for 17% of the time, Pallas kernels for 0%

profile of v5, /device:TPU:70, one launch (start us, length us, event | category | flops | bytes accessed | tf_op | source)
XLA Modules:
  0.0 187.7 jit_solution(7917615189177063350)
XLA Ops:
  7.3 1.4 dynamic_slice.16
  8.7 0.7 add_compare_fusion
  9.4 2.2 %fusion.3 = bf16[256,768]{1,0:T(8,128)(2,1)} fusion(bf16[1,768,768]{2,1,0:T(8,128)(2,1)S(1)} %copy-done, bf16[1,256,768]{2,1,0:T(8,128)(2,1)} %param.10, pred[256]{0:T(512)(128)(4,1)S(1)} %broadcast_bitcast_fusion), kind=kOutput, calls=%fused_computation.12 | convolution fusion | flops 302383104 | bytes 1966336 | tf_op jit(solution)/shard_map/dot_general | solution.py:117
  11.7 1.4 gather_fusion
  13.0 1.6 sort.34
  14.7 0.1 copy.20
  14.8 0.1 add.142
  15.0 0.2 dynamic-slice_reduce_fusion
  15.2 0.8 copy.23
  16.0 0.6 gather_fusion.1
  16.6 0.1 reshape.190
  16.7 0.8 gather_fusion.2
  17.6 0.1 fusion.17
  18.0 0.1 reshape.196
  18.1 2.1 %reshape.213 = bf16[16,128,4,128]{3,2,1,0:T(4,128)(2,1)} reshape(bf16[2048,512]{1,0:T(8,128)(2,1)S(1)} %copy-done.2) | data formatting | bytes 4194304 | tf_op jit(solution)/shard_map/reshape | solution.py:107
  20.2 2.1 %copy.27 = bf16[16,128,4,128]{3,1,2,0:T(8,128)(2,1)S(1)} copy(bf16[16,128,4,128]{3,2,1,0:T(4,128)(2,1)} %reshape.213) | data formatting | bytes 4194304 | tf_op jit(solution)/shard_map/reshape | solution.py:107
  22.4 3.1 %gather_fusion.3 = bf16[128,128,128]{2,1,0:T(8,128)(2,1)} fusion(bf16[16,128,4,128]{3,1,2,0:T(8,128)(2,1)S(1)} %copy.27, s32[128]{0:T(128)S(1)} %reshape.196), kind=kCustom, calls=%fused_computation.3 | custom fusion | bytes 8389632 | tf_op jit(solution)/shard_map/gather | solution.py:108
  25.4 4.6 %all-to-all-start = ((bf16[8,8,2,128,128]{4,3,2,1,0:T(8,128)(2,1)}), bf16[8,8,2,128,128]{4,3,2,1,0:T(8,128)(2,1)}, u32[]{:S(2)}, u32[]{:S(2)}) async-start(bf16[8,8,2,128,128]{4,3,2,1,0:T(8,128)(2,1)} %bitcast.59), calls=%async_computation | async-start | bytes 8388608 | tf_op jit(solution)/shard_map/all_to_all | solution.py:109
  30.1 0.1 copy.21
  30.2 0.1 add.137
  30.3 2.0 %sort.35 = (s32[64]{0:T(128)}, s32[64]{0:T(128)S(1)}) sort(s32[64]{0:T(128)S(1)} %add.137, s32[64]{0:T(128)S(1)} %iota.27), dimensions={0}, to_apply=%region_1.2 | sort | flops 384 | bytes 1024 | tf_op jit(solution)/shard_map/jit(argsort)/sort | solution.py:110
  32.4 47.4 %all-to-all-done = bf16[8,8,2,128,128]{4,3,2,1,0:T(8,128)(2,1)} async-done(((bf16[8,8,2,128,128]{4,3,2,1,0:T(8,128)(2,1)}), bf16[8,8,2,128,128]{4,3,2,1,0:T(8,128)(2,1)}, u32[]{:S(2)}, u32[]{:S(2)}) %all-to-all-start) | async-done | bytes 4194336 | tf_op jit(solution)/shard_map/all_to_all | solution.py:109
  79.7 5.2 %gather_fusion.4 = bf16[64,2,128,128]{3,2,1,0:T(8,128)(2,1)} fusion(bf16[64,2,128,128]{3,2,1,0:T(8,128)(2,1)} %bitcast.8, s32[1024]{0:T(1024)S(1)} %pad_clamp_fusion), kind=kCustom, calls=%fused_computation.4 | custom fusion | bytes 8388864 | tf_op jit(solution)/shard_map/jit(_take)/gather | solution.py:111
  84.9 4.9 %select_bitcast_fusion = bf16[2,128,64,128]{1,3,0,2:T(8,128)(2,1)} fusion(bf16[64,2,128,128]{3,2,1,0:T(8,128)(2,1)} %gather_fusion.4, pred[64]{0:T(512)(128)(4,1)S(1)} %compare_and_fusion.1), kind=kLoop, calls=%fused_computation.5 | loop fusion | flops 2097152 | bytes 8388672 | tf_op jit(solution)/shard_map/jit(_take)/select_n | solution.py:111
  89.8 6.4 %copy.32 = bf16[2,128,64,128]{3,1,0,2:T(8,128)(2,1)} copy(bf16[2,128,64,128]{1,3,0,2:T(8,128)(2,1)} %select_bitcast_fusion) | data formatting | bytes 8388608 | tf_op jit(solution)/shard_map/dot_general | solution.py:120
  96.2 33.9 %all-gather.2.cloned.1.call-done = bf16[8192,768]{1,0:T(8,128)(2,1)} async-done(((bf16[256,768]{1,0:T(8,128)(2,1)}), bf16[8192,768]{1,0:T(8,128)(2,1)}) %all-gather.2.cloned.1.call-update) | async-done | bytes 12582928 | tf_op jit(solution)/shard_map/all_gather | solution.py:119
  130.1 8.8 %fusion.2 = bf16[256,768]{1,0:T(8,128)(2,1)S(1)} fusion(bf16[256,64,128]{2,0,1:T(8,128)(2,1)} %bitcast.60, bf16[64,128,768]{2,1,0:T(8,128)(2,1)} %bitcast.63, pred[256]{0:T(512)(128)(4,1)S(1)} %broadcast_bitcast_fusion), kind=kOutput, calls=%fused_computation.11 | convolution fusion | flops 3221815296 | bytes 17170688 | tf_op jit(solution)/shard_map/dot_general | solution.py:120
  139.0 0.5 negate_convert_fusion
  139.5 1.9 reshape.170.refs_0_
  141.4 37.6 %shard_map.77 = f32[144,128]{1,0:T(8,128)} custom-call(bf16[32,144,128]{2,1,0:T(8,128)(2,1)} %reshape.170.refs_0_), custom_call_target="tpu_custom_call" | custom-call | tf_op jit(solution)/shard_map/pallas_call | solution.py:64
  178.9 0.9 reshape.171
  179.8 1.0 fusion.10
  (40 shorter events, 0.9 us)
Async XLA Ops:
  7.2 2.2 %copy-start = (bf16[1,768,768]{2,1,0:T(8,128)(2,1)S(1)}, bf16[1,768,768]{2,1,0:T(8,128)(2,1)}, u32[]{:S(2)}) copy-start(bf16[1,768,768]{2,1,0:T(8,128)(2,1)} %param.11) | copy-start | bytes 3538948
  7.2 9.5 %copy-start.1 = (s32[128]{0:T(128)S(1)}, s32[128]{0:T(128)}, u32[]{:S(2)}) copy-start(s32[128]{0:T(128)} %param.7) | copy-start | bytes 1540
  7.2 10.6 %copy-start.4 = (s32[8,64]{1,0:T(8,128)S(1)}, s32[8,64]{1,0:T(8,128)}, u32[]{:S(2)}) copy-start(s32[8,64]{1,0:T(8,128)} %param.8) | copy-start | bytes 6148
  7.2 10.9 %copy-start.2 = (bf16[2048,512]{1,0:T(8,128)(2,1)S(1)}, bf16[2048,512]{1,0:T(8,128)(2,1)}, u32[]{:S(2)}) copy-start(bf16[2048,512]{1,0:T(8,128)(2,1)} %param.6) | copy-start | bytes 6291460
  7.2 122.9 %all-gather.2.cloned.1.call-start = ((), (), s32[]{:S(2)}) async-start(), calls=%async_computation.1 | async-start | bytes 12976128 | tf_op jit(solution)/shard_map/all_gather | solution.py:119
  25.4 54.3 %all-to-all-start = ((bf16[8,8,2,128,128]{4,3,2,1,0:T(8,128)(2,1)}), bf16[8,8,2,128,128]{4,3,2,1,0:T(8,128)(2,1)}, u32[]{:S(2)}, u32[]{:S(2)}) async-start(bf16[8,8,2,128,128]{4,3,2,1,0:T(8,128)(2,1)} %bitcast.59), calls=%async_computation | async-start | bytes 8388608 | tf_op jit(solution)/shard_map/all_to_all | solution.py:109
  130.1 8.8 %copy-start.3 = (bf16[256,768]{1,0:T(8,128)(2,1)S(1)}, bf16[256,768]{1,0:T(8,128)(2,1)}, u32[]{:S(2)}) copy-start(bf16[256,768]{1,0:T(8,128)(2,1)} %fusion.3) | copy-start | bytes 1179652
  138.9 41.9 %copy-start.5 = (bf16[256,768]{1,0:T(8,128)(2,1)}, bf16[256,768]{1,0:T(8,128)(2,1)S(1)}, u32[]{:S(2)}) copy-start(bf16[256,768]{1,0:T(8,128)(2,1)S(1)} %fusion.2) | copy-start | bytes 1179652
Sparse Core Ops, SparseCore 0:
  11.8 118.3 all-gather.1

commit v6 on v2

--- a/solution.py
+++ b/solution.py
@@ -13,16 +13,6 @@
     me = lax.axis_index("pan")
     grp = lax.axis_index("grp")
     mesh_ids = pl.DeviceIdType.MESH
-
-    barrier = pltpu.get_barrier_semaphore()
-
-    def greet(k, carry):
-        peer = lax.rem(me + k, n)
-        pl.semaphore_signal(barrier, 1, device_id=(grp, peer), device_id_type=mesh_ids)
-        return carry
-
-    lax.fori_loop(1, n, greet, 0)
-    pl.semaphore_wait(barrier, n - 1)
 
     own = pltpu.make_async_copy(part_ref.at[me], buf.at[0], local_sem)
     own.start()
@@ -72,7 +62,7 @@
             pltpu.SemaphoreType.DMA((n,)),
             pltpu.SemaphoreType.DMA,
         ],
-        compiler_params=pltpu.CompilerParams(collective_id=0, has_side_effects=True),
+        compiler_params=pltpu.CompilerParams(has_side_effects=True),
     )(part)
 
 

time: 188 us -> 197 us (1.048); the launches traced: 187 us -> 194 us
  Pallas kernels: 37.5 us -> 44.2 us
    pallas_call x1, Pallas kernels: 37.5 us -> 44.2 us  [scatter_sum(): pl.pallas_call(lambda *refs: _scatter_sum_kernel(n, *refs), out_shape=jax...]
where the time goes in v6:
time: 197 us; the launch traced here: 194 us
  waiting for transfers between devices  81.3 us (41%)
  Pallas kernels  44.2 us (22%)
  local copies, waits for them, and re-layouts  25.1 us (13%)
  matrix products  14.5 us (7%)
  between operations  14.2 us (7%)
  other arithmetic  9.59 us (5%)
  starting transfers between devices  4.64 us (2%)
    all_to_all x1, waiting for transfers between devices, per_device(): lax.all_to_all(outgoing, 'grp', split_axis=0, concat_axis=0, tiled=True)  47.4 us
    pallas_call x1, Pallas kernels, scatter_sum(): pl.pallas_call(lambda *refs: _scatter_sum_kernel(n, *refs), out_shape=jax...  44.2 us
    all_gather x1, waiting for transfers between devices, per_device(): full = lax.all_gather(scaled, 'pan', axis=0, tiled=True)  33.9 us
    dot_general x1, matrix products, per_device(): lax.dot_general(sigma, full.reshape(front_len, BLK, P_SIZE), (((0, 2), (0...  8.79 us
    dot_general x1, local copies, waits for them, and re-layouts, per_device(): lax.dot_general(sigma, full.reshape(front_len, BLK, P_SIZE), (((0, 2), (0...  6.42 us
    gather x1, local copies, waits for them, and re-layouts, per_device(): jnp.take(received.reshape(groups * per_src, rb_local, BLK, BLK), order, a...  5.2 us
    select_n x2, other arithmetic, per_device(): jnp.take(received.reshape(groups * per_src, rb_local, BLK, BLK), order, a...  4.9 us
    all_to_all x1, starting transfers between devices, per_device(): lax.all_to_all(outgoing, 'grp', split_axis=0, concat_axis=0, tiled=True)  4.61 us
  transfers between devices with their start and end apart: 2, of which 2 were waited for; matrix products, arithmetic and copies ran while one was open for 17% of the time, Pallas kernels for 0%

profile of v6, /device:TPU:70, one launch (start us, length us, event | category | flops | bytes accessed | tf_op | source)
XLA Modules:
  0.0 193.5 jit_solution(11897337213538016205)
XLA Ops:
  7.3 1.4 dynamic_slice.16
  8.7 0.7 add_compare_fusion
  9.4 2.2 %fusion.3 = bf16[256,768]{1,0:T(8,128)(2,1)} fusion(bf16[1,768,768]{2,1,0:T(8,128)(2,1)S(1)} %copy-done, bf16[1,256,768]{2,1,0:T(8,128)(2,1)} %param.10, pred[256]{0:T(512)(128)(4,1)S(1)} %broadcast_bitcast_fusion), kind=kOutput, calls=%fused_computation.12 | convolution fusion | flops 302383104 | bytes 1966336 | tf_op jit(solution)/shard_map/dot_general | solution.py:107
  11.7 1.4 gather_fusion
  13.0 1.6 sort.34
  14.7 0.1 mul.53
  14.7 0.1 copy.20
  14.8 0.1 add.142
  15.0 0.2 dynamic-slice_reduce_fusion
  15.2 0.8 copy.23
  16.0 0.6 gather_fusion.1
  16.6 0.1 reshape.186
  16.7 0.8 gather_fusion.2
  17.5 0.1 reshape.185
  17.6 0.1 fusion.17
  18.0 0.1 reshape.192
  18.1 2.1 %reshape.209 = bf16[16,128,4,128]{3,2,1,0:T(4,128)(2,1)} reshape(bf16[2048,512]{1,0:T(8,128)(2,1)S(1)} %copy-done.2) | data formatting | bytes 4194304 | tf_op jit(solution)/shard_map/reshape | solution.py:97
  20.2 2.1 %copy.27 = bf16[16,128,4,128]{3,1,2,0:T(8,128)(2,1)S(1)} copy(bf16[16,128,4,128]{3,2,1,0:T(4,128)(2,1)} %reshape.209) | data formatting | bytes 4194304 | tf_op jit(solution)/shard_map/reshape | solution.py:97
  22.4 3.1 %gather_fusion.3 = bf16[128,128,128]{2,1,0:T(8,128)(2,1)} fusion(bf16[16,128,4,128]{3,1,2,0:T(8,128)(2,1)S(1)} %copy.27, s32[128]{0:T(128)S(1)} %reshape.192), kind=kCustom, calls=%fused_computation.3 | custom fusion | bytes 8389632 | tf_op jit(solution)/shard_map/gather | solution.py:98
  25.4 4.6 %all-to-all-start = ((bf16[8,8,2,128,128]{4,3,2,1,0:T(8,128)(2,1)}), bf16[8,8,2,128,128]{4,3,2,1,0:T(8,128)(2,1)}, u32[]{:S(2)}, u32[]{:S(2)}) async-start(bf16[8,8,2,128,128]{4,3,2,1,0:T(8,128)(2,1)} %bitcast.60), calls=%async_computation | async-start | bytes 8388608 | tf_op jit(solution)/shard_map/all_to_all | solution.py:99
  30.1 0.1 copy.21
  30.2 0.1 add.137
  30.3 2.0 %sort.35 = (s32[64]{0:T(128)}, s32[64]{0:T(128)S(1)}) sort(s32[64]{0:T(128)S(1)} %add.137, s32[64]{0:T(128)S(1)} %iota.27), dimensions={0}, to_apply=%region_1.2 | sort | flops 384 | bytes 1024 | tf_op jit(solution)/shard_map/jit(argsort)/sort | solution.py:100
  32.4 47.4 %all-to-all-done = bf16[8,8,2,128,128]{4,3,2,1,0:T(8,128)(2,1)} async-done(((bf16[8,8,2,128,128]{4,3,2,1,0:T(8,128)(2,1)}), bf16[8,8,2,128,128]{4,3,2,1,0:T(8,128)(2,1)}, u32[]{:S(2)}, u32[]{:S(2)}) %all-to-all-start) | async-done | bytes 4194336 | tf_op jit(solution)/shard_map/all_to_all | solution.py:99
  79.7 5.2 %gather_fusion.4 = bf16[64,2,128,128]{3,2,1,0:T(8,128)(2,1)} fusion(bf16[64,2,128,128]{3,2,1,0:T(8,128)(2,1)} %bitcast.8, s32[1024]{0:T(1024)S(1)} %pad_clamp_fusion), kind=kCustom, calls=%fused_computation.4 | custom fusion | bytes 8388864 | tf_op jit(solution)/shard_map/jit(_take)/gather | solution.py:101
  84.9 4.9 %select_bitcast_fusion = bf16[2,128,64,128]{1,3,0,2:T(8,128)(2,1)} fusion(bf16[64,2,128,128]{3,2,1,0:T(8,128)(2,1)} %gather_fusion.4, pred[64]{0:T(512)(128)(4,1)S(1)} %compare_and_fusion.1), kind=kLoop, calls=%fused_computation.5 | loop fusion | flops 2097152 | bytes 8388672 | tf_op jit(solution)/shard_map/jit(_take)/select_n | solution.py:101
  89.8 6.4 %copy.32 = bf16[2,128,64,128]{3,1,0,2:T(8,128)(2,1)} copy(bf16[2,128,64,128]{1,3,0,2:T(8,128)(2,1)} %select_bitcast_fusion) | data formatting | bytes 8388608 | tf_op jit(solution)/shard_map/dot_general | solution.py:110
  96.2 33.9 %all-gather.2.cloned.1.call-done = bf16[8192,768]{1,0:T(8,128)(2,1)} async-done(((bf16[256,768]{1,0:T(8,128)(2,1)}), bf16[8192,768]{1,0:T(8,128)(2,1)}) %all-gather.2.cloned.1.call-update) | async-done | bytes 12582928 | tf_op jit(solution)/shard_map/all_gather | solution.py:109
  130.1 8.8 %fusion.2 = bf16[256,768]{1,0:T(8,128)(2,1)S(1)} fusion(bf16[256,64,128]{2,0,1:T(8,128)(2,1)} %bitcast.61, bf16[64,128,768]{2,1,0:T(8,128)(2,1)} %bitcast.65, pred[256]{0:T(512)(128)(4,1)S(1)} %broadcast_bitcast_fusion), kind=kOutput, calls=%fused_computation.11 | convolution fusion | flops 3221815296 | bytes 17170688 | tf_op jit(solution)/shard_map/dot_general | solution.py:110
  139.0 1.5 negate_convert_fusion
  140.5 44.2 %shard_map.77 = f32[24,768]{1,0:T(8,128)} custom-call(bf16[32,24,768]{2,1,0:T(8,128)(2,1)} %bitcast.62), custom_call_target="tpu_custom_call" | custom-call | tf_op jit(solution)/shard_map/pallas_call | solution.py:54
  184.7 1.9 fusion.10
  (38 shorter events, 0.7 us)
Async XLA Ops:
  7.2 2.2 %copy-start = (bf16[1,768,768]{2,1,0:T(8,128)(2,1)S(1)}, bf16[1,768,768]{2,1,0:T(8,128)(2,1)}, u32[]{:S(2)}) copy-start(bf16[1,768,768]{2,1,0:T(8,128)(2,1)} %param.11) | copy-start | bytes 3538948
  7.2 9.5 %copy-start.1 = (s32[128]{0:T(128)S(1)}, s32[128]{0:T(128)}, u32[]{:S(2)}) copy-start(s32[128]{0:T(128)} %param.7) | copy-start | bytes 1540
  7.2 10.6 %copy-start.4 = (s32[8,64]{1,0:T(8,128)S(1)}, s32[8,64]{1,0:T(8,128)}, u32[]{:S(2)}) copy-start(s32[8,64]{1,0:T(8,128)} %param.8) | copy-start | bytes 6148
  7.2 10.9 %copy-start.2 = (bf16[2048,512]{1,0:T(8,128)(2,1)S(1)}, bf16[2048,512]{1,0:T(8,128)(2,1)}, u32[]{:S(2)}) copy-start(bf16[2048,512]{1,0:T(8,128)(2,1)} %param.6) | copy-start | bytes 6291460
  7.2 122.9 %all-gather.2.cloned.1.call-start = ((), (), s32[]{:S(2)}) async-start(), calls=%async_computation.1 | async-start | bytes 12976128 | tf_op jit(solution)/shard_map/all_gather | solution.py:109
  25.4 54.3 %all-to-all-start = ((bf16[8,8,2,128,128]{4,3,2,1,0:T(8,128)(2,1)}), bf16[8,8,2,128,128]{4,3,2,1,0:T(8,128)(2,1)}, u32[]{:S(2)}, u32[]{:S(2)}) async-start(bf16[8,8,2,128,128]{4,3,2,1,0:T(8,128)(2,1)} %bitcast.60), calls=%async_computation | async-start | bytes 8388608 | tf_op jit(solution)/shard_map/all_to_all | solution.py:99
  130.1 8.8 %copy-start.3 = (bf16[256,768]{1,0:T(8,128)(2,1)S(1)}, bf16[256,768]{1,0:T(8,128)(2,1)}, u32[]{:S(2)}) copy-start(bf16[256,768]{1,0:T(8,128)(2,1)} %fusion.3) | copy-start | bytes 1179652
  138.9 47.7 %copy-start.5 = (bf16[256,768]{1,0:T(8,128)(2,1)}, bf16[256,768]{1,0:T(8,128)(2,1)S(1)}, u32[]{:S(2)}) copy-start(bf16[256,768]{1,0:T(8,128)(2,1)S(1)} %fusion.2) | copy-start | bytes 1179652
Sparse Core Ops, SparseCore 0:
  11.8 118.3 all-gather.1

commit v7 on v2

--- a/solution.py
+++ b/solution.py
@@ -1,3 +1,5 @@
+import functools
+
 import jax
 import jax.numpy as jnp
 from jax import lax
@@ -9,71 +11,122 @@
 P_SIZE = 768
 
 
-def _scatter_sum_kernel(n, part_ref, out_ref, buf, send_sem, recv_sem, local_sem):
+PAN_INNER = 4
+
+
+def _scatter_sum_kernel(
+    inner, outer, part_ref, out_ref, first, mid, second, sems, local_sem
+):
     me = lax.axis_index("pan")
     grp = lax.axis_index("grp")
+    row, col = me // inner, me % inner
     mesh_ids = pl.DeviceIdType.MESH
+    send1, recv1, send2, recv2 = sems
 
     barrier = pltpu.get_barrier_semaphore()
 
-    def greet(k, carry):
-        peer = lax.rem(me + k, n)
+    def greet_row(k, carry):
+        peer = row * inner + lax.rem(col + k, inner)
         pl.semaphore_signal(barrier, 1, device_id=(grp, peer), device_id_type=mesh_ids)
         return carry
 
-    lax.fori_loop(1, n, greet, 0)
-    pl.semaphore_wait(barrier, n - 1)
-
-    own = pltpu.make_async_copy(part_ref.at[me], buf.at[0], local_sem)
+    def greet_col(k, carry):
+        peer = lax.rem(row + k, outer) * inner + col
+        pl.semaphore_signal(barrier, 1, device_id=(grp, peer), device_id_type=mesh_ids)
+        return carry
+
+    lax.fori_loop(1, inner, greet_row, 0)
+    lax.fori_loop(1, outer, greet_col, 0)
+    pl.semaphore_wait(barrier, inner + outer - 2)
+
+    own = pltpu.make_async_copy(part_ref.at[:, col], first.at[0], local_sem)
     own.start()
 
-    def send(k):
-        peer = lax.rem(me + k, n)
+    def stage_one(k):
+        dest = lax.rem(col + k, inner)
         return pltpu.make_async_remote_copy(
-            src_ref=part_ref.at[peer],
-            dst_ref=buf.at[k],
-            send_sem=send_sem.at[k],
-            recv_sem=recv_sem.at[k],
-            device_id=(grp, peer),
+            src_ref=part_ref.at[:, dest],
+            dst_ref=first.at[k],
+            send_sem=send1.at[k],
+            recv_sem=recv1.at[k],
+            device_id=(grp, row * inner + dest),
             device_id_type=mesh_ids,
         )
 
-    def start(k, carry):
-        send(k).start()
-        return carry
-
-    def finish(k, carry):
-        send(k).wait()
-        return carry
-
-    lax.fori_loop(1, n, start, 0)
+    def start_one(k, carry):
+        stage_one(k).start()
+        return carry
+
+    def finish_one(k, carry):
+        stage_one(k).wait()
+        return carry
+
+    lax.fori_loop(1, inner, start_one, 0)
     own.wait()
-    lax.fori_loop(1, n, finish, 0)
-
-    out_ref[...] = buf[0].astype(jnp.float32)
-
-    def accumulate(k, carry):
-        out_ref[...] += buf[k].astype(jnp.float32)
-        return carry
-
-    lax.fori_loop(1, n, accumulate, 0)
+    lax.fori_loop(1, inner, finish_one, 0)
+
+    mid[...] = first[0].astype(jnp.float32)
+
+    def add_first(k, carry):
+        mid[...] += first[k].astype(jnp.float32)
+        return carry
+
+    lax.fori_loop(1, inner, add_first, 0)
+
+    def stage_two(k):
+        dest = lax.rem(row + k, outer)
+        return pltpu.make_async_remote_copy(
+            src_ref=mid.at[dest],
+            dst_ref=second.at[k],
+            send_sem=send2.at[k],
+            recv_sem=recv2.at[k],
+            device_id=(grp, dest * inner + col),
+            device_id_type=mesh_ids,
+        )
+
+    def start_two(k, carry):
+        stage_two(k).start()
+        return carry
+
+    def finish_two(k, carry):
+        stage_two(k).wait()
+        return carry
+
+    lax.fori_loop(1, outer, start_two, 0)
+    lax.fori_loop(1, outer, finish_two, 0)
+
+    out_ref[...] = mid[row]
+
+    def add_second(k, carry):
+        out_ref[...] += second[k]
+        return carry
+
+    lax.fori_loop(1, outer, add_second, 0)
 
 
 def scatter_sum(part, n):
     _, rows, cols = part.shape
+    inner = PAN_INNER
+    outer = n // inner
     return pl.pallas_call(
-        lambda *refs: _scatter_sum_kernel(n, *refs),
+        functools.partial(_scatter_sum_kernel, inner, outer),
         out_shape=jax.ShapeDtypeStruct((rows, cols), jnp.float32),
         in_specs=[pl.BlockSpec(memory_space=pl.ANY)],
         out_specs=pl.BlockSpec(memory_space=pltpu.VMEM),
         scratch_shapes=[
-            pltpu.VMEM((n, rows, cols), part.dtype),
-            pltpu.SemaphoreType.DMA((n,)),
-            pltpu.SemaphoreType.DMA((n,)),
+            pltpu.VMEM((inner, outer, rows, cols), part.dtype),
+            pltpu.VMEM((outer, rows, cols), jnp.float32),
+            pltpu.VMEM((outer, rows, cols), jnp.float32),
+            (
+                pltpu.SemaphoreType.DMA((inner,)),
+                pltpu.SemaphoreType.DMA((inner,)),
+                pltpu.SemaphoreType.DMA((outer,)),
+                pltpu.SemaphoreType.DMA((outer,)),
+            ),
             pltpu.SemaphoreType.DMA,
         ],
         compiler_params=pltpu.CompilerParams(collective_id=0, has_side_effects=True),
-    )(part)
+    )(part.reshape(outer, inner, rows, cols))
 
 
 def per_device(anc_rows, row_home, block_lists, front_blocks, panel, pivot_inverse):

time: 188 us -> 187 us (level)
  no operation moved by 1% of the time
where the time goes in v7:
time: 187 us; the launch traced here: 186 us
  waiting for transfers between devices  81.3 us (43%)
  Pallas kernels  36.8 us (20%)
  local copies, waits for them, and re-layouts  25.1 us (13%)
  matrix products  14.5 us (8%)
  between operations  14.2 us (8%)
  other arithmetic  9.59 us (5%)
  starting transfers between devices  4.64 us (2%)
    all_to_all x1, waiting for transfers between devices, per_device(): lax.all_to_all(outgoing, 'grp', split_axis=0, concat_axis=0, tiled=True)  47.4 us
    pallas_call x1, Pallas kernels, scatter_sum(): pl.pallas_call(functools.partial(_scatter_sum_kernel, inner, outer), out_...  36.8 us
    all_gather x1, waiting for transfers between devices, per_device(): full = lax.all_gather(scaled, 'pan', axis=0, tiled=True)  33.9 us
    dot_general x1, matrix products, per_device(): lax.dot_general(sigma, full.reshape(front_len, BLK, P_SIZE), (((0, 2), (0...  8.79 us
    dot_general x1, local copies, waits for them, and re-layouts, per_device(): lax.dot_general(sigma, full.reshape(front_len, BLK, P_SIZE), (((0, 2), (0...  6.42 us
    gather x1, local copies, waits for them, and re-layouts, per_device(): jnp.take(received.reshape(groups * per_src, rb_local, BLK, BLK), order, a...  5.2 us
    select_n x2, other arithmetic, per_device(): jnp.take(received.reshape(groups * per_src, rb_local, BLK, BLK), order, a...  4.9 us
    all_to_all x1, starting transfers between devices, per_device(): lax.all_to_all(outgoing, 'grp', split_axis=0, concat_axis=0, tiled=True)  4.61 us
  transfers between devices with their start and end apart: 2, of which 2 were waited for; matrix products, arithmetic and copies ran while one was open for 17% of the time, Pallas kernels for 0%

profile of v7, /device:TPU:70, one launch (start us, length us, event | category | flops | bytes accessed | tf_op | source)
XLA Modules:
  0.0 186.1 jit_solution(11613790157997080534)
XLA Ops:
  7.3 1.4 dynamic_slice.16
  8.7 0.7 add_compare_fusion
  9.4 2.2 %fusion.3 = bf16[256,768]{1,0:T(8,128)(2,1)} fusion(bf16[1,768,768]{2,1,0:T(8,128)(2,1)S(1)} %copy-done, bf16[1,256,768]{2,1,0:T(8,128)(2,1)} %param.10, pred[256]{0:T(512)(128)(4,1)S(1)} %broadcast_bitcast_fusion), kind=kOutput, calls=%fused_computation.12 | convolution fusion | flops 302383104 | bytes 1966336 | tf_op jit(solution)/shard_map/dot_general | solution.py:170
  11.7 1.4 gather_fusion
  13.0 1.6 sort.34
  14.7 0.1 mul.53
  14.7 0.1 copy.20
  14.8 0.1 add.142
  15.0 0.2 dynamic-slice_reduce_fusion
  15.2 0.8 copy.23
  16.0 0.6 gather_fusion.1
  16.6 0.1 reshape.182
  16.7 0.8 gather_fusion.2
  17.5 0.1 reshape.181
  17.6 0.1 fusion.17
  18.0 0.1 reshape.188
  18.1 2.1 %reshape.205 = bf16[16,128,4,128]{3,2,1,0:T(4,128)(2,1)} reshape(bf16[2048,512]{1,0:T(8,128)(2,1)S(1)} %copy-done.2) | data formatting | bytes 4194304 | tf_op jit(solution)/shard_map/reshape | solution.py:160
  20.2 2.1 %copy.27 = bf16[16,128,4,128]{3,1,2,0:T(8,128)(2,1)S(1)} copy(bf16[16,128,4,128]{3,2,1,0:T(4,128)(2,1)} %reshape.205) | data formatting | bytes 4194304 | tf_op jit(solution)/shard_map/reshape | solution.py:160
  22.4 3.1 %gather_fusion.3 = bf16[128,128,128]{2,1,0:T(8,128)(2,1)} fusion(bf16[16,128,4,128]{3,1,2,0:T(8,128)(2,1)S(1)} %copy.27, s32[128]{0:T(128)S(1)} %reshape.188), kind=kCustom, calls=%fused_computation.3 | custom fusion | bytes 8389632 | tf_op jit(solution)/shard_map/gather | solution.py:161
  25.4 4.6 %all-to-all-start = ((bf16[8,8,2,128,128]{4,3,2,1,0:T(8,128)(2,1)}), bf16[8,8,2,128,128]{4,3,2,1,0:T(8,128)(2,1)}, u32[]{:S(2)}, u32[]{:S(2)}) async-start(bf16[8,8,2,128,128]{4,3,2,1,0:T(8,128)(2,1)} %bitcast.60), calls=%async_computation | async-start | bytes 8388608 | tf_op jit(solution)/shard_map/all_to_all | solution.py:162
  30.1 0.1 copy.21
  30.2 0.1 add.137
  30.3 2.0 %sort.35 = (s32[64]{0:T(128)}, s32[64]{0:T(128)S(1)}) sort(s32[64]{0:T(128)S(1)} %add.137, s32[64]{0:T(128)S(1)} %iota.27), dimensions={0}, to_apply=%region_1.2 | sort | flops 384 | bytes 1024 | tf_op jit(solution)/shard_map/jit(argsort)/sort | solution.py:163
  32.4 47.4 %all-to-all-done = bf16[8,8,2,128,128]{4,3,2,1,0:T(8,128)(2,1)} async-done(((bf16[8,8,2,128,128]{4,3,2,1,0:T(8,128)(2,1)}), bf16[8,8,2,128,128]{4,3,2,1,0:T(8,128)(2,1)}, u32[]{:S(2)}, u32[]{:S(2)}) %all-to-all-start) | async-done | bytes 4194336 | tf_op jit(solution)/shard_map/all_to_all | solution.py:162
  79.7 5.2 %gather_fusion.4 = bf16[64,2,128,128]{3,2,1,0:T(8,128)(2,1)} fusion(bf16[64,2,128,128]{3,2,1,0:T(8,128)(2,1)} %bitcast.8, s32[1024]{0:T(1024)S(1)} %pad_clamp_fusion), kind=kCustom, calls=%fused_computation.4 | custom fusion | bytes 8388864 | tf_op jit(solution)/shard_map/jit(_take)/gather | solution.py:164
  84.9 4.9 %select_bitcast_fusion = bf16[2,128,64,128]{1,3,0,2:T(8,128)(2,1)} fusion(bf16[64,2,128,128]{3,2,1,0:T(8,128)(2,1)} %gather_fusion.4, pred[64]{0:T(512)(128)(4,1)S(1)} %compare_and_fusion.1), kind=kLoop, calls=%fused_computation.5 | loop fusion | flops 2097152 | bytes 8388672 | tf_op jit(solution)/shard_map/jit(_take)/select_n | solution.py:164
  89.8 6.4 %copy.32 = bf16[2,128,64,128]{3,1,0,2:T(8,128)(2,1)} copy(bf16[2,128,64,128]{1,3,0,2:T(8,128)(2,1)} %select_bitcast_fusion) | data formatting | bytes 8388608 | tf_op jit(solution)/shard_map/dot_general | solution.py:173
  96.2 33.9 %all-gather.2.cloned.1.call-done = bf16[8192,768]{1,0:T(8,128)(2,1)} async-done(((bf16[256,768]{1,0:T(8,128)(2,1)}), bf16[8192,768]{1,0:T(8,128)(2,1)}) %all-gather.2.cloned.1.call-update) | async-done | bytes 12582928 | tf_op jit(solution)/shard_map/all_gather | solution.py:172
  130.1 8.8 %fusion.2 = bf16[256,768]{1,0:T(8,128)(2,1)S(1)} fusion(bf16[256,64,128]{2,0,1:T(8,128)(2,1)} %bitcast.61, bf16[64,128,768]{2,1,0:T(8,128)(2,1)} %bitcast.65, pred[256]{0:T(512)(128)(4,1)S(1)} %broadcast_bitcast_fusion), kind=kOutput, calls=%fused_computation.11 | convolution fusion | flops 3221815296 | bytes 17170688 | tf_op jit(solution)/shard_map/dot_general | solution.py:173
  139.0 1.5 negate_convert_fusion
  140.5 36.8 %shard_map.77 = f32[24,768]{1,0:T(8,128)} custom-call(bf16[8,4,24,768]{3,2,1,0:T(8,128)(2,1)} %bitcast.62), custom_call_target="tpu_custom_call" | custom-call | tf_op jit(solution)/shard_map/pallas_call | solution.py:111
  177.3 1.9 %fusion.10 = f32[1,24,768]{2,1,0:T(8,128)} fusion(f32[24,768]{1,0:T(8,128)} %shard_map.77, bf16[1,768,768]{2,1,0:T(8,128)(2,1)S(1)} %copy-done, s32[]{:T(128)S(6)} %select_n.138), kind=kOutput, calls=%fused_computation.17 | convolution fusion | flops 28329984 | bytes 1523716 | tf_op jit(solution)/shard_map/dot_general | solution.py:186
  (38 shorter events, 0.7 us)
Async XLA Ops:
  7.2 2.2 %copy-start = (bf16[1,768,768]{2,1,0:T(8,128)(2,1)S(1)}, bf16[1,768,768]{2,1,0:T(8,128)(2,1)}, u32[]{:S(2)}) copy-start(bf16[1,768,768]{2,1,0:T(8,128)(2,1)} %param.11) | copy-start | bytes 3538948
  7.2 9.5 %copy-start.1 = (s32[128]{0:T(128)S(1)}, s32[128]{0:T(128)}, u32[]{:S(2)}) copy-start(s32[128]{0:T(128)} %param.7) | copy-start | bytes 1540
  7.2 10.6 %copy-start.4 = (s32[8,64]{1,0:T(8,128)S(1)}, s32[8,64]{1,0:T(8,128)}, u32[]{:S(2)}) copy-start(s32[8,64]{1,0:T(8,128)} %param.8) | copy-start | bytes 6148
  7.2 10.9 %copy-start.2 = (bf16[2048,512]{1,0:T(8,128)(2,1)S(1)}, bf16[2048,512]{1,0:T(8,128)(2,1)}, u32[]{:S(2)}) copy-start(bf16[2048,512]{1,0:T(8,128)(2,1)} %param.6) | copy-start | bytes 6291460
  7.2 122.9 %all-gather.2.cloned.1.call-start = ((), (), s32[]{:S(2)}) async-start(), calls=%async_computation.1 | async-start | bytes 12976128 | tf_op jit(solution)/shard_map/all_gather | solution.py:172
  25.4 54.3 %all-to-all-start = ((bf16[8,8,2,128,128]{4,3,2,1,0:T(8,128)(2,1)}), bf16[8,8,2,128,128]{4,3,2,1,0:T(8,128)(2,1)}, u32[]{:S(2)}, u32[]{:S(2)}) async-start(bf16[8,8,2,128,128]{4,3,2,1,0:T(8,128)(2,1)} %bitcast.60), calls=%async_computation | async-start | bytes 8388608 | tf_op jit(solution)/shard_map/all_to_all | solution.py:162
  130.1 8.8 %copy-start.3 = (bf16[256,768]{1,0:T(8,128)(2,1)S(1)}, bf16[256,768]{1,0:T(8,128)(2,1)}, u32[]{:S(2)}) copy-start(bf16[256,768]{1,0:T(8,128)(2,1)} %fusion.3) | copy-start | bytes 1179652
  138.9 40.3 %copy-start.5 = (bf16[256,768]{1,0:T(8,128)(2,1)}, bf16[256,768]{1,0:T(8,128)(2,1)S(1)}, u32[]{:S(2)}) copy-start(bf16[256,768]{1,0:T(8,128)(2,1)S(1)} %fusion.2) | copy-start | bytes 1179652
Sparse Core Ops, SparseCore 0:
  11.8 118.3 all-gather.1

commit v8 on v2

--- a/solution.py
+++ b/solution.py
@@ -128,7 +128,10 @@
     part = (-lax.dot_general(scaled, cross, contract, preferred_element_type=jnp.float32)).astype(
         jnp.bfloat16
     )
-    shared = scatter_sum(part.reshape(pan_count, pivot_rows, P_SIZE), pan_count)
+    pieces = lax.all_to_all(
+        part.reshape(pan_count, pivot_rows, P_SIZE), "pan", split_axis=0, concat_axis=0, tiled=True
+    )
+    shared = jnp.sum(pieces.astype(jnp.float32), axis=0)
     own_columns = lax.dynamic_slice_in_dim(inverse_pivot, pan_idx * pivot_rows, pivot_rows, 1)
     triangle = lax.dot_general(
         own_columns, inverse_pivot, contract, preferred_element_type=jnp.float32

time: 188 us -> 190 us (1.011); the launches traced: 187 us -> 186 us
  Pallas kernels: 37.5 us -> 0 us
  waiting for transfers between devices: 81.3 us -> 110 us
  starting transfers between devices: 4.64 us -> 14 us
    pallas_call x1 -> x0, Pallas kernels: 37.5 us -> none  [scatter_sum(): pl.pallas_call(lambda *refs: _scatter_sum_kernel(n, *refs), out_shape=jax...]
    all_to_all x0 -> x1, waiting for transfers between devices: none -> 28.3 us  [per_device(): lax.all_to_all(part.reshape(pan_count, pivot_rows, P_SIZE), 'pan', split_...]
    all_to_all x0 -> x1, starting transfers between devices: none -> 9.36 us  [per_device(): lax.all_to_all(part.reshape(pan_count, pivot_rows, P_SIZE), 'pan', split_...]
  transfers between devices with their start and end apart: 2 -> 3, of which waited for: 2 -> 3; matrix products, arithmetic and copies ran while one was open for 17% -> 17% of each run, Pallas kernels for 0% -> 0%
where the time goes in v8:
time: 190 us; the launch traced here: 186 us
  waiting for transfers between devices  110 us (58%)
  local copies, waits for them, and re-layouts  25.1 us (13%)
  between operations  14.2 us (7%)
  starting transfers between devices  14 us (7%)
  matrix products  13.6 us (7%)
  other arithmetic  9.75 us (5%)
    all_to_all x1, waiting for transfers between devices, per_device(): lax.all_to_all(outgoing, 'grp', split_axis=0, concat_axis=0, tiled=True)  47.4 us
    all_gather x1, waiting for transfers between devices, per_device(): full = lax.all_gather(scaled, 'pan', axis=0, tiled=True)  33.9 us
    all_to_all x1, waiting for transfers between devices, per_device(): lax.all_to_all(part.reshape(pan_count, pivot_rows, P_SIZE), 'pan', split_...  28.3 us
    all_to_all x1, starting transfers between devices, per_device(): lax.all_to_all(part.reshape(pan_count, pivot_rows, P_SIZE), 'pan', split_...  9.36 us
    dot_general x1, matrix products, per_device(): lax.dot_general(sigma, full.reshape(front_len, BLK, P_SIZE), (((0, 2), (0...  8.79 us
    dot_general x1, local copies, waits for them, and re-layouts, per_device(): lax.dot_general(sigma, full.reshape(front_len, BLK, P_SIZE), (((0, 2), (0...  6.42 us
    gather x1, local copies, waits for them, and re-layouts, per_device(): jnp.take(received.reshape(groups * per_src, rb_local, BLK, BLK), order, a...  5.2 us
    select_n x2, other arithmetic, per_device(): jnp.take(received.reshape(groups * per_src, rb_local, BLK, BLK), order, a...  4.9 us
  transfers between devices with their start and end apart: 3, of which 3 were waited for; matrix products, arithmetic and copies ran while one was open for 17% of the time, Pallas kernels for 0%

profile of v8, /device:TPU:70, one launch (start us, length us, event | category | flops | bytes accessed | tf_op | source)
XLA Modules:
  0.0 186.2 jit_solution(3361466495713487284)
XLA Ops:
  7.3 1.4 dynamic_slice.16
  8.7 0.7 add_compare_fusion
  9.4 2.2 %fusion.3 = bf16[256,768]{1,0:T(8,128)(2,1)} fusion(bf16[1,768,768]{2,1,0:T(8,128)(2,1)S(1)} %copy-done, bf16[1,256,768]{2,1,0:T(8,128)(2,1)} %param.10, pred[256]{0:T(512)(128)(4,1)S(1)} %broadcast_bitcast_fusion), kind=kOutput, calls=%fused_computation.13 | convolution fusion | flops 302383104 | bytes 1966336 | tf_op jit(solution)/shard_map/dot_general | solution.py:117
  11.7 1.4 gather_fusion
  13.0 1.6 sort.34
  14.7 0.1 copy.20
  14.8 0.1 add.142
  15.0 0.2 dynamic-slice_reduce_fusion
  15.2 0.8 copy.23
  16.0 0.6 gather_fusion.1
  16.6 0.1 reshape.186
  16.7 0.8 gather_fusion.2
  17.6 0.1 fusion.17
  18.0 0.1 reshape.192
  18.1 2.1 %reshape.209 = bf16[16,128,4,128]{3,2,1,0:T(4,128)(2,1)} reshape(bf16[2048,512]{1,0:T(8,128)(2,1)S(1)} %copy-done.2) | data formatting | bytes 4194304 | tf_op jit(solution)/shard_map/reshape | solution.py:107
  20.2 2.1 %copy.27 = bf16[16,128,4,128]{3,1,2,0:T(8,128)(2,1)S(1)} copy(bf16[16,128,4,128]{3,2,1,0:T(4,128)(2,1)} %reshape.209) | data formatting | bytes 4194304 | tf_op jit(solution)/shard_map/reshape | solution.py:107
  22.4 3.1 %gather_fusion.3 = bf16[128,128,128]{2,1,0:T(8,128)(2,1)} fusion(bf16[16,128,4,128]{3,1,2,0:T(8,128)(2,1)S(1)} %copy.27, s32[128]{0:T(128)S(1)} %reshape.192), kind=kCustom, calls=%fused_computation.3 | custom fusion | bytes 8389632 | tf_op jit(solution)/shard_map/gather | solution.py:108
  25.4 4.6 %all-to-all-start = ((bf16[8,8,2,128,128]{4,3,2,1,0:T(8,128)(2,1)}), bf16[8,8,2,128,128]{4,3,2,1,0:T(8,128)(2,1)}, u32[]{:S(2)}, u32[]{:S(2)}) async-start(bf16[8,8,2,128,128]{4,3,2,1,0:T(8,128)(2,1)} %bitcast.60), calls=%async_computation | async-start | bytes 8388608 | tf_op jit(solution)/shard_map/all_to_all | solution.py:109
  30.1 0.1 copy.21
  30.2 0.1 add.137
  30.3 2.0 %sort.35 = (s32[64]{0:T(128)}, s32[64]{0:T(128)S(1)}) sort(s32[64]{0:T(128)S(1)} %add.137, s32[64]{0:T(128)S(1)} %iota.27), dimensions={0}, to_apply=%region_1.2 | sort | flops 384 | bytes 1024 | tf_op jit(solution)/shard_map/jit(argsort)/sort | solution.py:110
  32.4 47.4 %all-to-all-done = bf16[8,8,2,128,128]{4,3,2,1,0:T(8,128)(2,1)} async-done(((bf16[8,8,2,128,128]{4,3,2,1,0:T(8,128)(2,1)}), bf16[8,8,2,128,128]{4,3,2,1,0:T(8,128)(2,1)}, u32[]{:S(2)}, u32[]{:S(2)}) %all-to-all-start) | async-done | bytes 4194336 | tf_op jit(solution)/shard_map/all_to_all | solution.py:109
  79.7 5.2 %gather_fusion.4 = bf16[64,2,128,128]{3,2,1,0:T(8,128)(2,1)} fusion(bf16[64,2,128,128]{3,2,1,0:T(8,128)(2,1)} %bitcast.8, s32[1024]{0:T(1024)S(1)} %pad_clamp_fusion), kind=kCustom, calls=%fused_computation.4 | custom fusion | bytes 8388864 | tf_op jit(solution)/shard_map/jit(_take)/gather | solution.py:111
  84.9 4.9 %select_bitcast_fusion = bf16[2,128,64,128]{1,3,0,2:T(8,128)(2,1)} fusion(bf16[64,2,128,128]{3,2,1,0:T(8,128)(2,1)} %gather_fusion.4, pred[64]{0:T(512)(128)(4,1)S(1)} %compare_and_fusion.1), kind=kLoop, calls=%fused_computation.5 | loop fusion | flops 2097152 | bytes 8388672 | tf_op jit(solution)/shard_map/jit(_take)/select_n | solution.py:111
  89.8 6.4 %copy.32 = bf16[2,128,64,128]{3,1,0,2:T(8,128)(2,1)} copy(bf16[2,128,64,128]{1,3,0,2:T(8,128)(2,1)} %select_bitcast_fusion) | data formatting | bytes 8388608 | tf_op jit(solution)/shard_map/dot_general | solution.py:120
  96.2 33.9 %all-gather.2.cloned.1.call-done = bf16[8192,768]{1,0:T(8,128)(2,1)} async-done(((bf16[256,768]{1,0:T(8,128)(2,1)}), bf16[8192,768]{1,0:T(8,128)(2,1)}) %all-gather.2.cloned.1.call-update) | async-done | bytes 12582928 | tf_op jit(solution)/shard_map/all_gather | solution.py:119
  130.1 8.8 %fusion.2 = bf16[256,768]{1,0:T(8,128)(2,1)S(1)} fusion(bf16[256,64,128]{2,0,1:T(8,128)(2,1)} %bitcast.61, bf16[64,128,768]{2,1,0:T(8,128)(2,1)} %bitcast.64, pred[256]{0:T(512)(128)(4,1)S(1)} %broadcast_bitcast_fusion), kind=kOutput, calls=%fused_computation.12 | convolution fusion | flops 3221815296 | bytes 17170688 | tf_op jit(solution)/shard_map/dot_general | solution.py:120
  139.0 1.5 negate_convert_fusion
  140.5 9.4 %all-to-all-start.1 = ((bf16[32,24,768]{2,1,0:T(8,128)(2,1)}), bf16[32,24,768]{2,1,0:T(8,128)(2,1)S(1)}, u32[]{:S(2)}, u32[]{:S(2)}) async-start(bf16[32,24,768]{2,1,0:T(8,128)(2,1)} %bitcast.18), calls=%async_computation.1 | async-start | bytes 2359296 | tf_op jit(solution)/shard_map/all_to_all | solution.py:131
  149.9 28.3 %all-to-all-done.1 = bf16[32,24,768]{2,1,0:T(8,128)(2,1)S(1)} async-done(((bf16[32,24,768]{2,1,0:T(8,128)(2,1)}), bf16[32,24,768]{2,1,0:T(8,128)(2,1)S(1)}, u32[]{:S(2)}, u32[]{:S(2)}) %all-to-all-start.1) | async-done | bytes 1179680 | tf_op jit(solution)/shard_map/all_to_all | solution.py:131
  178.1 0.2 convert_reduce_fusion
  178.3 1.0 fusion.10
  (40 shorter events, 0.9 us)
Async XLA Ops:
  7.2 2.2 %copy-start = (bf16[1,768,768]{2,1,0:T(8,128)(2,1)S(1)}, bf16[1,768,768]{2,1,0:T(8,128)(2,1)}, u32[]{:S(2)}) copy-start(bf16[1,768,768]{2,1,0:T(8,128)(2,1)} %param.11) | copy-start | bytes 3538948
  7.2 9.5 %copy-start.1 = (s32[128]{0:T(128)S(1)}, s32[128]{0:T(128)}, u32[]{:S(2)}) copy-start(s32[128]{0:T(128)} %param.7) | copy-start | bytes 1540
  7.2 10.6 %copy-start.4 = (s32[8,64]{1,0:T(8,128)S(1)}, s32[8,64]{1,0:T(8,128)}, u32[]{:S(2)}) copy-start(s32[8,64]{1,0:T(8,128)} %param.8) | copy-start | bytes 6148
  7.2 10.9 %copy-start.2 = (bf16[2048,512]{1,0:T(8,128)(2,1)S(1)}, bf16[2048,512]{1,0:T(8,128)(2,1)}, u32[]{:S(2)}) copy-start(bf16[2048,512]{1,0:T(8,128)(2,1)} %param.6) | copy-start | bytes 6291460
  7.2 122.9 %all-gather.2.cloned.1.call-start = ((), (), s32[]{:S(2)}) async-start(), calls=%async_computation.2 | async-start | bytes 12976128 | tf_op jit(solution)/shard_map/all_gather | solution.py:119
  25.4 54.3 %all-to-all-start = ((bf16[8,8,2,128,128]{4,3,2,1,0:T(8,128)(2,1)}), bf16[8,8,2,128,128]{4,3,2,1,0:T(8,128)(2,1)}, u32[]{:S(2)}, u32[]{:S(2)}) async-start(bf16[8,8,2,128,128]{4,3,2,1,0:T(8,128)(2,1)} %bitcast.60), calls=%async_computation | async-start | bytes 8388608 | tf_op jit(solution)/shard_map/all_to_all | solution.py:109
  130.1 8.8 %copy-start.3 = (bf16[256,768]{1,0:T(8,128)(2,1)S(1)}, bf16[256,768]{1,0:T(8,128)(2,1)}, u32[]{:S(2)}) copy-start(bf16[256,768]{1,0:T(8,128)(2,1)} %fusion.3) | copy-start | bytes 1179652
  138.9 40.4 %copy-start.5 = (bf16[256,768]{1,0:T(8,128)(2,1)}, bf16[256,768]{1,0:T(8,128)(2,1)S(1)}, u32[]{:S(2)}) copy-start(bf16[256,768]{1,0:T(8,128)(2,1)S(1)} %fusion.2) | copy-start | bytes 1179652
  140.5 37.6 %all-to-all-start.1 = ((bf16[32,24,768]{2,1,0:T(8,128)(2,1)}), bf16[32,24,768]{2,1,0:T(8,128)(2,1)S(1)}, u32[]{:S(2)}, u32[]{:S(2)}) async-start(bf16[32,24,768]{2,1,0:T(8,128)(2,1)} %bitcast.18), calls=%async_computation.1 | async-start | bytes 2359296 | tf_op jit(solution)/shard_map/all_to_all | solution.py:131
Sparse Core Ops, SparseCore 0:
  11.8 118.3 all-gather.1

commit v9 on v2

--- a/solution.py
+++ b/solution.py
@@ -1,3 +1,5 @@
+import functools
+
 import jax
 import jax.numpy as jnp
 from jax import lax
@@ -7,6 +9,7 @@
 
 BLK = 128
 P_SIZE = 768
+SPREAD_COLS = 256
 
 
 def _scatter_sum_kernel(n, part_ref, out_ref, buf, send_sem, recv_sem, local_sem):
@@ -74,6 +77,67 @@
         ],
         compiler_params=pltpu.CompilerParams(collective_id=0, has_side_effects=True),
     )(part)
+
+
+def _spread_kernel(n, block_ref, out_ref, send_sem, recv_sem, local_sem):
+    me = lax.axis_index("pan")
+    grp = lax.axis_index("grp")
+    mesh_ids = pl.DeviceIdType.MESH
+
+    barrier = pltpu.get_barrier_semaphore()
+
+    def greet(k, carry):
+        peer = lax.rem(me + k, n)
+        pl.semaphore_signal(barrier, 1, device_id=(grp, peer), device_id_type=mesh_ids)
+        return carry
+
+    lax.fori_loop(1, n, greet, 0)
+    pl.semaphore_wait(barrier, n - 1)
+
+    own = pltpu.make_async_copy(block_ref, out_ref.at[0], local_sem)
+    own.start()
+
+    def send(k):
+        peer = lax.rem(me + k, n)
+        return pltpu.make_async_remote_copy(
+            src_ref=block_ref,
+            dst_ref=out_ref.at[k],
+            send_sem=send_sem.at[k],
+            recv_sem=recv_sem.at[k],
+            device_id=(grp, peer),
+            device_id_type=mesh_ids,
+        )
+
+    def start(k, carry):
+        send(k).start()
+        return carry
+
+    def finish(k, carry):
+        send(k).wait()
+        return carry
+
+    lax.fori_loop(1, n, start, 0)
+    own.wait()
+    lax.fori_loop(1, n, finish, 0)
+
+
+def spread(block, n):
+    rows, cols = block.shape
+    return pl.pallas_call(
+        functools.partial(_spread_kernel, n),
+        out_shape=jax.ShapeDtypeStruct((n, rows, cols), block.dtype),
+        in_specs=[pl.BlockSpec(memory_space=pl.ANY)],
+        out_specs=pl.BlockSpec(memory_space=pl.ANY),
+        scratch_shapes=[
+            pltpu.SemaphoreType.DMA((n,)),
+            pltpu.SemaphoreType.DMA((n,)),
+            pltpu.SemaphoreType.DMA,
+        ],
+        compiler_params=pltpu.CompilerParams(collective_id=1, has_side_effects=True),
+        cost_estimate=pl.CostEstimate(
+            flops=0, bytes_accessed=2 * n * rows * cols * block.dtype.itemsize, transcendentals=0
+        ),
+    )(block)
 
 
 def per_device(anc_rows, row_home, block_lists, front_blocks, panel, pivot_inverse):
@@ -116,13 +180,26 @@
     inverse_pivot = pivot_inverse[0]
     scaled = jnp.dot(panel[0], inverse_pivot, preferred_element_type=jnp.float32)
     scaled = jnp.where(alive_rows[:, None], scaled, jnp.zeros_like(scaled)).astype(jnp.bfloat16)
-    full = lax.all_gather(scaled, "pan", axis=0, tiled=True)
-    product = lax.dot_general(
+    gathered = P_SIZE - SPREAD_COLS
+    full = lax.all_gather(scaled[:, :gathered], "pan", axis=0, tiled=True)
+    near = lax.dot_general(
         sigma,
-        full.reshape(front_len, BLK, P_SIZE),
+        full.reshape(front_len, BLK, gathered),
         (((0, 2), (0, 1)), ((), ())),
         preferred_element_type=jnp.float32,
-    ).reshape(rb_local * BLK, P_SIZE)
+    ).reshape(rb_local * BLK, gathered)
+    slots = spread(scaled[:, gathered:], pan_count)
+    source = lax.rem(pan_idx - jnp.arange(pan_count, dtype=jnp.int32) + pan_count, pan_count)
+    sigma_by_slot = jnp.take(
+        sigma.reshape(pan_count, rb_local, rb_local, BLK, BLK), source, axis=0
+    )
+    far = lax.dot_general(
+        sigma_by_slot,
+        slots.reshape(pan_count, rb_local, BLK, SPREAD_COLS),
+        (((0, 1, 3), (0, 1, 2)), ((), ())),
+        preferred_element_type=jnp.float32,
+    ).reshape(rb_local * BLK, SPREAD_COLS)
+    product = jnp.concatenate([near, far], axis=1)
     cross = jnp.where(alive_rows[:, None], -product, jnp.zeros_like(product)).astype(jnp.bfloat16)
     pivot_rows = P_SIZE // pan_count
     part = (-lax.dot_general(scaled, cross, contract, preferred_element_type=jnp.float32)).astype(

time: 188 us -> 261 us (1.39)
  Pallas kernels: 37.5 us -> 164 us
  waiting for transfers between devices: 81.3 us -> 0.04 us
  local copies, waits for them, and re-layouts: 25.1 us -> 40.9 us
  other arithmetic: 9.59 us -> 19.4 us
    pallas_call x0 -> x1, Pallas kernels: none -> 126 us  [spread(): pl.pallas_call(functools.partial(_spread_kernel, n), out_shape=jax.ShapeD...]
    all_to_all x1, waiting for transfers between devices: 47.4 us -> 0.01 us  [per_device(): lax.all_to_all(outgoing, 'grp', split_axis=0, concat_axis=0, tiled=True)]
    all_gather x1, waiting for transfers between devices: 33.9 us -> 0.02 us  [per_device(): full = lax.all_gather(scaled[:, :gathered], 'pan', axis=0, tiled=True)]
    select_n x0 -> x1, local copies, waits for them, and re-layouts: none -> 6.42 us  [per_device(): jnp.take(sigma.reshape(pan_count, rb_local, rb_local, BLK, BLK), source,...]
    gather x0 -> x1, local copies, waits for them, and re-layouts: none -> 5.28 us  [per_device(): jnp.take(sigma.reshape(pan_count, rb_local, rb_local, BLK, BLK), source,...]
    select_n x0 -> x1, other arithmetic: none -> 4.64 us  [per_device(): jnp.take(sigma.reshape(pan_count, rb_local, rb_local, BLK, BLK), source,...]
    select_n x2 -> x3, other arithmetic: 4.9 us -> 9.18 us  [per_device(): jnp.take(received.reshape(groups * per_src, rb_local, BLK, BLK), order, a...]
    dot_general x1 -> x2, matrix products: 8.79 us -> 10.7 us  [the longest x1 6.04 us: per_device(): lax.dot_general(sigma, full.reshape(front_len, BLK, gathered), (((0, 2),...]
  transfers between devices with their start and end apart: 2 -> 2, of which waited for: 2 -> 0; matrix products, arithmetic and copies ran while one was open for 17% -> 23% of each run, Pallas kernels for 0% -> 49%
where the time goes in v9:
time: 261 us; the launch traced here: 259 us
  Pallas kernels  164 us (63%)
  local copies, waits for them, and re-layouts  40.9 us (16%)
  other arithmetic  19.4 us (7%)
  matrix products  15.7 us (6%)
  between operations  14.2 us (5%)
  starting transfers between devices  4.72 us (2%)
    pallas_call x1, Pallas kernels, spread(): pl.pallas_call(functools.partial(_spread_kernel, n), out_shape=jax.ShapeD...  126 us
    pallas_call x1, Pallas kernels, scatter_sum(): pl.pallas_call(lambda *refs: _scatter_sum_kernel(n, *refs), out_shape=jax...  38.1 us
    select_n x3, other arithmetic, per_device(): jnp.take(received.reshape(groups * per_src, rb_local, BLK, BLK), order, a...  9.18 us
    select_n x1, local copies, waits for them, and re-layouts, per_device(): jnp.take(sigma.reshape(pan_count, rb_local, rb_local, BLK, BLK), source,...  6.42 us
    dot_general x1, local copies, waits for them, and re-layouts, per_device(): lax.dot_general(sigma, full.reshape(front_len, BLK, gathered), (((0, 2),...  6.37 us
    reshape x2, local copies, waits for them, and re-layouts, per_device(): local = anc_rows.reshape(stored_blocks, BLK, cb_local, BLK)  6.15 us
    dot_general x1, matrix products, per_device(): lax.dot_general(sigma, full.reshape(front_len, BLK, gathered), (((0, 2),...  6.04 us
    gather x1, local copies, waits for them, and re-layouts, per_device(): jnp.take(sigma.reshape(pan_count, rb_local, rb_local, BLK, BLK), source,...  5.28 us
  transfers between devices with their start and end apart: 2, of which 0 were waited for; matrix products, arithmetic and copies ran while one was open for 23% of the time, Pallas kernels for 49%

profile of v9, /device:TPU:70, one launch (start us, length us, event | category | flops | bytes accessed | tf_op | source)
XLA Modules:
  0.0 259.2 jit_solution(1663867133261771626)
XLA Ops:
  7.3 1.3 dynamic_slice.16
  8.6 0.7 add_compare_fusion
  9.3 1.5 fusion
  10.8 0.7 copy-done.2
  11.5 0.7 slice.20
  12.3 1.4 gather_fusion
  13.7 1.6 sort.34
  15.6 0.2 dynamic-slice_reduce_fusion
  15.8 0.8 copy.30
  16.6 0.6 gather_fusion.1
  17.4 0.8 gather_fusion.2
  18.6 0.1 reshape.306
  18.8 4.0 %reshape.332 = bf16[16,128,4,128]{3,2,1,0:T(4,128)(2,1)} reshape(bf16[2048,512]{1,0:T(8,128)(2,1)} %param.6) | data formatting | bytes 4194304 | tf_op jit(solution)/shard_map/reshape | solution.py:171
  22.8 2.1 copy.34
  24.9 3.1 %gather_fusion.3 = bf16[128,128,128]{2,1,0:T(8,128)(2,1)} fusion(bf16[16,128,4,128]{3,1,2,0:T(8,128)(2,1)S(1)} %copy.34, s32[128]{0:T(128)S(1)} %reshape.306), kind=kCustom, calls=%fused_computation.3 | custom fusion | bytes 8389632 | tf_op jit(solution)/shard_map/gather | solution.py:172
  28.0 4.7 %all-to-all-start = ((bf16[8,8,2,128,128]{4,3,2,1,0:T(8,128)(2,1)}), bf16[8,8,2,128,128]{4,3,2,1,0:T(8,128)(2,1)}, u32[]{:S(2)}, u32[]{:S(2)}) async-start(bf16[8,8,2,128,128]{4,3,2,1,0:T(8,128)(2,1)} %bitcast.67), calls=%async_computation | async-start | bytes 8388608 | tf_op jit(solution)/shard_map/all_to_all | solution.py:173
  32.7 0.7 slice.21.block_ref
  33.6 2.0 sort.35
  35.8 126.1 %shard_map.77 = bf16[32,256,256]{2,1,0:T(8,128)(2,1)} custom-call(bf16[256,256]{1,0:T(8,128)(2,1)} %slice.21.block_ref), custom_call_target="tpu_custom_call" | custom-call | bytes 8388608 | tf_op jit(solution)/shard_map/pallas_call | solution.py:126
  162.0 5.2 %gather_fusion.4 = bf16[64,2,128,128]{3,2,1,0:T(8,128)(2,1)} fusion(bf16[64,2,128,128]{3,2,1,0:T(8,128)(2,1)} %bitcast.8, s32[1024]{0:T(1024)S(1)} %pad_clamp_fusion.1), kind=kCustom, calls=%fused_computation.4 | custom fusion | bytes 8388864 | tf_op jit(solution)/shard_map/jit(_take)/gather | solution.py:175
  167.2 4.6 %broadcast_select_fusion = bf16[32,2,2,128,128]{4,3,2,1,0:T(8,128)(2,1)} fusion(bf16[32,2,2,128,128]{4,3,2,1,0:T(8,128)(2,1)} %bitcast.66, pred[32,2]{1,0:T(8,128)(4,1)S(1)} %broadcast_in_dim.94), kind=kLoop, calls=%fused_computation.8 | loop fusion | flops 2097152 | bytes 8388672 | tf_op jit(solution)/shard_map/jit(_take)/select_n | solution.py:175
  171.8 5.3 %gather_fusion.5 = bf16[32,2,2,128,128]{4,3,2,1,0:T(8,128)(2,1)} fusion(bf16[32,2,2,128,128]{4,3,2,1,0:T(8,128)(2,1)} %broadcast_select_fusion, s32[1024]{0:T(1024)S(1)} %pad_clamp_fusion), kind=kCustom, calls=%fused_computation.5 | custom fusion | bytes 8388736 | tf_op jit(solution)/shard_map/jit(_take)/gather | solution.py:193
  177.1 4.6 %select_bitcast_fusion = bf16[2,128,32,2,128]{1,4,0,3,2:T(8,128)(2,1)} fusion(bf16[32,2,2,128,128]{4,3,2,1,0:T(8,128)(2,1)} %gather_fusion.5, pred[32]{0:T(512)(128)(4,1)S(1)} %compare_and_fusion), kind=kLoop, calls=%fused_computation.6 | loop fusion | flops 2097152 | bytes 8388640 | tf_op jit(solution)/shard_map/jit(_take)/select_n | solution.py:193
  181.7 6.4 %copy.37 = bf16[2,128,32,2,128]{4,1,0,3,2:T(8,128)(2,1)} copy(bf16[2,128,32,2,128]{1,4,0,3,2:T(8,128)(2,1)} %select_bitcast_fusion) | data formatting | bytes 8388608 | tf_op jit(solution)/shard_map/jit(_take)/select_n | solution.py:193
  188.2 4.6 %select_bitcast_fusion.1 = bf16[2,128,64,128]{1,3,0,2:T(8,128)(2,1)} fusion(bf16[64,2,128,128]{3,2,1,0:T(8,128)(2,1)} %gather_fusion.4, pred[64]{0:T(512)(128)(4,1)S(1)} %compare_and_fusion.2), kind=kLoop, calls=%fused_computation.7 | loop fusion | flops 2097152 | bytes 8388672 | tf_op jit(solution)/shard_map/jit(_take)/select_n | solution.py:175
  192.7 6.4 %copy.45 = bf16[2,128,64,128]{3,1,0,2:T(8,128)(2,1)} copy(bf16[2,128,64,128]{1,3,0,2:T(8,128)(2,1)} %select_bitcast_fusion.1) | data formatting | bytes 8388608 | tf_op jit(solution)/shard_map/dot_general | solution.py:185
  199.1 4.7 %fusion.33 = f32[256,256,1,1]{1,0,3,2:T(8,128)S(1)} fusion(bf16[256,32,2,128]{3,0,2,1:T(8,128)(2,1)} %bitcast.70, bf16[32,2,128,256]{3,2,1,0:T(8,128)(2,1)} %bitcast.68), kind=kOutput, calls=%fused_computation.76 | convolution fusion | flops 1073741824 | bytes 8650752 | tf_op jit(solution)/shard_map/dot_general | solution.py:196
  203.9 6.0 %fusion.32 = f32[256,512,1]{1,0,2:T(8,128)S(1)} fusion(bf16[256,64,128]{2,0,1:T(8,128)(2,1)} %bitcast.69, bf16[64,128,512]{2,1,0:T(8,128)(2,1)} %bitcast.78), kind=kOutput, calls=%fused_computation.75 | convolution fusion | flops 2147483648 | bytes 13107200 | tf_op jit(solution)/shard_map/dot_general | solution.py:185
  209.9 1.6 negate_convert_fusion
  211.5 38.1 %shard_map.78 = f32[24,768]{1,0:T(8,128)} custom-call(bf16[32,24,768]{2,1,0:T(8,128)(2,1)} %bitcast.71), custom_call_target="tpu_custom_call" | custom-call | tf_op jit(solution)/shard_map/pallas_call | solution.py:67
  249.6 1.9 fusion.7
  251.5 0.9 fusion.11
  (48 shorter events, 1.6 us)
Async XLA Ops:
  7.2 2.1 copy-start
  7.2 10.2 %copy-start.1 = (s32[128]{0:T(128)S(1)}, s32[128]{0:T(128)}, u32[]{:S(2)}) copy-start(s32[128]{0:T(128)} %param.7) | copy-start | bytes 1540
  7.2 11.3 %copy-start.4 = (s32[8,64]{1,0:T(8,128)S(1)}, s32[8,64]{1,0:T(8,128)}, u32[]{:S(2)}) copy-start(s32[8,64]{1,0:T(8,128)} %param.8) | copy-start | bytes 6148
  7.2 196.7 %all-gather.2.cloned.1.call-start = ((), (), s32[]{:S(2)}) async-start(), calls=%async_computation.1 | async-start | bytes 8650752 | tf_op jit(solution)/shard_map/all_gather | solution.py:184
  10.8 0.7 copy-start.2
  28.0 4.7 %copy-start.3 = (bf16[256,768]{1,0:T(8,128)(2,1)S(1)}, bf16[256,768]{1,0:T(8,128)(2,1)}, u32[]{:S(2)}) copy-start(bf16[256,768]{1,0:T(8,128)(2,1)} %copy-done.2) | copy-start | bytes 1179652
  28.0 134.0 %all-to-all-start = ((bf16[8,8,2,128,128]{4,3,2,1,0:T(8,128)(2,1)}), bf16[8,8,2,128,128]{4,3,2,1,0:T(8,128)(2,1)}, u32[]{:S(2)}, u32[]{:S(2)}) async-start(bf16[8,8,2,128,128]{4,3,2,1,0:T(8,128)(2,1)} %bitcast.67), calls=%async_computation | async-start | bytes 8388608 | tf_op jit(solution)/shard_map/all_to_all | solution.py:173
Sparse Core Ops, SparseCore 0:
  12.4 171.1 all-gather.1

commit v10 on v2

--- a/solution.py
+++ b/solution.py
@@ -64,7 +64,7 @@
     return pl.pallas_call(
         lambda *refs: _scatter_sum_kernel(n, *refs),
         out_shape=jax.ShapeDtypeStruct((rows, cols), jnp.float32),
-        in_specs=[pl.BlockSpec(memory_space=pl.ANY)],
+        in_specs=[pl.BlockSpec(memory_space=pltpu.VMEM)],
         out_specs=pl.BlockSpec(memory_space=pltpu.VMEM),
         scratch_shapes=[
             pltpu.VMEM((n, rows, cols), part.dtype),

time: 188 us -> 189 us (level)
  no operation moved by 1% of the time
where the time goes in v10:
time: 189 us; the launch traced here: 188 us
  waiting for transfers between devices  81.3 us (43%)
  Pallas kernels  38.6 us (20%)
  local copies, waits for them, and re-layouts  25.1 us (13%)
  matrix products  14.5 us (8%)
  between operations  14.2 us (8%)
  other arithmetic  9.59 us (5%)
  starting transfers between devices  4.64 us (2%)
    all_to_all x1, waiting for transfers between devices, per_device(): lax.all_to_all(outgoing, 'grp', split_axis=0, concat_axis=0, tiled=True)  47.4 us
    pallas_call x1, Pallas kernels, scatter_sum(): pl.pallas_call(lambda *refs: _scatter_sum_kernel(n, *refs), out_shape=jax...  38.6 us
    all_gather x1, waiting for transfers between devices, per_device(): full = lax.all_gather(scaled, 'pan', axis=0, tiled=True)  33.9 us
    dot_general x1, matrix products, per_device(): lax.dot_general(sigma, full.reshape(front_len, BLK, P_SIZE), (((0, 2), (0...  8.79 us
    dot_general x1, local copies, waits for them, and re-layouts, per_device(): lax.dot_general(sigma, full.reshape(front_len, BLK, P_SIZE), (((0, 2), (0...  6.42 us
    gather x1, local copies, waits for them, and re-layouts, per_device(): jnp.take(received.reshape(groups * per_src, rb_local, BLK, BLK), order, a...  5.2 us
    select_n x2, other arithmetic, per_device(): jnp.take(received.reshape(groups * per_src, rb_local, BLK, BLK), order, a...  4.9 us
    all_to_all x1, starting transfers between devices, per_device(): lax.all_to_all(outgoing, 'grp', split_axis=0, concat_axis=0, tiled=True)  4.61 us
  transfers between devices with their start and end apart: 2, of which 2 were waited for; matrix products, arithmetic and copies ran while one was open for 17% of the time, Pallas kernels for 0%

profile of v10, /device:TPU:70, one launch (start us, length us, event | category | flops | bytes accessed | tf_op | source)
XLA Modules:
  0.0 187.8 jit_solution(4918155269866233999)
XLA Ops:
  7.3 1.4 dynamic_slice.16
  8.7 0.7 add_compare_fusion
  9.4 2.2 %fusion.3 = bf16[256,768]{1,0:T(8,128)(2,1)} fusion(bf16[1,768,768]{2,1,0:T(8,128)(2,1)S(1)} %copy-done, bf16[1,256,768]{2,1,0:T(8,128)(2,1)} %param.10, pred[256]{0:T(512)(128)(4,1)S(1)} %broadcast_bitcast_fusion), kind=kOutput, calls=%fused_computation.12 | convolution fusion | flops 302383104 | bytes 1966336 | tf_op jit(solution)/shard_map/dot_general | solution.py:117
  11.7 1.4 gather_fusion
  13.0 1.6 sort.34
  14.7 0.1 mul.53
  14.7 0.1 copy.20
  14.8 0.1 add.142
  15.0 0.2 dynamic-slice_reduce_fusion
  15.2 0.8 copy.23
  16.0 0.6 gather_fusion.1
  16.6 0.1 reshape.186
  16.7 0.8 gather_fusion.2
  17.5 0.1 reshape.185
  17.6 0.1 fusion.17
  18.0 0.1 reshape.192
  18.1 2.1 %reshape.209 = bf16[16,128,4,128]{3,2,1,0:T(4,128)(2,1)} reshape(bf16[2048,512]{1,0:T(8,128)(2,1)S(1)} %copy-done.2) | data formatting | bytes 4194304 | tf_op jit(solution)/shard_map/reshape | solution.py:107
  20.2 2.1 %copy.27 = bf16[16,128,4,128]{3,1,2,0:T(8,128)(2,1)S(1)} copy(bf16[16,128,4,128]{3,2,1,0:T(4,128)(2,1)} %reshape.209) | data formatting | bytes 4194304 | tf_op jit(solution)/shard_map/reshape | solution.py:107
  22.4 3.1 %gather_fusion.3 = bf16[128,128,128]{2,1,0:T(8,128)(2,1)} fusion(bf16[16,128,4,128]{3,1,2,0:T(8,128)(2,1)S(1)} %copy.27, s32[128]{0:T(128)S(1)} %reshape.192), kind=kCustom, calls=%fused_computation.3 | custom fusion | bytes 8389632 | tf_op jit(solution)/shard_map/gather | solution.py:108
  25.4 4.6 %all-to-all-start = ((bf16[8,8,2,128,128]{4,3,2,1,0:T(8,128)(2,1)}), bf16[8,8,2,128,128]{4,3,2,1,0:T(8,128)(2,1)}, u32[]{:S(2)}, u32[]{:S(2)}) async-start(bf16[8,8,2,128,128]{4,3,2,1,0:T(8,128)(2,1)} %bitcast.60), calls=%async_computation | async-start | bytes 8388608 | tf_op jit(solution)/shard_map/all_to_all | solution.py:109
  30.1 0.1 copy.21
  30.2 0.1 add.137
  30.3 2.0 %sort.35 = (s32[64]{0:T(128)}, s32[64]{0:T(128)S(1)}) sort(s32[64]{0:T(128)S(1)} %add.137, s32[64]{0:T(128)S(1)} %iota.27), dimensions={0}, to_apply=%region_1.2 | sort | flops 384 | bytes 1024 | tf_op jit(solution)/shard_map/jit(argsort)/sort | solution.py:110
  32.4 47.4 %all-to-all-done = bf16[8,8,2,128,128]{4,3,2,1,0:T(8,128)(2,1)} async-done(((bf16[8,8,2,128,128]{4,3,2,1,0:T(8,128)(2,1)}), bf16[8,8,2,128,128]{4,3,2,1,0:T(8,128)(2,1)}, u32[]{:S(2)}, u32[]{:S(2)}) %all-to-all-start) | async-done | bytes 4194336 | tf_op jit(solution)/shard_map/all_to_all | solution.py:109
  79.7 5.2 %gather_fusion.4 = bf16[64,2,128,128]{3,2,1,0:T(8,128)(2,1)} fusion(bf16[64,2,128,128]{3,2,1,0:T(8,128)(2,1)} %bitcast.8, s32[1024]{0:T(1024)S(1)} %pad_clamp_fusion), kind=kCustom, calls=%fused_computation.4 | custom fusion | bytes 8388864 | tf_op jit(solution)/shard_map/jit(_take)/gather | solution.py:111
  84.9 4.9 %select_bitcast_fusion = bf16[2,128,64,128]{1,3,0,2:T(8,128)(2,1)} fusion(bf16[64,2,128,128]{3,2,1,0:T(8,128)(2,1)} %gather_fusion.4, pred[64]{0:T(512)(128)(4,1)S(1)} %compare_and_fusion.1), kind=kLoop, calls=%fused_computation.5 | loop fusion | flops 2097152 | bytes 8388672 | tf_op jit(solution)/shard_map/jit(_take)/select_n | solution.py:111
  89.8 6.4 %copy.32 = bf16[2,128,64,128]{3,1,0,2:T(8,128)(2,1)} copy(bf16[2,128,64,128]{1,3,0,2:T(8,128)(2,1)} %select_bitcast_fusion) | data formatting | bytes 8388608 | tf_op jit(solution)/shard_map/dot_general | solution.py:120
  96.2 33.9 %all-gather.2.cloned.1.call-done = bf16[8192,768]{1,0:T(8,128)(2,1)} async-done(((bf16[256,768]{1,0:T(8,128)(2,1)}), bf16[8192,768]{1,0:T(8,128)(2,1)}) %all-gather.2.cloned.1.call-update) | async-done | bytes 12582928 | tf_op jit(solution)/shard_map/all_gather | solution.py:119
  130.1 8.8 %fusion.2 = bf16[256,768]{1,0:T(8,128)(2,1)S(1)} fusion(bf16[256,64,128]{2,0,1:T(8,128)(2,1)} %bitcast.61, bf16[64,128,768]{2,1,0:T(8,128)(2,1)} %bitcast.65, pred[256]{0:T(512)(128)(4,1)S(1)} %broadcast_bitcast_fusion), kind=kOutput, calls=%fused_computation.11 | convolution fusion | flops 3221815296 | bytes 17170688 | tf_op jit(solution)/shard_map/dot_general | solution.py:120
  139.0 1.5 negate_convert_fusion
  140.5 38.6 %shard_map.77 = f32[24,768]{1,0:T(8,128)} custom-call(bf16[32,24,768]{2,1,0:T(8,128)(2,1)} %bitcast.62), custom_call_target="tpu_custom_call" | custom-call | tf_op jit(solution)/shard_map/pallas_call | solution.py:64
  179.1 1.9 %fusion.10 = f32[1,24,768]{2,1,0:T(8,128)} fusion(f32[24,768]{1,0:T(8,128)} %shard_map.77, bf16[1,768,768]{2,1,0:T(8,128)(2,1)S(1)} %copy-done, s32[]{:T(128)S(6)} %select_n.138), kind=kOutput, calls=%fused_computation.17 | convolution fusion | flops 28329984 | bytes 1523716 | tf_op jit(solution)/shard_map/dot_general | solution.py:133
  (38 shorter events, 0.7 us)
Async XLA Ops:
  7.2 2.2 %copy-start = (bf16[1,768,768]{2,1,0:T(8,128)(2,1)S(1)}, bf16[1,768,768]{2,1,0:T(8,128)(2,1)}, u32[]{:S(2)}) copy-start(bf16[1,768,768]{2,1,0:T(8,128)(2,1)} %param.11) | copy-start | bytes 3538948
  7.2 9.5 %copy-start.1 = (s32[128]{0:T(128)S(1)}, s32[128]{0:T(128)}, u32[]{:S(2)}) copy-start(s32[128]{0:T(128)} %param.7) | copy-start | bytes 1540
  7.2 10.6 %copy-start.4 = (s32[8,64]{1,0:T(8,128)S(1)}, s32[8,64]{1,0:T(8,128)}, u32[]{:S(2)}) copy-start(s32[8,64]{1,0:T(8,128)} %param.8) | copy-start | bytes 6148
  7.2 10.9 %copy-start.2 = (bf16[2048,512]{1,0:T(8,128)(2,1)S(1)}, bf16[2048,512]{1,0:T(8,128)(2,1)}, u32[]{:S(2)}) copy-start(bf16[2048,512]{1,0:T(8,128)(2,1)} %param.6) | copy-start | bytes 6291460
  7.2 122.9 %all-gather.2.cloned.1.call-start = ((), (), s32[]{:S(2)}) async-start(), calls=%async_computation.1 | async-start | bytes 12976128 | tf_op jit(solution)/shard_map/all_gather | solution.py:119
  25.4 54.3 %all-to-all-start = ((bf16[8,8,2,128,128]{4,3,2,1,0:T(8,128)(2,1)}), bf16[8,8,2,128,128]{4,3,2,1,0:T(8,128)(2,1)}, u32[]{:S(2)}, u32[]{:S(2)}) async-start(bf16[8,8,2,128,128]{4,3,2,1,0:T(8,128)(2,1)} %bitcast.60), calls=%async_computation | async-start | bytes 8388608 | tf_op jit(solution)/shard_map/all_to_all | solution.py:109
  130.1 8.8 %copy-start.3 = (bf16[256,768]{1,0:T(8,128)(2,1)S(1)}, bf16[256,768]{1,0:T(8,128)(2,1)}, u32[]{:S(2)}) copy-start(bf16[256,768]{1,0:T(8,128)(2,1)} %fusion.3) | copy-start | bytes 1179652
  138.9 42.1 %copy-start.5 = (bf16[256,768]{1,0:T(8,128)(2,1)}, bf16[256,768]{1,0:T(8,128)(2,1)S(1)}, u32[]{:S(2)}) copy-start(bf16[256,768]{1,0:T(8,128)(2,1)S(1)} %fusion.2) | copy-start | bytes 1179652
Sparse Core Ops, SparseCore 0:
  11.8 118.3 all-gather.1

commit v11 on v9

--- a/solution.py
+++ b/solution.py
@@ -9,7 +9,6 @@
 
 BLK = 128
 P_SIZE = 768
-SPREAD_COLS = 256
 
 
 def _scatter_sum_kernel(n, part_ref, out_ref, buf, send_sem, recv_sem, local_sem):
@@ -79,10 +78,19 @@
     )(part)
 
 
-def _spread_kernel(n, block_ref, out_ref, send_sem, recv_sem, local_sem):
+CHUNKS = 4
+
+
+def _tail_kernel(
+    n, sigma_ref, full_ref, scaled_ref, keep_ref, cross_ref, out_ref,
+    sig_v, full_v, acc, part_v, buf, load_sem, send_sem, recv_sem, local_sem,
+):
     me = lax.axis_index("pan")
     grp = lax.axis_index("grp")
     mesh_ids = pl.DeviceIdType.MESH
+    blocks = sig_v.shape[0]
+    per_chunk = blocks // CHUNKS
+    rows = part_v.shape[1]
 
     barrier = pltpu.get_barrier_semaphore()
 
@@ -92,16 +100,52 @@
         return carry
 
     lax.fori_loop(1, n, greet, 0)
+
+    def loads(c):
+        span = pl.ds(c * per_chunk, per_chunk)
+        return (
+            pltpu.make_async_copy(sigma_ref.at[span], sig_v.at[span], load_sem.at[0, c]),
+            pltpu.make_async_copy(full_ref.at[span], full_v.at[span], load_sem.at[1, c]),
+        )
+
+    for c in range(CHUNKS):
+        for copy in loads(c):
+            copy.start()
+
+    acc[...] = jnp.zeros_like(acc)
+    contract = (((0,), (0,)), ((), ()))
+    for c in range(CHUNKS):
+        for copy in loads(c):
+            copy.wait()
+
+        def step(j, carry):
+            block = full_v[j]
+            for u in range(acc.shape[0]):
+                acc[u] += lax.dot_general(
+                    sig_v[j, u], block, contract, preferred_element_type=jnp.float32
+                )
+            return carry
+
+        lax.fori_loop(c * per_chunk, (c + 1) * per_chunk, step, 0)
+
+    width = acc.shape[2]
+    total = acc[...].reshape(acc.shape[0] * acc.shape[1], width)
+    cross = jnp.where(keep_ref[...] > 0, -total, jnp.zeros_like(total)).astype(cross_ref.dtype)
+    cross_ref[...] = cross
+    part = -lax.dot_general(scaled_ref[...], cross, contract, preferred_element_type=jnp.float32)
+    for k in range(n):
+        part_v[k] = part[k * rows : (k + 1) * rows]
+
     pl.semaphore_wait(barrier, n - 1)
 
-    own = pltpu.make_async_copy(block_ref, out_ref.at[0], local_sem)
+    own = pltpu.make_async_copy(part_v.at[me], buf.at[0], local_sem)
     own.start()
 
     def send(k):
         peer = lax.rem(me + k, n)
         return pltpu.make_async_remote_copy(
-            src_ref=block_ref,
-            dst_ref=out_ref.at[k],
+            src_ref=part_v.at[peer],
+            dst_ref=buf.at[k],
             send_sem=send_sem.at[k],
             recv_sem=recv_sem.at[k],
             device_id=(grp, peer),
@@ -120,24 +164,57 @@
     own.wait()
     lax.fori_loop(1, n, finish, 0)
 
-
-def spread(block, n):
-    rows, cols = block.shape
+    out_ref[...] = buf[0]
+
+    def accumulate(k, carry):
+        out_ref[...] += buf[k]
+        return carry
+
+    lax.fori_loop(1, n, accumulate, 0)
+
+
+def cross_and_pivot_sum(sigma, full, scaled, keep, n):
+    blocks, halves, _, _ = sigma.shape
+    width = full.shape[1]
+    out_rows = halves * BLK
+    rows = width // n
+    full = full.reshape(blocks, BLK, width)
     return pl.pallas_call(
-        functools.partial(_spread_kernel, n),
-        out_shape=jax.ShapeDtypeStruct((n, rows, cols), block.dtype),
-        in_specs=[pl.BlockSpec(memory_space=pl.ANY)],
-        out_specs=pl.BlockSpec(memory_space=pl.ANY),
+        functools.partial(_tail_kernel, n),
+        out_shape=(
+            jax.ShapeDtypeStruct((out_rows, width), jnp.bfloat16),
+            jax.ShapeDtypeStruct((rows, width), jnp.float32),
+        ),
+        in_specs=[
+            pl.BlockSpec(memory_space=pl.ANY),
+            pl.BlockSpec(memory_space=pl.ANY),
+            pl.BlockSpec(memory_space=pltpu.VMEM),
+            pl.BlockSpec(memory_space=pltpu.VMEM),
+        ],
+        out_specs=(
+            pl.BlockSpec(memory_space=pltpu.VMEM),
+            pl.BlockSpec(memory_space=pltpu.VMEM),
+        ),
         scratch_shapes=[
+            pltpu.VMEM(sigma.shape, sigma.dtype),
+            pltpu.VMEM(full.shape, full.dtype),
+            pltpu.VMEM((halves, BLK, width), jnp.float32),
+            pltpu.VMEM((n, rows, width), jnp.float32),
+            pltpu.VMEM((n, rows, width), jnp.float32),
+            pltpu.SemaphoreType.DMA((2, CHUNKS)),
             pltpu.SemaphoreType.DMA((n,)),
             pltpu.SemaphoreType.DMA((n,)),
             pltpu.SemaphoreType.DMA,
         ],
-        compiler_params=pltpu.CompilerParams(collective_id=1, has_side_effects=True),
+        compiler_params=pltpu.CompilerParams(
+            collective_id=0, has_side_effects=True, vmem_limit_bytes=60 * 1024 * 1024
+        ),
         cost_estimate=pl.CostEstimate(
-            flops=0, bytes_accessed=2 * n * rows * cols * block.dtype.itemsize, transcendentals=0
-        ),
-    )(block)
+            flops=2 * out_rows * blocks * BLK * width + 2 * width * out_rows * width,
+            bytes_accessed=sigma.size * 2 + full.size * 2 + 2 * n * rows * width * 4,
+            transcendentals=0,
+        ),
+    )(sigma, full, scaled, keep)
 
 
 def per_device(anc_rows, row_home, block_lists, front_blocks, panel, pivot_inverse):
@@ -180,32 +257,10 @@
     inverse_pivot = pivot_inverse[0]
     scaled = jnp.dot(panel[0], inverse_pivot, preferred_element_type=jnp.float32)
     scaled = jnp.where(alive_rows[:, None], scaled, jnp.zeros_like(scaled)).astype(jnp.bfloat16)
-    gathered = P_SIZE - SPREAD_COLS
-    full = lax.all_gather(scaled[:, :gathered], "pan", axis=0, tiled=True)
-    near = lax.dot_general(
-        sigma,
-        full.reshape(front_len, BLK, gathered),
-        (((0, 2), (0, 1)), ((), ())),
-        preferred_element_type=jnp.float32,
-    ).reshape(rb_local * BLK, gathered)
-    slots = spread(scaled[:, gathered:], pan_count)
-    source = lax.rem(pan_idx - jnp.arange(pan_count, dtype=jnp.int32) + pan_count, pan_count)
-    sigma_by_slot = jnp.take(
-        sigma.reshape(pan_count, rb_local, rb_local, BLK, BLK), source, axis=0
-    )
-    far = lax.dot_general(
-        sigma_by_slot,
-        slots.reshape(pan_count, rb_local, BLK, SPREAD_COLS),
-        (((0, 1, 3), (0, 1, 2)), ((), ())),
-        preferred_element_type=jnp.float32,
-    ).reshape(rb_local * BLK, SPREAD_COLS)
-    product = jnp.concatenate([near, far], axis=1)
-    cross = jnp.where(alive_rows[:, None], -product, jnp.zeros_like(product)).astype(jnp.bfloat16)
+    full = lax.all_gather(scaled, "pan", axis=0, tiled=True)
     pivot_rows = P_SIZE // pan_count
-    part = (-lax.dot_general(scaled, cross, contract, preferred_element_type=jnp.float32)).astype(
-        jnp.bfloat16
-    )
-    shared = scatter_sum(part.reshape(pan_count, pivot_rows, P_SIZE), pan_count)
+    keep = alive_rows[:, None].astype(jnp.float32)
+    cross, shared = cross_and_pivot_sum(sigma, full, scaled, keep, pan_count)
     own_columns = lax.dynamic_slice_in_dim(inverse_pivot, pan_idx * pivot_rows, pivot_rows, 1)
     triangle = lax.dot_general(
         own_columns, inverse_pivot, contract, preferred_element_type=jnp.float32

time: 261 us -> 225 us (0.86)
  waiting for transfers between devices: 0.04 us -> 86.7 us
  Pallas kernels: 164 us -> 84.3 us
  local copies, waits for them, and re-layouts: 40.9 us -> 21.3 us
  matrix products: 15.7 us -> 4.14 us
  other arithmetic: 19.4 us -> 9.6 us
    pallas_call x2 -> x1, Pallas kernels: 164 us -> 84.3 us  [cross_and_pivot_sum(): pl.pallas_call(functools.partial(_tail_kernel, n), out_shape=(jax.ShapeDt...]
    all_to_all x1, waiting for transfers between devices: 0.01 us -> 46.5 us  [per_device(): lax.all_to_all(outgoing, 'grp', split_axis=0, concat_axis=0, tiled=True)]
    all_gather x1, waiting for transfers between devices: 0.02 us -> 40.1 us  [per_device(): full = lax.all_gather(scaled, 'pan', axis=0, tiled=True)]
    dot_general x3 -> x0, matrix products: 12.3 us -> none  [the longest x1 6.04 us: per_device(): lax.dot_general(sigma, full.reshape(front_len, BLK, gathered), (((0, 2),...]
    select_n x1 -> x0, local copies, waits for them, and re-layouts: 6.42 us -> none  [per_device(): jnp.take(sigma.reshape(pan_count, rb_local, rb_local, BLK, BLK), source,...]
    dot_general x1 -> x0, local copies, waits for them, and re-layouts: 6.37 us -> none  [per_device(): lax.dot_general(sigma, full.reshape(front_len, BLK, gathered), (((0, 2),...]
    gather x1 -> x0, local copies, waits for them, and re-layouts: 5.28 us -> none  [per_device(): jnp.take(sigma.reshape(pan_count, rb_local, rb_local, BLK, BLK), source,...]
    select_n x1 -> x0, other arithmetic: 4.64 us -> none  [per_device(): jnp.take(sigma.reshape(pan_count, rb_local, rb_local, BLK, BLK), source,...]
  transfers between devices with their start and end apart: 2 -> 2, of which waited for: 0 -> 2; matrix products, arithmetic and copies ran while one was open for 23% -> 12% of each run, Pallas kernels for 49% -> 0%
where the time goes in v11:
time: 225 us
  waiting for transfers between devices  86.7 us (39%)
  Pallas kernels  84.3 us (37%)
  local copies, waits for them, and re-layouts  21.3 us (9%)
  between operations  14.2 us (6%)
  other arithmetic  9.6 us (4%)
  starting transfers between devices  4.64 us (2%)
  matrix products  4.14 us (2%)
    pallas_call x1, Pallas kernels, cross_and_pivot_sum(): pl.pallas_call(functools.partial(_tail_kernel, n), out_shape=(jax.ShapeDt...  84.3 us
    all_to_all x1, waiting for transfers between devices, per_device(): lax.all_to_all(outgoing, 'grp', split_axis=0, concat_axis=0, tiled=True)  46.5 us
    all_gather x1, waiting for transfers between devices, per_device(): full = lax.all_gather(scaled, 'pan', axis=0, tiled=True)  40.1 us
    gather x1, local copies, waits for them, and re-layouts, per_device(): jnp.take(received.reshape(groups * per_src, rb_local, BLK, BLK), order, a...  5.22 us
    select_n x2, other arithmetic, per_device(): jnp.take(received.reshape(groups * per_src, rb_local, BLK, BLK), order, a...  4.92 us
    all_to_all x1, starting transfers between devices, per_device(): lax.all_to_all(outgoing, 'grp', split_axis=0, concat_axis=0, tiled=True)  4.61 us
  transfers between devices with their start and end apart: 2, of which 2 were waited for; matrix products, arithmetic and copies ran while one was open for 12% of the time, Pallas kernels for 0%

profile of v11, /device:TPU:70, one launch (start us, length us, event | category | flops | bytes accessed | tf_op | source)
XLA Modules:
  0.0 224.8 jit_solution(9564962550801104502)
XLA Ops:
  7.3 1.4 dynamic_slice.18
  8.7 0.7 fusion.20
  9.4 2.2 fusion.scaled_ref
  11.7 1.4 gather_fusion
  13.0 1.6 sort.34
  14.7 0.1 mul.52
  14.7 0.1 copy.21
  14.8 0.1 add.139
  15.0 0.2 dynamic-slice_reduce_fusion
  15.2 0.8 copy.24
  16.0 0.6 gather_fusion.1
  16.6 0.1 reshape.193
  16.7 0.8 gather_fusion.2
  17.5 0.1 reshape.192
  17.6 0.1 fusion.14
  17.8 0.1 fusion.16
  18.0 0.1 reshape.199
  18.1 2.1 reshape.215
  20.2 2.1 copy.28
  22.4 3.1 %gather_fusion.3 = bf16[128,128,128]{2,1,0:T(8,128)(2,1)} fusion(bf16[16,128,4,128]{3,1,2,0:T(8,128)(2,1)S(1)} %copy.28, s32[128]{0:T(128)S(1)} %reshape.199), kind=kCustom, calls=%fused_computation.3 | custom fusion | bytes 8389632 | tf_op jit(solution)/shard_map/gather | solution.py:249
  25.4 4.6 %all-to-all-start = ((bf16[8,8,2,128,128]{4,3,2,1,0:T(8,128)(2,1)}), bf16[8,8,2,128,128]{4,3,2,1,0:T(8,128)(2,1)}, u32[]{:S(2)}, u32[]{:S(2)}) async-start(bf16[8,8,2,128,128]{4,3,2,1,0:T(8,128)(2,1)} %bitcast.44), calls=%async_computation | async-start | bytes 8388608 | tf_op jit(solution)/shard_map/all_to_all | solution.py:250
  30.1 0.1 copy.22
  30.2 0.1 add.134
  30.4 0.8 copy.29.keep_ref
  31.1 2.0 sort.35
  33.2 46.5 %all-to-all-done = bf16[8,8,2,128,128]{4,3,2,1,0:T(8,128)(2,1)} async-done(((bf16[8,8,2,128,128]{4,3,2,1,0:T(8,128)(2,1)}), bf16[8,8,2,128,128]{4,3,2,1,0:T(8,128)(2,1)}, u32[]{:S(2)}, u32[]{:S(2)}) %all-to-all-start) | async-done | bytes 4194336 | tf_op jit(solution)/shard_map/all_to_all | solution.py:250
  79.7 5.2 %gather_fusion.4 = bf16[64,2,128,128]{3,2,1,0:T(8,128)(2,1)} fusion(bf16[64,2,128,128]{3,2,1,0:T(8,128)(2,1)} %bitcast.6, s32[1024]{0:T(1024)S(1)} %pad_clamp_fusion), kind=kCustom, calls=%fused_computation.4 | custom fusion | bytes 8388864 | tf_op jit(solution)/shard_map/jit(_take)/gather | solution.py:252
  84.9 4.9 %broadcast_select_fusion.sigma_ref = bf16[64,2,128,128]{3,2,1,0:T(8,128)(2,1)} fusion(bf16[64,2,128,128]{3,2,1,0:T(8,128)(2,1)} %gather_fusion.4, pred[64]{0:T(512)(128)(4,1)S(1)} %compare_and_fusion.1), kind=kLoop, calls=%fused_computation.5 | loop fusion | flops 2097152 | bytes 8388672 | tf_op jit(solution)/shard_map/jit(_take)/select_n | solution.py:252
  89.9 40.1 %all-gather.2.cloned.1.call-done = bf16[8192,768]{1,0:T(8,128)(2,1)} async-done(((bf16[256,768]{1,0:T(8,128)(2,1)}), bf16[8192,768]{1,0:T(8,128)(2,1)}) %all-gather.2.cloned.1.call-update) | async-done | bytes 12582928 | tf_op jit(solution)/shard_map/all_gather | solution.py:260
  130.0 84.3 %shard_map.77 = (bf16[256,768]{1,0:T(8,128)(2,1)}, f32[24,768]{1,0:T(8,128)}) custom-call(bf16[64,2,128,128]{3,2,1,0:T(8,128)(2,1)} %broadcast_select_fusion.sigma_ref, bf16[64,128,768]{2,1,0:T(8,128)(2,1)} %bitcast.45, bf16[256,768]{1,0:T(8,128)(2,1)} %fusion.scaled_ref, f32[256,1]{1,0:T(8,128)} %copy.29.keep_ref), custom_call_target="tpu_custom_call" | custom-call | flops 3523215360 | bytes 21495808 | tf_op jit(solution)/shard_map/pallas_call | solution.py:182
  214.3 1.9 fusion.7
  216.2 1.8 copy.33
  (34 shorter events, 0.7 us)
Async XLA Ops:
  7.2 2.2 copy-start
  7.2 9.5 %copy-start.1 = (s32[128]{0:T(128)S(1)}, s32[128]{0:T(128)}, u32[]{:S(2)}) copy-start(s32[128]{0:T(128)} %param.7) | copy-start | bytes 1540
  7.2 10.6 %copy-start.3 = (s32[8,64]{1,0:T(8,128)S(1)}, s32[8,64]{1,0:T(8,128)}, u32[]{:S(2)}) copy-start(s32[8,64]{1,0:T(8,128)} %param.8) | copy-start | bytes 6148
  7.2 10.9 %copy-start.2 = (bf16[2048,512]{1,0:T(8,128)(2,1)S(1)}, bf16[2048,512]{1,0:T(8,128)(2,1)}, u32[]{:S(2)}) copy-start(bf16[2048,512]{1,0:T(8,128)(2,1)} %param.6) | copy-start | bytes 6291460
  7.2 122.8 %all-gather.2.cloned.1.call-start = ((), (), s32[]{:S(2)}) async-start(), calls=%async_computation.1 | async-start | bytes 12976128 | tf_op jit(solution)/shard_map/all_gather | solution.py:260
  25.4 54.3 %all-to-all-start = ((bf16[8,8,2,128,128]{4,3,2,1,0:T(8,128)(2,1)}), bf16[8,8,2,128,128]{4,3,2,1,0:T(8,128)(2,1)}, u32[]{:S(2)}, u32[]{:S(2)}) async-start(bf16[8,8,2,128,128]{4,3,2,1,0:T(8,128)(2,1)} %bitcast.44), calls=%async_computation | async-start | bytes 8388608 | tf_op jit(solution)/shard_map/all_to_all | solution.py:250
Sparse Core Ops, SparseCore 0:
  11.8 118.2 all-gather.1

commit v12 on v11

--- a/solution.py
+++ b/solution.py
@@ -88,8 +88,7 @@
     me = lax.axis_index("pan")
     grp = lax.axis_index("grp")
     mesh_ids = pl.DeviceIdType.MESH
-    blocks = sig_v.shape[0]
-    per_chunk = blocks // CHUNKS
+    per_chunk = full_v.shape[0] // CHUNKS
     rows = part_v.shape[1]
 
     barrier = pltpu.get_barrier_semaphore()
@@ -104,7 +103,7 @@
     def loads(c):
         span = pl.ds(c * per_chunk, per_chunk)
         return (
-            pltpu.make_async_copy(sigma_ref.at[span], sig_v.at[span], load_sem.at[0, c]),
+            pltpu.make_async_copy(sigma_ref.at[c], sig_v.at[c], load_sem.at[0, c]),
             pltpu.make_async_copy(full_ref.at[span], full_v.at[span], load_sem.at[1, c]),
         )
 
@@ -117,19 +116,11 @@
     for c in range(CHUNKS):
         for copy in loads(c):
             copy.wait()
-
-        def step(j, carry):
-            block = full_v[j]
-            for u in range(acc.shape[0]):
-                acc[u] += lax.dot_general(
-                    sig_v[j, u], block, contract, preferred_element_type=jnp.float32
-                )
-            return carry
-
-        lax.fori_loop(c * per_chunk, (c + 1) * per_chunk, step, 0)
-
-    width = acc.shape[2]
-    total = acc[...].reshape(acc.shape[0] * acc.shape[1], width)
+        acc[...] += jnp.dot(
+            sig_v[c], full_v[pl.ds(c * per_chunk, per_chunk)], preferred_element_type=jnp.float32
+        )
+
+    total = acc[...]
     cross = jnp.where(keep_ref[...] > 0, -total, jnp.zeros_like(total)).astype(cross_ref.dtype)
     cross_ref[...] = cross
     part = -lax.dot_general(scaled_ref[...], cross, contract, preferred_element_type=jnp.float32)
@@ -178,7 +169,9 @@
     width = full.shape[1]
     out_rows = halves * BLK
     rows = width // n
-    full = full.reshape(blocks, BLK, width)
+    depth = blocks * BLK // CHUNKS
+    sigma = jnp.transpose(sigma, (1, 3, 0, 2)).reshape(out_rows, CHUNKS, depth)
+    sigma = jnp.transpose(sigma, (1, 0, 2))
     return pl.pallas_call(
         functools.partial(_tail_kernel, n),
         out_shape=(
@@ -198,7 +191,7 @@
         scratch_shapes=[
             pltpu.VMEM(sigma.shape, sigma.dtype),
             pltpu.VMEM(full.shape, full.dtype),
-            pltpu.VMEM((halves, BLK, width), jnp.float32),
+            pltpu.VMEM((out_rows, width), jnp.float32),
             pltpu.VMEM((n, rows, width), jnp.float32),
             pltpu.VMEM((n, rows, width), jnp.float32),
             pltpu.SemaphoreType.DMA((2, CHUNKS)),

time: 225 us -> 212 us (0.942)
  local copies, waits for them, and re-layouts: 21.3 us -> 43.2 us
  waiting for transfers between devices: 86.7 us -> 65 us
  Pallas kernels: 84.3 us -> 70.4 us
    all_gather x1, waiting for transfers between devices: 40.1 us -> 18.5 us  [per_device(): full = lax.all_gather(scaled, 'pan', axis=0, tiled=True)]
    pallas_call x1, Pallas kernels: 84.3 us -> 70.4 us  [cross_and_pivot_sum(): pl.pallas_call(functools.partial(_tail_kernel, n), out_shape=(jax.ShapeDt...]
    reshape x0 -> x2, local copies, waits for them, and re-layouts: none -> 13.5 us  [cross_and_pivot_sum(): sigma = jnp.transpose(sigma, (1, 3, 0, 2)).reshape(out_rows, CHUNKS, depth)]
    select_n x0 -> x1, local copies, waits for them, and re-layouts: none -> 6.58 us  [per_device(): jnp.take(received.reshape(groups * per_src, rb_local, BLK, BLK), order, a...]
  transfers between devices with their start and end apart: 2 -> 2, of which waited for: 2 -> 2; matrix products, arithmetic and copies ran while one was open for 12% -> 23% of each run, Pallas kernels for 0% -> 0%
where the time goes in v12:
time: 212 us; the launch traced here: 211 us
  Pallas kernels  70.4 us (33%)
  waiting for transfers between devices  65 us (31%)
  local copies, waits for them, and re-layouts  43.2 us (20%)
  between operations  14.2 us (7%)
  other arithmetic  9.26 us (4%)
  starting transfers between devices  4.62 us (2%)
  matrix products  4.14 us (2%)
    pallas_call x1, Pallas kernels, cross_and_pivot_sum(): pl.pallas_call(functools.partial(_tail_kernel, n), out_shape=(jax.ShapeDt...  70.4 us
    all_to_all x1, waiting for transfers between devices, per_device(): lax.all_to_all(outgoing, 'grp', split_axis=0, concat_axis=0, tiled=True)  46.5 us
    all_gather x1, waiting for transfers between devices, per_device(): full = lax.all_gather(scaled, 'pan', axis=0, tiled=True)  18.5 us
    reshape x2, local copies, waits for them, and re-layouts, cross_and_pivot_sum(): sigma = jnp.transpose(sigma, (1, 3, 0, 2)).reshape(out_rows, CHUNKS, depth)  13.5 us
    select_n x1, local copies, waits for them, and re-layouts, per_device(): jnp.take(received.reshape(groups * per_src, rb_local, BLK, BLK), order, a...  6.58 us
    reshape x2, local copies, waits for them, and re-layouts, per_device(): local = anc_rows.reshape(stored_blocks, BLK, cb_local, BLK)  6.14 us
    gather x1, local copies, waits for them, and re-layouts, per_device(): jnp.take(received.reshape(groups * per_src, rb_local, BLK, BLK), order, a...  5.3 us
    all_to_all x1, starting transfers between devices, per_device(): lax.all_to_all(outgoing, 'grp', split_axis=0, concat_axis=0, tiled=True)  4.58 us
  transfers between devices with their start and end apart: 2, of which 2 were waited for; matrix products, arithmetic and copies ran while one was open for 23% of the time, Pallas kernels for 0%

profile of v12, /device:TPU:70, one launch (start us, length us, event | category | flops | bytes accessed | tf_op | source)
XLA Modules:
  0.0 210.9 jit_solution(11897797994790333231)
XLA Ops:
  7.3 1.3 dynamic_slice.18
  8.6 0.7 fusion.20
  9.3 2.2 %fusion.scaled_ref = bf16[256,768]{1,0:T(8,128)(2,1)} fusion(bf16[1,768,768]{2,1,0:T(8,128)(2,1)S(1)} %copy-done, bf16[1,256,768]{2,1,0:T(8,128)(2,1)} %param.10, pred[256]{0:T(512)(128)(4,1)S(1)} %broadcast_bitcast_fusion), kind=kOutput, calls=%fused_computation.8 | convolution fusion | flops 302383104 | bytes 1966336 | tf_op jit(solution)/shard_map/dot_general | solution.py:251
  11.6 1.4 gather_fusion
  13.0 1.6 sort.34
  14.7 0.1 copy.22
  14.7 0.1 add.139
  14.9 0.2 dynamic-slice_reduce_fusion
  15.1 0.8 copy.25
  15.9 0.6 gather_fusion.1
  16.5 0.1 reshape.193
  16.6 0.8 gather_fusion.2
  17.6 0.1 fusion.14
  17.9 0.1 reshape.199
  18.0 4.0 %reshape.215 = bf16[16,128,4,128]{3,2,1,0:T(4,128)(2,1)} reshape(bf16[2048,512]{1,0:T(8,128)(2,1)} %param.6) | data formatting | bytes 4194304 | tf_op jit(solution)/shard_map/reshape | solution.py:241
  22.0 2.1 %copy.29 = bf16[16,128,4,128]{3,1,2,0:T(8,128)(2,1)S(1)} copy(bf16[16,128,4,128]{3,2,1,0:T(4,128)(2,1)} %reshape.215) | data formatting | bytes 4194304 | tf_op jit(solution)/shard_map/reshape | solution.py:241
  24.2 3.1 %gather_fusion.3 = bf16[128,128,128]{2,1,0:T(8,128)(2,1)} fusion(bf16[16,128,4,128]{3,1,2,0:T(8,128)(2,1)S(1)} %copy.29, s32[128]{0:T(128)S(1)} %reshape.199), kind=kCustom, calls=%fused_computation.3 | custom fusion | bytes 8389632 | tf_op jit(solution)/shard_map/gather | solution.py:242
  27.2 4.6 %all-to-all-start = ((bf16[8,8,2,128,128]{4,3,2,1,0:T(8,128)(2,1)}), bf16[8,8,2,128,128]{4,3,2,1,0:T(8,128)(2,1)}, u32[]{:S(2)}, u32[]{:S(2)}) async-start(bf16[8,8,2,128,128]{4,3,2,1,0:T(8,128)(2,1)} %bitcast.50), calls=%async_computation | async-start | bytes 8388608 | tf_op jit(solution)/shard_map/all_to_all | solution.py:243
  31.8 0.1 copy.23
  31.9 0.1 add.134
  32.1 0.8 copy.32.keep_ref
  32.9 2.0 sort.35
  35.0 46.5 %all-to-all-done = bf16[8,8,2,128,128]{4,3,2,1,0:T(8,128)(2,1)} async-done(((bf16[8,8,2,128,128]{4,3,2,1,0:T(8,128)(2,1)}), bf16[8,8,2,128,128]{4,3,2,1,0:T(8,128)(2,1)}, u32[]{:S(2)}, u32[]{:S(2)}) %all-to-all-start) | async-done | bytes 4194336 | tf_op jit(solution)/shard_map/all_to_all | solution.py:243
  81.5 5.3 %gather_fusion.4 = bf16[64,2,128,128]{3,2,1,0:T(8,128)(2,1)} fusion(bf16[64,2,128,128]{3,2,1,0:T(8,128)(2,1)} %bitcast.6, s32[1024]{0:T(1024)S(1)} %pad_clamp_fusion), kind=kCustom, calls=%fused_computation.4 | custom fusion | bytes 8388864 | tf_op jit(solution)/shard_map/jit(_take)/gather | solution.py:245
  86.8 4.6 %select_bitcast_fusion = bf16[2,128,64,128]{1,3,0,2:T(8,128)(2,1)} fusion(bf16[64,2,128,128]{3,2,1,0:T(8,128)(2,1)} %gather_fusion.4, pred[64]{0:T(512)(128)(4,1)S(1)} %compare_and_fusion.1), kind=kLoop, calls=%fused_computation.6 | loop fusion | flops 2097152 | bytes 8388672 | tf_op jit(solution)/shard_map/jit(_take)/select_n | solution.py:245
  91.3 6.6 %copy.30 = bf16[2,128,64,128]{3,2,1,0:T(8,128)(2,1)} copy(bf16[2,128,64,128]{1,3,0,2:T(8,128)(2,1)} %select_bitcast_fusion) | data formatting | bytes 8388608 | tf_op jit(solution)/shard_map/jit(_take)/select_n | solution.py:245
  97.9 7.0 %reshape.174 = bf16[256,4,2048]{2,1,0:T(4,128)(2,1)} reshape(bf16[2,128,64,128]{3,2,1,0:T(8,128)(2,1)} %copy.30) | data formatting | bytes 8388608 | tf_op jit(solution)/shard_map/reshape | solution.py:173
  105.0 6.5 %copy.36 = bf16[256,4,2048]{2,0,1:T(8,128)(2,1)} copy(bf16[256,4,2048]{2,1,0:T(4,128)(2,1)} %reshape.174) | data formatting | bytes 8388608 | tf_op jit(solution)/shard_map/reshape | solution.py:173
  111.4 18.5 %all-gather.2.cloned.1.call-done.full_ref = bf16[8192,768]{1,0:T(8,128)(2,1)} async-done(((bf16[256,768]{1,0:T(8,128)(2,1)}), bf16[8192,768]{1,0:T(8,128)(2,1)}) %all-gather.2.cloned.1.call-update) | async-done | bytes 12582928 | tf_op jit(solution)/shard_map/all_gather | solution.py:253
  129.9 70.4 %shard_map.77 = (bf16[256,768]{1,0:T(8,128)(2,1)}, f32[24,768]{1,0:T(8,128)}) custom-call(bf16[4,256,2048]{2,1,0:T(8,128)(2,1)} %bitcast.51, bf16[8192,768]{1,0:T(8,128)(2,1)} %all-gather.2.cloned.1.call-done.full_ref, bf16[256,768]{1,0:T(8,128)(2,1)} %fusion.scaled_ref, f32[256,1]{1,0:T(8,128)} %copy.32.keep_ref), custom_call_target="tpu_custom_call" | custom-call | flops 3523215360 | bytes 21495808 | tf_op jit(solution)/shard_map/pallas_call | solution.py:175
  200.3 1.9 fusion.7
  202.2 1.8 copy.38
  (35 shorter events, 0.9 us)
Async XLA Ops:
  7.2 2.1 %copy-start = (bf16[1,768,768]{2,1,0:T(8,128)(2,1)S(1)}, bf16[1,768,768]{2,1,0:T(8,128)(2,1)}, u32[]{:S(2)}) copy-start(bf16[1,768,768]{2,1,0:T(8,128)(2,1)} %param.11) | copy-start | bytes 3538948
  7.2 9.4 %copy-start.1 = (s32[128]{0:T(128)S(1)}, s32[128]{0:T(128)}, u32[]{:S(2)}) copy-start(s32[128]{0:T(128)} %param.7) | copy-start | bytes 1540
  7.2 10.5 %copy-start.2 = (s32[8,64]{1,0:T(8,128)S(1)}, s32[8,64]{1,0:T(8,128)}, u32[]{:S(2)}) copy-start(s32[8,64]{1,0:T(8,128)} %param.8) | copy-start | bytes 6148
  7.2 122.7 %all-gather.2.cloned.1.call-start = ((), (), s32[]{:S(2)}) async-start(), calls=%async_computation.1 | async-start | bytes 12976128 | tf_op jit(solution)/shard_map/all_gather | solution.py:253
  27.2 54.3 %all-to-all-start = ((bf16[8,8,2,128,128]{4,3,2,1,0:T(8,128)(2,1)}), bf16[8,8,2,128,128]{4,3,2,1,0:T(8,128)(2,1)}, u32[]{:S(2)}, u32[]{:S(2)}) async-start(bf16[8,8,2,128,128]{4,3,2,1,0:T(8,128)(2,1)} %bitcast.50), calls=%async_computation | async-start | bytes 8388608 | tf_op jit(solution)/shard_map/all_to_all | solution.py:243
Sparse Core Ops, SparseCore 0:
  11.7 118.2 all-gather.1

commit v13 on v7

--- a/solution.py
+++ b/solution.py
@@ -186,6 +186,7 @@
     triangle = lax.dot_general(
         own_columns, inverse_pivot, contract, preferred_element_type=jnp.float32
     )
+    triangle, shared = lax.optimization_barrier((triangle, shared))
     pivot = triangle + shared
     return (cross[None], pivot[None])
 

time: 187 us -> 186 us (level)
  transfers between devices with their start and end apart: 2 -> 2, of which waited for: 2 -> 2; matrix products, arithmetic and copies ran while one was open for 17% -> 18% of each run, Pallas kernels for 0% -> 0%
where the time goes in v13:
time: 186 us
  waiting for transfers between devices  80.9 us (43%)
  Pallas kernels  36.8 us (20%)
  local copies, waits for them, and re-layouts  25.1 us (13%)
  between operations  14.2 us (8%)
  matrix products  12.9 us (7%)
  other arithmetic  11.1 us (6%)
  starting transfers between devices  4.64 us (2%)
    all_to_all x1, waiting for transfers between devices, per_device(): lax.all_to_all(outgoing, 'grp', split_axis=0, concat_axis=0, tiled=True)  47 us
    pallas_call x1, Pallas kernels, scatter_sum(): pl.pallas_call(functools.partial(_scatter_sum_kernel, inner, outer), out_...  36.8 us
    all_gather x1, waiting for transfers between devices, per_device(): full = lax.all_gather(scaled, 'pan', axis=0, tiled=True)  33.9 us
    dot_general x1, matrix products, per_device(): lax.dot_general(sigma, full.reshape(front_len, BLK, P_SIZE), (((0, 2), (0...  8.79 us
    dot_general x1, local copies, waits for them, and re-layouts, per_device(): lax.dot_general(sigma, full.reshape(front_len, BLK, P_SIZE), (((0, 2), (0...  6.42 us
    gather x1, local copies, waits for them, and re-layouts, per_device(): jnp.take(received.reshape(groups * per_src, rb_local, BLK, BLK), order, a...  5.2 us
    select_n x2, other arithmetic, per_device(): jnp.take(received.reshape(groups * per_src, rb_local, BLK, BLK), order, a...  4.9 us
    all_to_all x1, starting transfers between devices, per_device(): lax.all_to_all(outgoing, 'grp', split_axis=0, concat_axis=0, tiled=True)  4.61 us
  transfers between devices with their start and end apart: 2, of which 2 were waited for; matrix products, arithmetic and copies ran while one was open for 18% of the time, Pallas kernels for 0%

profile of v13, /device:TPU:70, one launch (start us, length us, event | category | flops | bytes accessed | tf_op | source)
XLA Modules:
  0.0 185.7 jit_solution(15639546743249127371)
XLA Ops:
  7.3 1.4 dynamic_slice.16
  8.7 0.7 add_compare_fusion
  9.4 2.2 %fusion.3 = bf16[256,768]{1,0:T(8,128)(2,1)} fusion(bf16[1,768,768]{2,1,0:T(8,128)(2,1)S(1)} %copy-done, bf16[1,256,768]{2,1,0:T(8,128)(2,1)} %param.10, pred[256]{0:T(512)(128)(4,1)S(1)} %broadcast_bitcast_fusion), kind=kOutput, calls=%fused_computation.12 | convolution fusion | flops 302383104 | bytes 1966336 | tf_op jit(solution)/shard_map/dot_general | solution.py:170
  11.7 1.4 gather_fusion
  13.0 1.6 sort.34
  14.7 0.1 mul.53
  14.7 0.1 copy.20
  14.8 0.1 add.142
  15.0 0.2 dynamic-slice_reduce_fusion
  15.2 0.8 copy.23
  16.0 0.6 gather_fusion.1
  16.6 0.1 reshape.182
  16.7 0.8 gather_fusion.2
  17.6 0.1 fusion.11
  18.0 0.1 reshape.188
  18.1 2.1 %reshape.205 = bf16[16,128,4,128]{3,2,1,0:T(4,128)(2,1)} reshape(bf16[2048,512]{1,0:T(8,128)(2,1)S(1)} %copy-done.2) | data formatting | bytes 4194304 | tf_op jit(solution)/shard_map/reshape | solution.py:160
  20.2 2.1 %copy.27 = bf16[16,128,4,128]{3,1,2,0:T(8,128)(2,1)S(1)} copy(bf16[16,128,4,128]{3,2,1,0:T(4,128)(2,1)} %reshape.205) | data formatting | bytes 4194304 | tf_op jit(solution)/shard_map/reshape | solution.py:160
  22.4 3.1 %gather_fusion.3 = bf16[128,128,128]{2,1,0:T(8,128)(2,1)} fusion(bf16[16,128,4,128]{3,1,2,0:T(8,128)(2,1)S(1)} %copy.27, s32[128]{0:T(128)S(1)} %reshape.188), kind=kCustom, calls=%fused_computation.3 | custom fusion | bytes 8389632 | tf_op jit(solution)/shard_map/gather | solution.py:161
  25.4 4.6 %all-to-all-start = ((bf16[8,8,2,128,128]{4,3,2,1,0:T(8,128)(2,1)}), bf16[8,8,2,128,128]{4,3,2,1,0:T(8,128)(2,1)}, u32[]{:S(2)}, u32[]{:S(2)}) async-start(bf16[8,8,2,128,128]{4,3,2,1,0:T(8,128)(2,1)} %bitcast.56), calls=%async_computation | async-start | bytes 8388608 | tf_op jit(solution)/shard_map/all_to_all | solution.py:162
  30.1 0.1 copy.21
  30.2 0.1 add.137
  30.3 2.0 %sort.35 = (s32[64]{0:T(128)}, s32[64]{0:T(128)S(1)}) sort(s32[64]{0:T(128)S(1)} %add.137, s32[64]{0:T(128)S(1)} %iota.27), dimensions={0}, to_apply=%region_1.2 | sort | flops 384 | bytes 1024 | tf_op jit(solution)/shard_map/jit(argsort)/sort | solution.py:163
  32.4 0.3 fusion.4
  32.7 47.0 %all-to-all-done = bf16[8,8,2,128,128]{4,3,2,1,0:T(8,128)(2,1)} async-done(((bf16[8,8,2,128,128]{4,3,2,1,0:T(8,128)(2,1)}), bf16[8,8,2,128,128]{4,3,2,1,0:T(8,128)(2,1)}, u32[]{:S(2)}, u32[]{:S(2)}) %all-to-all-start) | async-done | bytes 4194336 | tf_op jit(solution)/shard_map/all_to_all | solution.py:162
  79.7 5.2 %gather_fusion.4 = bf16[64,2,128,128]{3,2,1,0:T(8,128)(2,1)} fusion(bf16[64,2,128,128]{3,2,1,0:T(8,128)(2,1)} %bitcast.8, s32[1024]{0:T(1024)S(1)} %pad_clamp_fusion), kind=kCustom, calls=%fused_computation.4 | custom fusion | bytes 8388864 | tf_op jit(solution)/shard_map/jit(_take)/gather | solution.py:164
  84.9 4.9 %select_bitcast_fusion = bf16[2,128,64,128]{1,3,0,2:T(8,128)(2,1)} fusion(bf16[64,2,128,128]{3,2,1,0:T(8,128)(2,1)} %gather_fusion.4, pred[64]{0:T(512)(128)(4,1)S(1)} %compare_and_fusion.1), kind=kLoop, calls=%fused_computation.5 | loop fusion | flops 2097152 | bytes 8388672 | tf_op jit(solution)/shard_map/jit(_take)/select_n | solution.py:164
  89.8 6.4 %copy.32 = bf16[2,128,64,128]{3,1,0,2:T(8,128)(2,1)} copy(bf16[2,128,64,128]{1,3,0,2:T(8,128)(2,1)} %select_bitcast_fusion) | data formatting | bytes 8388608 | tf_op jit(solution)/shard_map/dot_general | solution.py:173
  96.2 33.9 %all-gather.2.cloned.1.call-done = bf16[8192,768]{1,0:T(8,128)(2,1)} async-done(((bf16[256,768]{1,0:T(8,128)(2,1)}), bf16[8192,768]{1,0:T(8,128)(2,1)}) %all-gather.2.cloned.1.call-update) | async-done | bytes 12582928 | tf_op jit(solution)/shard_map/all_gather | solution.py:172
  130.1 8.8 %fusion.2 = bf16[256,768]{1,0:T(8,128)(2,1)S(1)} fusion(bf16[256,64,128]{2,0,1:T(8,128)(2,1)} %bitcast.57, bf16[64,128,768]{2,1,0:T(8,128)(2,1)} %bitcast.61, pred[256]{0:T(512)(128)(4,1)S(1)} %broadcast_bitcast_fusion), kind=kOutput, calls=%fused_computation.11 | convolution fusion | flops 3221815296 | bytes 17170688 | tf_op jit(solution)/shard_map/dot_general | solution.py:173
  139.0 1.5 negate_convert_fusion
  140.5 36.8 %shard_map.77 = f32[24,768]{1,0:T(8,128)} custom-call(bf16[8,4,24,768]{3,2,1,0:T(8,128)(2,1)} %bitcast.58), custom_call_target="tpu_custom_call" | custom-call | tf_op jit(solution)/shard_map/pallas_call | solution.py:111
  177.3 1.5 add_bitcast_fusion
  (39 shorter events, 0.8 us)
Async XLA Ops:
  7.2 2.2 %copy-start = (bf16[1,768,768]{2,1,0:T(8,128)(2,1)S(1)}, bf16[1,768,768]{2,1,0:T(8,128)(2,1)}, u32[]{:S(2)}) copy-start(bf16[1,768,768]{2,1,0:T(8,128)(2,1)} %param.11) | copy-start | bytes 3538948
  7.2 9.5 %copy-start.1 = (s32[128]{0:T(128)S(1)}, s32[128]{0:T(128)}, u32[]{:S(2)}) copy-start(s32[128]{0:T(128)} %param.7) | copy-start | bytes 1540
  7.2 10.6 %copy-start.4 = (s32[8,64]{1,0:T(8,128)S(1)}, s32[8,64]{1,0:T(8,128)}, u32[]{:S(2)}) copy-start(s32[8,64]{1,0:T(8,128)} %param.8) | copy-start | bytes 6148
  7.2 10.9 %copy-start.2 = (bf16[2048,512]{1,0:T(8,128)(2,1)S(1)}, bf16[2048,512]{1,0:T(8,128)(2,1)}, u32[]{:S(2)}) copy-start(bf16[2048,512]{1,0:T(8,128)(2,1)} %param.6) | copy-start | bytes 6291460
  7.2 122.9 %all-gather.2.cloned.1.call-start = ((), (), s32[]{:S(2)}) async-start(), calls=%async_computation.1 | async-start | bytes 12976128 | tf_op jit(solution)/shard_map/all_gather | solution.py:172
  25.4 54.3 %all-to-all-start = ((bf16[8,8,2,128,128]{4,3,2,1,0:T(8,128)(2,1)}), bf16[8,8,2,128,128]{4,3,2,1,0:T(8,128)(2,1)}, u32[]{:S(2)}, u32[]{:S(2)}) async-start(bf16[8,8,2,128,128]{4,3,2,1,0:T(8,128)(2,1)} %bitcast.56), calls=%async_computation | async-start | bytes 8388608 | tf_op jit(solution)/shard_map/all_to_all | solution.py:162
  130.1 8.8 %copy-start.3 = (bf16[256,768]{1,0:T(8,128)(2,1)S(1)}, bf16[256,768]{1,0:T(8,128)(2,1)}, u32[]{:S(2)}) copy-start(bf16[256,768]{1,0:T(8,128)(2,1)} %fusion.3) | copy-start | bytes 1179652
  138.9 39.9 %copy-start.5 = (bf16[256,768]{1,0:T(8,128)(2,1)}, bf16[256,768]{1,0:T(8,128)(2,1)S(1)}, u32[]{:S(2)}) copy-start(bf16[256,768]{1,0:T(8,128)(2,1)S(1)} %fusion.2) | copy-start | bytes 1179652
Sparse Core Ops, SparseCore 0:
  11.8 118.3 all-gather.1

commit v14 on v13

--- a/solution.py
+++ b/solution.py
@@ -35,8 +35,10 @@
         pl.semaphore_signal(barrier, 1, device_id=(grp, peer), device_id_type=mesh_ids)
         return carry
 
-    lax.fori_loop(1, inner, greet_row, 0)
-    lax.fori_loop(1, outer, greet_col, 0)
+    for k in range(1, inner):
+        greet_row(k, 0)
+    for k in range(1, outer):
+        greet_col(k, 0)
     pl.semaphore_wait(barrier, inner + outer - 2)
 
     own = pltpu.make_async_copy(part_ref.at[:, col], first.at[0], local_sem)
@@ -61,9 +63,11 @@
         stage_one(k).wait()
         return carry
 
-    lax.fori_loop(1, inner, start_one, 0)
+    for k in range(1, inner):
+        start_one(k, 0)
     own.wait()
-    lax.fori_loop(1, inner, finish_one, 0)
+    for k in range(1, inner):
+        finish_one(k, 0)
 
     mid[...] = first[0].astype(jnp.float32)
 
@@ -71,7 +75,8 @@
         mid[...] += first[k].astype(jnp.float32)
         return carry
 
-    lax.fori_loop(1, inner, add_first, 0)
+    for k in range(1, inner):
+        add_first(k, 0)
 
     def stage_two(k):
         dest = lax.rem(row + k, outer)
@@ -92,8 +97,10 @@
         stage_two(k).wait()
         return carry
 
-    lax.fori_loop(1, outer, start_two, 0)
-    lax.fori_loop(1, outer, finish_two, 0)
+    for k in range(1, outer):
+        start_two(k, 0)
+    for k in range(1, outer):
+        finish_two(k, 0)
 
     out_ref[...] = mid[row]
 
@@ -101,7 +108,8 @@
         out_ref[...] += second[k]
         return carry
 
-    lax.fori_loop(1, outer, add_second, 0)
+    for k in range(1, outer):
+        add_second(k, 0)
 
 
 def scatter_sum(part, n):

time: 186 us -> 186 us (level)
  no operation moved by 1% of the time
where the time goes in v14:
time: 186 us
  waiting for transfers between devices  80.9 us (43%)
  Pallas kernels  36.8 us (20%)
  local copies, waits for them, and re-layouts  25.1 us (13%)
  between operations  14.2 us (8%)
  matrix products  12.9 us (7%)
  other arithmetic  11.1 us (6%)
  starting transfers between devices  4.64 us (2%)
    all_to_all x1, waiting for transfers between devices, per_device(): lax.all_to_all(outgoing, 'grp', split_axis=0, concat_axis=0, tiled=True)  47 us
    pallas_call x1, Pallas kernels, scatter_sum(): pl.pallas_call(functools.partial(_scatter_sum_kernel, inner, outer), out_...  36.8 us
    all_gather x1, waiting for transfers between devices, per_device(): full = lax.all_gather(scaled, 'pan', axis=0, tiled=True)  33.9 us
    dot_general x1, matrix products, per_device(): lax.dot_general(sigma, full.reshape(front_len, BLK, P_SIZE), (((0, 2), (0...  8.79 us
    dot_general x1, local copies, waits for them, and re-layouts, per_device(): lax.dot_general(sigma, full.reshape(front_len, BLK, P_SIZE), (((0, 2), (0...  6.42 us
    gather x1, local copies, waits for them, and re-layouts, per_device(): jnp.take(received.reshape(groups * per_src, rb_local, BLK, BLK), order, a...  5.2 us
    select_n x2, other arithmetic, per_device(): jnp.take(received.reshape(groups * per_src, rb_local, BLK, BLK), order, a...  4.9 us
    all_to_all x1, starting transfers between devices, per_device(): lax.all_to_all(outgoing, 'grp', split_axis=0, concat_axis=0, tiled=True)  4.61 us
  transfers between devices with their start and end apart: 2, of which 2 were waited for; matrix products, arithmetic and copies ran while one was open for 18% of the time, Pallas kernels for 0%

profile of v14, /device:TPU:70, one launch (start us, length us, event | category | flops | bytes accessed | tf_op | source)
XLA Modules:
  0.0 185.7 jit_solution(1295746577194180056)
XLA Ops:
  7.3 1.4 dynamic_slice.16
  8.7 0.7 add_compare_fusion
  9.4 2.2 %fusion.3 = bf16[256,768]{1,0:T(8,128)(2,1)} fusion(bf16[1,768,768]{2,1,0:T(8,128)(2,1)S(1)} %copy-done, bf16[1,256,768]{2,1,0:T(8,128)(2,1)} %param.10, pred[256]{0:T(512)(128)(4,1)S(1)} %broadcast_bitcast_fusion), kind=kOutput, calls=%fused_computation.12 | convolution fusion | flops 302383104 | bytes 1966336 | tf_op jit(solution)/shard_map/dot_general | solution.py:178
  11.7 1.4 gather_fusion
  13.0 1.6 sort.34
  14.7 0.1 mul.53
  14.7 0.1 copy.20
  14.8 0.1 add.142
  15.0 0.2 dynamic-slice_reduce_fusion
  15.2 0.8 copy.23
  16.0 0.6 gather_fusion.1
  16.6 0.1 reshape.182
  16.7 0.8 gather_fusion.2
  17.6 0.1 fusion.11
  18.0 0.1 reshape.188
  18.1 2.1 %reshape.205 = bf16[16,128,4,128]{3,2,1,0:T(4,128)(2,1)} reshape(bf16[2048,512]{1,0:T(8,128)(2,1)S(1)} %copy-done.2) | data formatting | bytes 4194304 | tf_op jit(solution)/shard_map/reshape | solution.py:168
  20.2 2.1 %copy.27 = bf16[16,128,4,128]{3,1,2,0:T(8,128)(2,1)S(1)} copy(bf16[16,128,4,128]{3,2,1,0:T(4,128)(2,1)} %reshape.205) | data formatting | bytes 4194304 | tf_op jit(solution)/shard_map/reshape | solution.py:168
  22.4 3.1 %gather_fusion.3 = bf16[128,128,128]{2,1,0:T(8,128)(2,1)} fusion(bf16[16,128,4,128]{3,1,2,0:T(8,128)(2,1)S(1)} %copy.27, s32[128]{0:T(128)S(1)} %reshape.188), kind=kCustom, calls=%fused_computation.3 | custom fusion | bytes 8389632 | tf_op jit(solution)/shard_map/gather | solution.py:169
  25.4 4.6 %all-to-all-start = ((bf16[8,8,2,128,128]{4,3,2,1,0:T(8,128)(2,1)}), bf16[8,8,2,128,128]{4,3,2,1,0:T(8,128)(2,1)}, u32[]{:S(2)}, u32[]{:S(2)}) async-start(bf16[8,8,2,128,128]{4,3,2,1,0:T(8,128)(2,1)} %bitcast.56), calls=%async_computation | async-start | bytes 8388608 | tf_op jit(solution)/shard_map/all_to_all | solution.py:170
  30.1 0.1 copy.21
  30.2 0.1 add.137
  30.3 2.0 %sort.35 = (s32[64]{0:T(128)}, s32[64]{0:T(128)S(1)}) sort(s32[64]{0:T(128)S(1)} %add.137, s32[64]{0:T(128)S(1)} %iota.27), dimensions={0}, to_apply=%region_1.2 | sort | flops 384 | bytes 1024 | tf_op jit(solution)/shard_map/jit(argsort)/sort | solution.py:171
  32.4 0.3 fusion.4
  32.7 47.0 %all-to-all-done = bf16[8,8,2,128,128]{4,3,2,1,0:T(8,128)(2,1)} async-done(((bf16[8,8,2,128,128]{4,3,2,1,0:T(8,128)(2,1)}), bf16[8,8,2,128,128]{4,3,2,1,0:T(8,128)(2,1)}, u32[]{:S(2)}, u32[]{:S(2)}) %all-to-all-start) | async-done | bytes 4194336 | tf_op jit(solution)/shard_map/all_to_all | solution.py:170
  79.7 5.2 %gather_fusion.4 = bf16[64,2,128,128]{3,2,1,0:T(8,128)(2,1)} fusion(bf16[64,2,128,128]{3,2,1,0:T(8,128)(2,1)} %bitcast.8, s32[1024]{0:T(1024)S(1)} %pad_clamp_fusion), kind=kCustom, calls=%fused_computation.4 | custom fusion | bytes 8388864 | tf_op jit(solution)/shard_map/jit(_take)/gather | solution.py:172
  84.9 4.9 %select_bitcast_fusion = bf16[2,128,64,128]{1,3,0,2:T(8,128)(2,1)} fusion(bf16[64,2,128,128]{3,2,1,0:T(8,128)(2,1)} %gather_fusion.4, pred[64]{0:T(512)(128)(4,1)S(1)} %compare_and_fusion.1), kind=kLoop, calls=%fused_computation.5 | loop fusion | flops 2097152 | bytes 8388672 | tf_op jit(solution)/shard_map/jit(_take)/select_n | solution.py:172
  89.8 6.4 %copy.32 = bf16[2,128,64,128]{3,1,0,2:T(8,128)(2,1)} copy(bf16[2,128,64,128]{1,3,0,2:T(8,128)(2,1)} %select_bitcast_fusion) | data formatting | bytes 8388608 | tf_op jit(solution)/shard_map/dot_general | solution.py:181
  96.2 33.9 %all-gather.2.cloned.1.call-done = bf16[8192,768]{1,0:T(8,128)(2,1)} async-done(((bf16[256,768]{1,0:T(8,128)(2,1)}), bf16[8192,768]{1,0:T(8,128)(2,1)}) %all-gather.2.cloned.1.call-update) | async-done | bytes 12582928 | tf_op jit(solution)/shard_map/all_gather | solution.py:180
  130.1 8.8 %fusion.2 = bf16[256,768]{1,0:T(8,128)(2,1)S(1)} fusion(bf16[256,64,128]{2,0,1:T(8,128)(2,1)} %bitcast.57, bf16[64,128,768]{2,1,0:T(8,128)(2,1)} %bitcast.61, pred[256]{0:T(512)(128)(4,1)S(1)} %broadcast_bitcast_fusion), kind=kOutput, calls=%fused_computation.11 | convolution fusion | flops 3221815296 | bytes 17170688 | tf_op jit(solution)/shard_map/dot_general | solution.py:181
  139.0 1.5 negate_convert_fusion
  140.5 36.8 %shard_map.77 = f32[24,768]{1,0:T(8,128)} custom-call(bf16[8,4,24,768]{3,2,1,0:T(8,128)(2,1)} %bitcast.58), custom_call_target="tpu_custom_call" | custom-call | tf_op jit(solution)/shard_map/pallas_call | solution.py:119
  177.3 1.5 add_bitcast_fusion
  (39 shorter events, 0.8 us)
Async XLA Ops:
  7.2 2.2 %copy-start = (bf16[1,768,768]{2,1,0:T(8,128)(2,1)S(1)}, bf16[1,768,768]{2,1,0:T(8,128)(2,1)}, u32[]{:S(2)}) copy-start(bf16[1,768,768]{2,1,0:T(8,128)(2,1)} %param.11) | copy-start | bytes 3538948
  7.2 9.5 %copy-start.1 = (s32[128]{0:T(128)S(1)}, s32[128]{0:T(128)}, u32[]{:S(2)}) copy-start(s32[128]{0:T(128)} %param.7) | copy-start | bytes 1540
  7.2 10.6 %copy-start.4 = (s32[8,64]{1,0:T(8,128)S(1)}, s32[8,64]{1,0:T(8,128)}, u32[]{:S(2)}) copy-start(s32[8,64]{1,0:T(8,128)} %param.8) | copy-start | bytes 6148
  7.2 10.9 %copy-start.2 = (bf16[2048,512]{1,0:T(8,128)(2,1)S(1)}, bf16[2048,512]{1,0:T(8,128)(2,1)}, u32[]{:S(2)}) copy-start(bf16[2048,512]{1,0:T(8,128)(2,1)} %param.6) | copy-start | bytes 6291460
  7.2 122.9 %all-gather.2.cloned.1.call-start = ((), (), s32[]{:S(2)}) async-start(), calls=%async_computation.1 | async-start | bytes 12976128 | tf_op jit(solution)/shard_map/all_gather | solution.py:180
  25.4 54.3 %all-to-all-start = ((bf16[8,8,2,128,128]{4,3,2,1,0:T(8,128)(2,1)}), bf16[8,8,2,128,128]{4,3,2,1,0:T(8,128)(2,1)}, u32[]{:S(2)}, u32[]{:S(2)}) async-start(bf16[8,8,2,128,128]{4,3,2,1,0:T(8,128)(2,1)} %bitcast.56), calls=%async_computation | async-start | bytes 8388608 | tf_op jit(solution)/shard_map/all_to_all | solution.py:170
  130.1 8.8 %copy-start.3 = (bf16[256,768]{1,0:T(8,128)(2,1)S(1)}, bf16[256,768]{1,0:T(8,128)(2,1)}, u32[]{:S(2)}) copy-start(bf16[256,768]{1,0:T(8,128)(2,1)} %fusion.3) | copy-start | bytes 1179652
  138.9 39.9 %copy-start.5 = (bf16[256,768]{1,0:T(8,128)(2,1)}, bf16[256,768]{1,0:T(8,128)(2,1)S(1)}, u32[]{:S(2)}) copy-start(bf16[256,768]{1,0:T(8,128)(2,1)S(1)} %fusion.2) | copy-start | bytes 1179652
Sparse Core Ops, SparseCore 0:
  11.8 118.3 all-gather.1

commit v15 on v14

--- a/solution.py
+++ b/solution.py
@@ -15,7 +15,7 @@
 
 
 def _scatter_sum_kernel(
-    inner, outer, part_ref, out_ref, first, mid, second, sems, local_sem
+    inner, outer, scaled_ref, cross_ref, out_ref, part_ref, first, mid, second, sems, local_sem
 ):
     me = lax.axis_index("pan")
     grp = lax.axis_index("grp")
@@ -40,6 +40,16 @@
     for k in range(1, outer):
         greet_col(k, 0)
     pl.semaphore_wait(barrier, inner + outer - 2)
+
+    rows = part_ref.shape[2]
+    part = -lax.dot_general(
+        scaled_ref[...], cross_ref[...], (((0,), (0,)), ((), ())),
+        preferred_element_type=jnp.float32,
+    )
+    for o in range(outer):
+        for i in range(inner):
+            slab = o * inner + i
+            part_ref[o, i] = part[slab * rows : (slab + 1) * rows].astype(part_ref.dtype)
 
     own = pltpu.make_async_copy(part_ref.at[:, col], first.at[0], local_sem)
     own.start()
@@ -112,17 +122,19 @@
         add_second(k, 0)
 
 
-def scatter_sum(part, n):
-    _, rows, cols = part.shape
+def scatter_sum(scaled, cross, n):
+    cols = cross.shape[1]
+    rows = scaled.shape[1] // n
     inner = PAN_INNER
     outer = n // inner
     return pl.pallas_call(
         functools.partial(_scatter_sum_kernel, inner, outer),
         out_shape=jax.ShapeDtypeStruct((rows, cols), jnp.float32),
-        in_specs=[pl.BlockSpec(memory_space=pl.ANY)],
+        in_specs=[pl.BlockSpec(memory_space=pltpu.VMEM), pl.BlockSpec(memory_space=pltpu.VMEM)],
         out_specs=pl.BlockSpec(memory_space=pltpu.VMEM),
         scratch_shapes=[
-            pltpu.VMEM((inner, outer, rows, cols), part.dtype),
+            pltpu.VMEM((outer, inner, rows, cols), cross.dtype),
+            pltpu.VMEM((inner, outer, rows, cols), cross.dtype),
             pltpu.VMEM((outer, rows, cols), jnp.float32),
             pltpu.VMEM((outer, rows, cols), jnp.float32),
             (
@@ -134,7 +146,7 @@
             pltpu.SemaphoreType.DMA,
         ],
         compiler_params=pltpu.CompilerParams(collective_id=0, has_side_effects=True),
-    )(part.reshape(outer, inner, rows, cols))
+    )(scaled, cross)
 
 
 def per_device(anc_rows, row_home, block_lists, front_blocks, panel, pivot_inverse):
@@ -186,10 +198,7 @@
     ).reshape(rb_local * BLK, P_SIZE)
     cross = jnp.where(alive_rows[:, None], -product, jnp.zeros_like(product)).astype(jnp.bfloat16)
     pivot_rows = P_SIZE // pan_count
-    part = (-lax.dot_general(scaled, cross, contract, preferred_element_type=jnp.float32)).astype(
-        jnp.bfloat16
-    )
-    shared = scatter_sum(part.reshape(pan_count, pivot_rows, P_SIZE), pan_count)
+    shared = scatter_sum(scaled, cross, pan_count)
     own_columns = lax.dynamic_slice_in_dim(inverse_pivot, pan_idx * pivot_rows, pivot_rows, 1)
     triangle = lax.dot_general(
         own_columns, inverse_pivot, contract, preferred_element_type=jnp.float32

time: 186 us -> 187 us (level)
  no operation moved by 1% of the time
where the time goes in v15:
time: 187 us; the launch traced here: 186 us
  waiting for transfers between devices  80.9 us (43%)
  Pallas kernels  38.3 us (20%)
  local copies, waits for them, and re-layouts  25.1 us (13%)
  between operations  14.2 us (8%)
  matrix products  12 us (6%)
  other arithmetic  11.1 us (6%)
  starting transfers between devices  4.64 us (2%)
    all_to_all x1, waiting for transfers between devices, per_device(): lax.all_to_all(outgoing, 'grp', split_axis=0, concat_axis=0, tiled=True)  47 us
    pallas_call x1, Pallas kernels, scatter_sum(): pl.pallas_call(functools.partial(_scatter_sum_kernel, inner, outer), out_...  38.3 us
    all_gather x1, waiting for transfers between devices, per_device(): full = lax.all_gather(scaled, 'pan', axis=0, tiled=True)  33.9 us
    dot_general x1, matrix products, per_device(): lax.dot_general(sigma, full.reshape(front_len, BLK, P_SIZE), (((0, 2), (0...  9.41 us
    dot_general x1, local copies, waits for them, and re-layouts, per_device(): lax.dot_general(sigma, full.reshape(front_len, BLK, P_SIZE), (((0, 2), (0...  6.42 us
    gather x1, local copies, waits for them, and re-layouts, per_device(): jnp.take(received.reshape(groups * per_src, rb_local, BLK, BLK), order, a...  5.2 us
    select_n x2, other arithmetic, per_device(): jnp.take(received.reshape(groups * per_src, rb_local, BLK, BLK), order, a...  4.9 us
    all_to_all x1, starting transfers between devices, per_device(): lax.all_to_all(outgoing, 'grp', split_axis=0, concat_axis=0, tiled=True)  4.61 us
  transfers between devices with their start and end apart: 2, of which 2 were waited for; matrix products, arithmetic and copies ran while one was open for 18% of the time, Pallas kernels for 0%

profile of v15, /device:TPU:70, one launch (start us, length us, event | category | flops | bytes accessed | tf_op | source)
XLA Modules:
  0.0 186.2 jit_solution(11143689693356586908)
XLA Ops:
  7.3 1.4 dynamic_slice.16
  8.7 0.7 add_compare_fusion
  9.4 2.2 %fusion.3.scaled_ref = bf16[256,768]{1,0:T(8,128)(2,1)} fusion(bf16[1,768,768]{2,1,0:T(8,128)(2,1)S(1)} %copy-done, bf16[1,256,768]{2,1,0:T(8,128)(2,1)} %param.10, pred[256]{0:T(512)(128)(4,1)S(1)} %broadcast_bitcast_fusion), kind=kOutput, calls=%fused_computation.11 | convolution fusion | flops 302383104 | bytes 1966336 | tf_op jit(solution)/shard_map/dot_general | solution.py:190
  11.7 1.4 gather_fusion
  13.1 1.6 sort.34
  14.7 0.1 mul.53
  14.7 0.1 copy.20
  14.8 0.1 add.142
  15.0 0.2 dynamic-slice_reduce_fusion
  15.2 0.8 copy.23
  16.0 0.6 gather_fusion.1
  16.6 0.1 reshape.182
  16.7 0.8 gather_fusion.2
  17.5 0.1 reshape.181
  17.6 0.1 fusion.11
  18.0 0.1 reshape.188
  18.1 2.1 %reshape.205 = bf16[16,128,4,128]{3,2,1,0:T(4,128)(2,1)} reshape(bf16[2048,512]{1,0:T(8,128)(2,1)S(1)} %copy-done.2) | data formatting | bytes 4194304 | tf_op jit(solution)/shard_map/reshape | solution.py:180
  20.2 2.1 %copy.27 = bf16[16,128,4,128]{3,1,2,0:T(8,128)(2,1)S(1)} copy(bf16[16,128,4,128]{3,2,1,0:T(4,128)(2,1)} %reshape.205) | data formatting | bytes 4194304 | tf_op jit(solution)/shard_map/reshape | solution.py:180
  22.4 3.1 %gather_fusion.3 = bf16[128,128,128]{2,1,0:T(8,128)(2,1)} fusion(bf16[16,128,4,128]{3,1,2,0:T(8,128)(2,1)S(1)} %copy.27, s32[128]{0:T(128)S(1)} %reshape.188), kind=kCustom, calls=%fused_computation.3 | custom fusion | bytes 8389632 | tf_op jit(solution)/shard_map/gather | solution.py:181
  25.4 4.6 %all-to-all-start = ((bf16[8,8,2,128,128]{4,3,2,1,0:T(8,128)(2,1)}), bf16[8,8,2,128,128]{4,3,2,1,0:T(8,128)(2,1)}, u32[]{:S(2)}, u32[]{:S(2)}) async-start(bf16[8,8,2,128,128]{4,3,2,1,0:T(8,128)(2,1)} %bitcast.53), calls=%async_computation | async-start | bytes 8388608 | tf_op jit(solution)/shard_map/all_to_all | solution.py:182
  30.1 0.1 copy.21
  30.2 0.1 add.137
  30.3 2.0 %sort.35 = (s32[64]{0:T(128)}, s32[64]{0:T(128)S(1)}) sort(s32[64]{0:T(128)S(1)} %add.137, s32[64]{0:T(128)S(1)} %iota.27), dimensions={0}, to_apply=%region_1.2 | sort | flops 384 | bytes 1024 | tf_op jit(solution)/shard_map/jit(argsort)/sort | solution.py:183
  32.4 0.3 fusion.4
  32.7 47.0 %all-to-all-done = bf16[8,8,2,128,128]{4,3,2,1,0:T(8,128)(2,1)} async-done(((bf16[8,8,2,128,128]{4,3,2,1,0:T(8,128)(2,1)}), bf16[8,8,2,128,128]{4,3,2,1,0:T(8,128)(2,1)}, u32[]{:S(2)}, u32[]{:S(2)}) %all-to-all-start) | async-done | bytes 4194336 | tf_op jit(solution)/shard_map/all_to_all | solution.py:182
  79.7 5.2 %gather_fusion.4 = bf16[64,2,128,128]{3,2,1,0:T(8,128)(2,1)} fusion(bf16[64,2,128,128]{3,2,1,0:T(8,128)(2,1)} %bitcast.8, s32[1024]{0:T(1024)S(1)} %pad_clamp_fusion), kind=kCustom, calls=%fused_computation.4 | custom fusion | bytes 8388864 | tf_op jit(solution)/shard_map/jit(_take)/gather | solution.py:184
  84.9 4.9 %select_bitcast_fusion = bf16[2,128,64,128]{1,3,0,2:T(8,128)(2,1)} fusion(bf16[64,2,128,128]{3,2,1,0:T(8,128)(2,1)} %gather_fusion.4, pred[64]{0:T(512)(128)(4,1)S(1)} %compare_and_fusion.1), kind=kLoop, calls=%fused_computation.5 | loop fusion | flops 2097152 | bytes 8388672 | tf_op jit(solution)/shard_map/jit(_take)/select_n | solution.py:184
  89.8 6.4 %copy.32 = bf16[2,128,64,128]{3,1,0,2:T(8,128)(2,1)} copy(bf16[2,128,64,128]{1,3,0,2:T(8,128)(2,1)} %select_bitcast_fusion) | data formatting | bytes 8388608 | tf_op jit(solution)/shard_map/dot_general | solution.py:193
  96.2 33.9 %all-gather.2.cloned.1.call-done = bf16[8192,768]{1,0:T(8,128)(2,1)} async-done(((bf16[256,768]{1,0:T(8,128)(2,1)}), bf16[8192,768]{1,0:T(8,128)(2,1)}) %all-gather.2.cloned.1.call-update) | async-done | bytes 12582928 | tf_op jit(solution)/shard_map/all_gather | solution.py:192
  130.1 9.4 %fusion.2.cross_ref = bf16[256,768]{1,0:T(8,128)(2,1)} fusion(bf16[256,64,128]{2,0,1:T(8,128)(2,1)} %bitcast.54, bf16[64,128,768]{2,1,0:T(8,128)(2,1)} %bitcast.58, pred[256]{0:T(512)(128)(4,1)S(1)} %broadcast_bitcast_fusion), kind=kOutput, calls=%fused_computation.10 | convolution fusion | flops 3221815296 | bytes 17170688 | tf_op jit(solution)/shard_map/dot_general | solution.py:193
  139.5 38.3 %shard_map.77 = f32[24,768]{1,0:T(8,128)} custom-call(bf16[256,768]{1,0:T(8,128)(2,1)} %fusion.3.scaled_ref, bf16[256,768]{1,0:T(8,128)(2,1)} %fusion.2.cross_ref), custom_call_target="tpu_custom_call" | custom-call | tf_op jit(solution)/shard_map/pallas_call | solution.py:130
  177.8 1.5 add_bitcast_fusion
  (34 shorter events, 0.7 us)
Async XLA Ops:
  7.2 2.2 %copy-start = (bf16[1,768,768]{2,1,0:T(8,128)(2,1)S(1)}, bf16[1,768,768]{2,1,0:T(8,128)(2,1)}, u32[]{:S(2)}) copy-start(bf16[1,768,768]{2,1,0:T(8,128)(2,1)} %param.11) | copy-start | bytes 3538948
  7.2 9.5 %copy-start.1 = (s32[128]{0:T(128)S(1)}, s32[128]{0:T(128)}, u32[]{:S(2)}) copy-start(s32[128]{0:T(128)} %param.7) | copy-start | bytes 1540
  7.2 10.6 %copy-start.3 = (s32[8,64]{1,0:T(8,128)S(1)}, s32[8,64]{1,0:T(8,128)}, u32[]{:S(2)}) copy-start(s32[8,64]{1,0:T(8,128)} %param.8) | copy-start | bytes 6148
  7.2 10.9 %copy-start.2 = (bf16[2048,512]{1,0:T(8,128)(2,1)S(1)}, bf16[2048,512]{1,0:T(8,128)(2,1)}, u32[]{:S(2)}) copy-start(bf16[2048,512]{1,0:T(8,128)(2,1)} %param.6) | copy-start | bytes 6291460
  7.2 122.9 %all-gather.2.cloned.1.call-start = ((), (), s32[]{:S(2)}) async-start(), calls=%async_computation.1 | async-start | bytes 12976128 | tf_op jit(solution)/shard_map/all_gather | solution.py:192
  25.4 54.3 %all-to-all-start = ((bf16[8,8,2,128,128]{4,3,2,1,0:T(8,128)(2,1)}), bf16[8,8,2,128,128]{4,3,2,1,0:T(8,128)(2,1)}, u32[]{:S(2)}, u32[]{:S(2)}) async-start(bf16[8,8,2,128,128]{4,3,2,1,0:T(8,128)(2,1)} %bitcast.53), calls=%async_computation | async-start | bytes 8388608 | tf_op jit(solution)/shard_map/all_to_all | solution.py:182
Sparse Core Ops, SparseCore 0:
  11.8 118.3 all-gather.1

commit v16 on v14

--- a/solution.py
+++ b/solution.py
@@ -175,9 +175,11 @@
     front_live = lax.dynamic_index_in_dim(front_blocks, group_idx, 0, keepdims=False)
     alive_rows = jnp.repeat(my_blocks < front_live, BLK)
     inverse_pivot = pivot_inverse[0]
-    scaled = jnp.dot(panel[0], inverse_pivot, preferred_element_type=jnp.float32)
-    scaled = jnp.where(alive_rows[:, None], scaled, jnp.zeros_like(scaled)).astype(jnp.bfloat16)
-    full = lax.all_gather(scaled, "pan", axis=0, tiled=True)
+    raw = jnp.dot(panel[0], inverse_pivot, preferred_element_type=jnp.float32).astype(jnp.bfloat16)
+    full = lax.all_gather(raw, "pan", axis=0, tiled=True)
+    scaled = jnp.where(alive_rows[:, None], raw, jnp.zeros_like(raw))
+    alive_blocks = jnp.arange(front_len, dtype=jnp.int32) < front_live
+    sigma = jnp.where(alive_blocks[:, None, None, None], sigma, jnp.zeros_like(sigma))
     product = lax.dot_general(
         sigma,
         full.reshape(front_len, BLK, P_SIZE),

time: 186 us -> 186 us (level)
    select_n x2 -> x1, other arithmetic: 4.9 us -> 0.01 us  [per_device(): jnp.take(received.reshape(groups * per_src, rb_local, BLK, BLK), order, a...]
    select_n x0 -> x1, other arithmetic: none -> 4.19 us  [per_device(): jnp.where(alive_blocks[:, None, None, None], sigma, jnp.zeros_like(sigma))]
    all_to_all x1, waiting for transfers between devices: 47 us -> 45.1 us  [per_device(): lax.all_to_all(outgoing, 'grp', split_axis=0, concat_axis=0, tiled=True)]
where the time goes in v16:
time: 186 us; the launch traced here: 185 us
  waiting for transfers between devices  80.1 us (43%)
  Pallas kernels  36.8 us (20%)
  local copies, waits for them, and re-layouts  25.5 us (14%)
  between operations  14.2 us (8%)
  matrix products  13 us (7%)
  other arithmetic  11 us (6%)
  starting transfers between devices  4.81 us (3%)
    all_to_all x1, waiting for transfers between devices, per_device(): lax.all_to_all(outgoing, 'grp', split_axis=0, concat_axis=0, tiled=True)  45.1 us
    pallas_call x1, Pallas kernels, scatter_sum(): pl.pallas_call(functools.partial(_scatter_sum_kernel, inner, outer), out_...  36.8 us
    all_gather x1, waiting for transfers between devices, per_device(): full = lax.all_gather(raw, 'pan', axis=0, tiled=True)  35 us
    dot_general x1, matrix products, per_device(): lax.dot_general(sigma, full.reshape(front_len, BLK, P_SIZE), (((0, 2), (0...  8.79 us
    dot_general x1, local copies, waits for them, and re-layouts, per_device(): lax.dot_general(sigma, full.reshape(front_len, BLK, P_SIZE), (((0, 2), (0...  6.39 us
    gather x1, local copies, waits for them, and re-layouts, per_device(): jnp.take(received.reshape(groups * per_src, rb_local, BLK, BLK), order, a...  5.19 us
    all_to_all x1, starting transfers between devices, per_device(): lax.all_to_all(outgoing, 'grp', split_axis=0, concat_axis=0, tiled=True)  4.77 us
    reshape x2, local copies, waits for them, and re-layouts, per_device(): local = anc_rows.reshape(stored_blocks, BLK, cb_local, BLK)  4.26 us
  transfers between devices with their start and end apart: 2, of which 2 were waited for; matrix products, arithmetic and copies ran while one was open for 18% of the time, Pallas kernels for 0%

profile of v16, /device:TPU:70, one launch (start us, length us, event | category | flops | bytes accessed | tf_op | source)
XLA Modules:
  0.0 185.3 jit_solution(4593313947800567673)
XLA Ops:
  7.3 1.2 copy-done
  8.4 2.2 %convolution_convert_fusion = bf16[256,768]{1,0:T(8,128)(2,1)} fusion(bf16[1,768,768]{2,1,0:T(8,128)(2,1)S(1)} %copy-done, bf16[1,256,768]{2,1,0:T(8,128)(2,1)} %param.10), kind=kOutput, calls=%fused_computation.11 | convolution fusion | flops 302186496 | bytes 1966080 | tf_op jit(solution)/shard_map/dot_general | solution.py:178
  10.7 1.4 gather_fusion
  12.1 1.6 sort.34
  13.8 0.1 copy.20
  13.9 0.1 add.142
  14.0 0.8 copy.23
  14.8 0.2 dynamic-slice_reduce_fusion
  15.0 0.6 gather_fusion.1
  15.7 0.1 reshape.186
  15.8 0.8 gather_fusion.2
  17.0 0.1 reshape.192
  17.2 2.1 %reshape.209 = bf16[16,128,4,128]{3,2,1,0:T(4,128)(2,1)} reshape(bf16[2048,512]{1,0:T(8,128)(2,1)S(1)} %copy-done.2) | data formatting | bytes 4194304 | tf_op jit(solution)/shard_map/reshape | solution.py:168
  19.3 2.1 %copy.27 = bf16[16,128,4,128]{3,1,2,0:T(8,128)(2,1)S(1)} copy(bf16[16,128,4,128]{3,2,1,0:T(4,128)(2,1)} %reshape.209) | data formatting | bytes 4194304 | tf_op jit(solution)/shard_map/reshape | solution.py:168
  21.4 3.1 %gather_fusion.3 = bf16[128,128,128]{2,1,0:T(8,128)(2,1)} fusion(bf16[16,128,4,128]{3,1,2,0:T(8,128)(2,1)S(1)} %copy.27, s32[128]{0:T(128)S(1)} %reshape.192), kind=kCustom, calls=%fused_computation.3 | custom fusion | bytes 8389632 | tf_op jit(solution)/shard_map/gather | solution.py:169
  24.5 4.8 %all-to-all-start = ((bf16[8,8,2,128,128]{4,3,2,1,0:T(8,128)(2,1)}), bf16[8,8,2,128,128]{4,3,2,1,0:T(8,128)(2,1)}, u32[]{:S(2)}, u32[]{:S(2)}) async-start(bf16[8,8,2,128,128]{4,3,2,1,0:T(8,128)(2,1)} %bitcast.55), calls=%async_computation | async-start | bytes 8388608 | tf_op jit(solution)/shard_map/all_to_all | solution.py:170
  29.3 0.1 copy.21
  29.4 0.1 add.137
  29.5 0.6 dynamic_slice.16
  30.1 2.0 %sort.35 = (s32[64]{0:T(128)}, s32[64]{0:T(128)S(1)}) sort(s32[64]{0:T(128)S(1)} %add.137, s32[64]{0:T(128)S(1)} %iota.33), dimensions={0}, to_apply=%region_1.2 | sort | flops 384 | bytes 1024 | tf_op jit(solution)/shard_map/jit(argsort)/sort | solution.py:171
  32.2 0.6 add_compare_fusion
  32.9 0.6 compare_and_fusion.1
  33.5 0.3 fusion.3
  33.9 45.1 %all-to-all-done = bf16[8,8,2,128,128]{4,3,2,1,0:T(8,128)(2,1)} async-done(((bf16[8,8,2,128,128]{4,3,2,1,0:T(8,128)(2,1)}), bf16[8,8,2,128,128]{4,3,2,1,0:T(8,128)(2,1)}, u32[]{:S(2)}, u32[]{:S(2)}) %all-to-all-start) | async-done | bytes 4194336 | tf_op jit(solution)/shard_map/all_to_all | solution.py:170
  78.9 5.2 %gather_fusion.4 = bf16[64,2,128,128]{3,2,1,0:T(8,128)(2,1)} fusion(bf16[64,2,128,128]{3,2,1,0:T(8,128)(2,1)} %bitcast.8, s32[1024]{0:T(1024)S(1)} %pad_clamp_fusion), kind=kCustom, calls=%fused_computation.4 | custom fusion | bytes 8388864 | tf_op jit(solution)/shard_map/jit(_take)/gather | solution.py:172
  84.1 4.2 %select_bitcast_fusion = bf16[2,128,64,128]{1,3,0,2:T(8,128)(2,1)} fusion(bf16[64,2,128,128]{3,2,1,0:T(8,128)(2,1)} %gather_fusion.4, pred[64]{0:T(512)(128)(4,1)S(1)} %get-tuple-element.10, pred[64]{0:T(512)(128)(4,1)S(1)} %get-tuple-element.11), kind=kLoop, calls=%fused_computation.5 | loop fusion | flops 4194304 | bytes 8388736 | tf_op jit(solution)/shard_map/jit(_where)/select_n | solution.py:182
  88.3 6.4 %copy.32 = bf16[2,128,64,128]{3,1,0,2:T(8,128)(2,1)} copy(bf16[2,128,64,128]{1,3,0,2:T(8,128)(2,1)} %select_bitcast_fusion) | data formatting | bytes 8388608 | tf_op jit(solution)/shard_map/dot_general | solution.py:183
  94.7 35.0 %all-gather.2.cloned.1.call-done = bf16[8192,768]{1,0:T(8,128)(2,1)} async-done(((bf16[256,768]{1,0:T(8,128)(2,1)}), bf16[8192,768]{1,0:T(8,128)(2,1)}) %all-gather.2.cloned.1.call-update) | async-done | bytes 12582928 | tf_op jit(solution)/shard_map/all_gather | solution.py:179
  129.7 8.8 %fusion.2 = bf16[256,768]{1,0:T(8,128)(2,1)S(1)} fusion(bf16[256,64,128]{2,0,1:T(8,128)(2,1)} %bitcast.56, bf16[64,128,768]{2,1,0:T(8,128)(2,1)} %bitcast.60, pred[256]{0:T(512)(128)(4,1)S(1)} %broadcast_bitcast_fusion), kind=kOutput, calls=%fused_computation.10 | convolution fusion | flops 3221815296 | bytes 17170688 | tf_op jit(solution)/shard_map/dot_general | solution.py:183
  138.5 1.6 negate_convert_fusion
  140.1 36.8 %shard_map.77 = f32[24,768]{1,0:T(8,128)} custom-call(bf16[8,4,24,768]{3,2,1,0:T(8,128)(2,1)} %bitcast.57), custom_call_target="tpu_custom_call" | custom-call | tf_op jit(solution)/shard_map/pallas_call | solution.py:119
  176.9 1.5 add_bitcast_fusion
  (41 shorter events, 0.9 us)
Async XLA Ops:
  7.2 1.3 copy-start
  7.2 8.6 %copy-start.1 = (s32[128]{0:T(128)S(1)}, s32[128]{0:T(128)}, u32[]{:S(2)}) copy-start(s32[128]{0:T(128)} %param.7) | copy-start | bytes 1540
  7.2 9.7 %copy-start.4 = (s32[8,64]{1,0:T(8,128)S(1)}, s32[8,64]{1,0:T(8,128)}, u32[]{:S(2)}) copy-start(s32[8,64]{1,0:T(8,128)} %param.8) | copy-start | bytes 6148
  7.2 10.0 %copy-start.2 = (bf16[2048,512]{1,0:T(8,128)(2,1)S(1)}, bf16[2048,512]{1,0:T(8,128)(2,1)}, u32[]{:S(2)}) copy-start(bf16[2048,512]{1,0:T(8,128)(2,1)} %param.6) | copy-start | bytes 6291460
  7.2 122.5 %all-gather.2.cloned.1.call-start = ((), (), s32[]{:S(2)}) async-start(), calls=%async_computation.1 | async-start | bytes 12976128 | tf_op jit(solution)/shard_map/all_gather | solution.py:179
  24.5 5.0 %copy-start.5 = (s32[8]{0:T(128)S(1)}, s32[8]{0:T(128)}, u32[]{:S(2)}) copy-start(s32[8]{0:T(128)} %param.9) | copy-start | bytes 100
  24.5 54.4 %all-to-all-start = ((bf16[8,8,2,128,128]{4,3,2,1,0:T(8,128)(2,1)}), bf16[8,8,2,128,128]{4,3,2,1,0:T(8,128)(2,1)}, u32[]{:S(2)}, u32[]{:S(2)}) async-start(bf16[8,8,2,128,128]{4,3,2,1,0:T(8,128)(2,1)} %bitcast.55), calls=%async_computation | async-start | bytes 8388608 | tf_op jit(solution)/shard_map/all_to_all | solution.py:170
  129.7 8.8 %copy-start.3 = (bf16[256,768]{1,0:T(8,128)(2,1)S(1)}, bf16[256,768]{1,0:T(8,128)(2,1)}, u32[]{:S(2)}) copy-start(bf16[256,768]{1,0:T(8,128)(2,1)} %convolution_convert_fusion) | copy-start | bytes 1179652
  138.5 40.0 %copy-start.6 = (bf16[256,768]{1,0:T(8,128)(2,1)}, bf16[256,768]{1,0:T(8,128)(2,1)S(1)}, u32[]{:S(2)}) copy-start(bf16[256,768]{1,0:T(8,128)(2,1)S(1)} %fusion.2) | copy-start | bytes 1179652
Sparse Core Ops, SparseCore 0:
  11.2 118.4 all-gather.1

commit v17 on v14

--- a/solution.py
+++ b/solution.py
@@ -15,7 +15,7 @@
 
 
 def _scatter_sum_kernel(
-    inner, outer, part_ref, out_ref, first, mid, second, sems, local_sem
+    inner, outer, part_ref, out_ref, first, mid, mid_out, second, sems, local_sem
 ):
     me = lax.axis_index("pan")
     grp = lax.axis_index("grp")
@@ -77,11 +77,12 @@
 
     for k in range(1, inner):
         add_first(k, 0)
+    mid_out[...] = mid[...].astype(mid_out.dtype)
 
     def stage_two(k):
         dest = lax.rem(row + k, outer)
         return pltpu.make_async_remote_copy(
-            src_ref=mid.at[dest],
+            src_ref=mid_out.at[dest],
             dst_ref=second.at[k],
             send_sem=send2.at[k],
             recv_sem=recv2.at[k],
@@ -105,7 +106,7 @@
     out_ref[...] = mid[row]
 
     def add_second(k, carry):
-        out_ref[...] += second[k]
+        out_ref[...] += second[k].astype(jnp.float32)
         return carry
 
     for k in range(1, outer):
@@ -124,7 +125,8 @@
         scratch_shapes=[
             pltpu.VMEM((inner, outer, rows, cols), part.dtype),
             pltpu.VMEM((outer, rows, cols), jnp.float32),
-            pltpu.VMEM((outer, rows, cols), jnp.float32),
+            pltpu.VMEM((outer, rows, cols), part.dtype),
+            pltpu.VMEM((outer, rows, cols), part.dtype),
             (
                 pltpu.SemaphoreType.DMA((inner,)),
                 pltpu.SemaphoreType.DMA((inner,)),

time: 186 us -> 180 us (0.968)
  Pallas kernels: 36.8 us -> 30.5 us
    pallas_call x1, Pallas kernels: 36.8 us -> 30.5 us  [scatter_sum(): pl.pallas_call(functools.partial(_scatter_sum_kernel, inner, outer), out_...]
where the time goes in v17:
time: 180 us; the launch traced here: 179 us
  waiting for transfers between devices  80.9 us (45%)
  Pallas kernels  30.5 us (17%)
  local copies, waits for them, and re-layouts  25.1 us (14%)
  between operations  14.2 us (8%)
  matrix products  12.9 us (7%)
  other arithmetic  11.1 us (6%)
  starting transfers between devices  4.64 us (3%)
    all_to_all x1, waiting for transfers between devices, per_device(): lax.all_to_all(outgoing, 'grp', split_axis=0, concat_axis=0, tiled=True)  47 us
    all_gather x1, waiting for transfers between devices, per_device(): full = lax.all_gather(scaled, 'pan', axis=0, tiled=True)  33.9 us
    pallas_call x1, Pallas kernels, scatter_sum(): pl.pallas_call(functools.partial(_scatter_sum_kernel, inner, outer), out_...  30.5 us
    dot_general x1, matrix products, per_device(): lax.dot_general(sigma, full.reshape(front_len, BLK, P_SIZE), (((0, 2), (0...  8.79 us
    dot_general x1, local copies, waits for them, and re-layouts, per_device(): lax.dot_general(sigma, full.reshape(front_len, BLK, P_SIZE), (((0, 2), (0...  6.42 us
    gather x1, local copies, waits for them, and re-layouts, per_device(): jnp.take(received.reshape(groups * per_src, rb_local, BLK, BLK), order, a...  5.2 us
    select_n x2, other arithmetic, per_device(): jnp.take(received.reshape(groups * per_src, rb_local, BLK, BLK), order, a...  4.9 us
    all_to_all x1, starting transfers between devices, per_device(): lax.all_to_all(outgoing, 'grp', split_axis=0, concat_axis=0, tiled=True)  4.61 us
  transfers between devices with their start and end apart: 2, of which 2 were waited for; matrix products, arithmetic and copies ran while one was open for 18% of the time, Pallas kernels for 0%

profile of v17, /device:TPU:70, one launch (start us, length us, event | category | flops | bytes accessed | tf_op | source)
XLA Modules:
  0.0 179.4 jit_solution(7048401993394685621)
XLA Ops:
  7.3 1.4 dynamic_slice.16
  8.7 0.7 add_compare_fusion
  9.4 2.2 %fusion.3 = bf16[256,768]{1,0:T(8,128)(2,1)} fusion(bf16[1,768,768]{2,1,0:T(8,128)(2,1)S(1)} %copy-done, bf16[1,256,768]{2,1,0:T(8,128)(2,1)} %param.10, pred[256]{0:T(512)(128)(4,1)S(1)} %broadcast_bitcast_fusion), kind=kOutput, calls=%fused_computation.12 | convolution fusion | flops 302383104 | bytes 1966336 | tf_op jit(solution)/shard_map/dot_general | solution.py:180
  11.7 1.4 gather_fusion
  13.0 1.6 sort.34
  14.7 0.1 mul.53
  14.7 0.1 copy.20
  14.8 0.1 add.142
  15.0 0.2 dynamic-slice_reduce_fusion
  15.2 0.8 copy.23
  16.0 0.6 gather_fusion.1
  16.6 0.1 reshape.182
  16.7 0.8 gather_fusion.2
  17.6 0.1 fusion.11
  18.0 0.1 reshape.188
  18.1 2.1 %reshape.205 = bf16[16,128,4,128]{3,2,1,0:T(4,128)(2,1)} reshape(bf16[2048,512]{1,0:T(8,128)(2,1)S(1)} %copy-done.2) | data formatting | bytes 4194304 | tf_op jit(solution)/shard_map/reshape | solution.py:170
  20.2 2.1 %copy.27 = bf16[16,128,4,128]{3,1,2,0:T(8,128)(2,1)S(1)} copy(bf16[16,128,4,128]{3,2,1,0:T(4,128)(2,1)} %reshape.205) | data formatting | bytes 4194304 | tf_op jit(solution)/shard_map/reshape | solution.py:170
  22.4 3.1 %gather_fusion.3 = bf16[128,128,128]{2,1,0:T(8,128)(2,1)} fusion(bf16[16,128,4,128]{3,1,2,0:T(8,128)(2,1)S(1)} %copy.27, s32[128]{0:T(128)S(1)} %reshape.188), kind=kCustom, calls=%fused_computation.3 | custom fusion | bytes 8389632 | tf_op jit(solution)/shard_map/gather | solution.py:171
  25.4 4.6 %all-to-all-start = ((bf16[8,8,2,128,128]{4,3,2,1,0:T(8,128)(2,1)}), bf16[8,8,2,128,128]{4,3,2,1,0:T(8,128)(2,1)}, u32[]{:S(2)}, u32[]{:S(2)}) async-start(bf16[8,8,2,128,128]{4,3,2,1,0:T(8,128)(2,1)} %bitcast.56), calls=%async_computation | async-start | bytes 8388608 | tf_op jit(solution)/shard_map/all_to_all | solution.py:172
  30.1 0.1 copy.21
  30.2 0.1 add.137
  30.3 2.0 %sort.35 = (s32[64]{0:T(128)}, s32[64]{0:T(128)S(1)}) sort(s32[64]{0:T(128)S(1)} %add.137, s32[64]{0:T(128)S(1)} %iota.27), dimensions={0}, to_apply=%region_1.2 | sort | flops 384 | bytes 1024 | tf_op jit(solution)/shard_map/jit(argsort)/sort | solution.py:173
  32.4 0.3 fusion.4
  32.7 47.0 %all-to-all-done = bf16[8,8,2,128,128]{4,3,2,1,0:T(8,128)(2,1)} async-done(((bf16[8,8,2,128,128]{4,3,2,1,0:T(8,128)(2,1)}), bf16[8,8,2,128,128]{4,3,2,1,0:T(8,128)(2,1)}, u32[]{:S(2)}, u32[]{:S(2)}) %all-to-all-start) | async-done | bytes 4194336 | tf_op jit(solution)/shard_map/all_to_all | solution.py:172
  79.7 5.2 %gather_fusion.4 = bf16[64,2,128,128]{3,2,1,0:T(8,128)(2,1)} fusion(bf16[64,2,128,128]{3,2,1,0:T(8,128)(2,1)} %bitcast.8, s32[1024]{0:T(1024)S(1)} %pad_clamp_fusion), kind=kCustom, calls=%fused_computation.4 | custom fusion | bytes 8388864 | tf_op jit(solution)/shard_map/jit(_take)/gather | solution.py:174
  84.9 4.9 %select_bitcast_fusion = bf16[2,128,64,128]{1,3,0,2:T(8,128)(2,1)} fusion(bf16[64,2,128,128]{3,2,1,0:T(8,128)(2,1)} %gather_fusion.4, pred[64]{0:T(512)(128)(4,1)S(1)} %compare_and_fusion.1), kind=kLoop, calls=%fused_computation.5 | loop fusion | flops 2097152 | bytes 8388672 | tf_op jit(solution)/shard_map/jit(_take)/select_n | solution.py:174
  89.8 6.4 %copy.32 = bf16[2,128,64,128]{3,1,0,2:T(8,128)(2,1)} copy(bf16[2,128,64,128]{1,3,0,2:T(8,128)(2,1)} %select_bitcast_fusion) | data formatting | bytes 8388608 | tf_op jit(solution)/shard_map/dot_general | solution.py:183
  96.2 33.9 %all-gather.2.cloned.1.call-done = bf16[8192,768]{1,0:T(8,128)(2,1)} async-done(((bf16[256,768]{1,0:T(8,128)(2,1)}), bf16[8192,768]{1,0:T(8,128)(2,1)}) %all-gather.2.cloned.1.call-update) | async-done | bytes 12582928 | tf_op jit(solution)/shard_map/all_gather | solution.py:182
  130.1 8.8 %fusion.2 = bf16[256,768]{1,0:T(8,128)(2,1)S(1)} fusion(bf16[256,64,128]{2,0,1:T(8,128)(2,1)} %bitcast.57, bf16[64,128,768]{2,1,0:T(8,128)(2,1)} %bitcast.61, pred[256]{0:T(512)(128)(4,1)S(1)} %broadcast_bitcast_fusion), kind=kOutput, calls=%fused_computation.11 | convolution fusion | flops 3221815296 | bytes 17170688 | tf_op jit(solution)/shard_map/dot_general | solution.py:183
  139.0 1.5 negate_convert_fusion
  140.5 30.5 %shard_map.77 = f32[24,768]{1,0:T(8,128)} custom-call(bf16[8,4,24,768]{3,2,1,0:T(8,128)(2,1)} %bitcast.58), custom_call_target="tpu_custom_call" | custom-call | tf_op jit(solution)/shard_map/pallas_call | solution.py:120
  171.0 1.5 add_bitcast_fusion
  (39 shorter events, 0.8 us)
Async XLA Ops:
  7.2 2.2 %copy-start = (bf16[1,768,768]{2,1,0:T(8,128)(2,1)S(1)}, bf16[1,768,768]{2,1,0:T(8,128)(2,1)}, u32[]{:S(2)}) copy-start(bf16[1,768,768]{2,1,0:T(8,128)(2,1)} %param.11) | copy-start | bytes 3538948
  7.2 9.5 %copy-start.1 = (s32[128]{0:T(128)S(1)}, s32[128]{0:T(128)}, u32[]{:S(2)}) copy-start(s32[128]{0:T(128)} %param.7) | copy-start | bytes 1540
  7.2 10.6 %copy-start.4 = (s32[8,64]{1,0:T(8,128)S(1)}, s32[8,64]{1,0:T(8,128)}, u32[]{:S(2)}) copy-start(s32[8,64]{1,0:T(8,128)} %param.8) | copy-start | bytes 6148
  7.2 10.9 %copy-start.2 = (bf16[2048,512]{1,0:T(8,128)(2,1)S(1)}, bf16[2048,512]{1,0:T(8,128)(2,1)}, u32[]{:S(2)}) copy-start(bf16[2048,512]{1,0:T(8,128)(2,1)} %param.6) | copy-start | bytes 6291460
  7.2 122.9 %all-gather.2.cloned.1.call-start = ((), (), s32[]{:S(2)}) async-start(), calls=%async_computation.1 | async-start | bytes 12976128 | tf_op jit(solution)/shard_map/all_gather | solution.py:182
  25.4 54.3 %all-to-all-start = ((bf16[8,8,2,128,128]{4,3,2,1,0:T(8,128)(2,1)}), bf16[8,8,2,128,128]{4,3,2,1,0:T(8,128)(2,1)}, u32[]{:S(2)}, u32[]{:S(2)}) async-start(bf16[8,8,2,128,128]{4,3,2,1,0:T(8,128)(2,1)} %bitcast.56), calls=%async_computation | async-start | bytes 8388608 | tf_op jit(solution)/shard_map/all_to_all | solution.py:172
  130.1 8.8 %copy-start.3 = (bf16[256,768]{1,0:T(8,128)(2,1)S(1)}, bf16[256,768]{1,0:T(8,128)(2,1)}, u32[]{:S(2)}) copy-start(bf16[256,768]{1,0:T(8,128)(2,1)} %fusion.3) | copy-start | bytes 1179652
  138.9 33.6 %copy-start.5 = (bf16[256,768]{1,0:T(8,128)(2,1)}, bf16[256,768]{1,0:T(8,128)(2,1)S(1)}, u32[]{:S(2)}) copy-start(bf16[256,768]{1,0:T(8,128)(2,1)S(1)} %fusion.2) | copy-start | bytes 1179652
Sparse Core Ops, SparseCore 0:
  11.8 118.3 all-gather.1

commit v18 on v17

--- a/solution.py
+++ b/solution.py
@@ -191,7 +191,10 @@
     part = (-lax.dot_general(scaled, cross, contract, preferred_element_type=jnp.float32)).astype(
         jnp.bfloat16
     )
-    shared = scatter_sum(part.reshape(pan_count, pivot_rows, P_SIZE), pan_count)
+    slab_rows = pivot_rows * P_SIZE // BLK
+    shared = scatter_sum(part.reshape(pan_count, slab_rows, BLK), pan_count).reshape(
+        pivot_rows, P_SIZE
+    )
     own_columns = lax.dynamic_slice_in_dim(inverse_pivot, pan_idx * pivot_rows, pivot_rows, 1)
     triangle = lax.dot_general(
         own_columns, inverse_pivot, contract, preferred_element_type=jnp.float32

time: 180 us -> 181 us (level)
  local copies, waits for them, and re-layouts: 25.1 us -> 27.8 us
    another operation x0 -> x1, local copies, waits for them, and re-layouts: none -> 1.86 us  [scatter_sum(): part.reshape(outer, inner, rows, cols)]
where the time goes in v18:
time: 181 us; the launch traced here: 180 us
  waiting for transfers between devices  80.9 us (45%)
  Pallas kernels  30.5 us (17%)
  local copies, waits for them, and re-layouts  27.8 us (15%)
  between operations  14.2 us (8%)
  matrix products  11.9 us (7%)
  other arithmetic  10.2 us (6%)
  starting transfers between devices  4.64 us (3%)
    all_to_all x1, waiting for transfers between devices, per_device(): lax.all_to_all(outgoing, 'grp', split_axis=0, concat_axis=0, tiled=True)  47 us
    all_gather x1, waiting for transfers between devices, per_device(): full = lax.all_gather(scaled, 'pan', axis=0, tiled=True)  33.9 us
    pallas_call x1, Pallas kernels, scatter_sum(): pl.pallas_call(functools.partial(_scatter_sum_kernel, inner, outer), out_...  30.5 us
    dot_general x1, matrix products, per_device(): lax.dot_general(sigma, full.reshape(front_len, BLK, P_SIZE), (((0, 2), (0...  8.79 us
    dot_general x1, local copies, waits for them, and re-layouts, per_device(): lax.dot_general(sigma, full.reshape(front_len, BLK, P_SIZE), (((0, 2), (0...  6.42 us
    gather x1, local copies, waits for them, and re-layouts, per_device(): jnp.take(received.reshape(groups * per_src, rb_local, BLK, BLK), order, a...  5.2 us
    select_n x2, other arithmetic, per_device(): jnp.take(received.reshape(groups * per_src, rb_local, BLK, BLK), order, a...  4.9 us
    all_to_all x1, starting transfers between devices, per_device(): lax.all_to_all(outgoing, 'grp', split_axis=0, concat_axis=0, tiled=True)  4.61 us
  transfers between devices with their start and end apart: 2, of which 2 were waited for; matrix products, arithmetic and copies ran while one was open for 18% of the time, Pallas kernels for 0%

profile of v18, /device:TPU:70, one launch (start us, length us, event | category | flops | bytes accessed | tf_op | source)
XLA Modules:
  0.0 180.3 jit_solution(17217927944468305783)
XLA Ops:
  7.3 1.4 dynamic_slice.16
  8.7 0.7 add_compare_fusion
  9.4 2.2 %fusion.3 = bf16[256,768]{1,0:T(8,128)(2,1)} fusion(bf16[1,768,768]{2,1,0:T(8,128)(2,1)S(1)} %copy-done, bf16[1,256,768]{2,1,0:T(8,128)(2,1)} %param.10, pred[256]{0:T(512)(128)(4,1)S(1)} %broadcast_bitcast_fusion), kind=kOutput, calls=%fused_computation.12 | convolution fusion | flops 302383104 | bytes 1966336 | tf_op jit(solution)/shard_map/dot_general | solution.py:180
  11.7 1.4 gather_fusion
  13.0 1.6 sort.34
  14.7 0.1 copy.20
  14.8 0.1 add.142
  15.0 0.2 dynamic-slice_reduce_fusion
  15.2 0.8 copy.23
  16.0 0.6 gather_fusion.1
  16.6 0.1 reshape.186
  16.7 0.8 gather_fusion.2
  18.0 0.1 reshape.192
  18.1 2.1 %reshape.209 = bf16[16,128,4,128]{3,2,1,0:T(4,128)(2,1)} reshape(bf16[2048,512]{1,0:T(8,128)(2,1)S(1)} %copy-done.2) | data formatting | bytes 4194304 | tf_op jit(solution)/shard_map/reshape | solution.py:170
  20.2 2.1 %copy.27 = bf16[16,128,4,128]{3,1,2,0:T(8,128)(2,1)S(1)} copy(bf16[16,128,4,128]{3,2,1,0:T(4,128)(2,1)} %reshape.209) | data formatting | bytes 4194304 | tf_op jit(solution)/shard_map/reshape | solution.py:170
  22.4 3.1 %gather_fusion.3 = bf16[128,128,128]{2,1,0:T(8,128)(2,1)} fusion(bf16[16,128,4,128]{3,1,2,0:T(8,128)(2,1)S(1)} %copy.27, s32[128]{0:T(128)S(1)} %reshape.192), kind=kCustom, calls=%fused_computation.3 | custom fusion | bytes 8389632 | tf_op jit(solution)/shard_map/gather | solution.py:171
  25.4 4.6 %all-to-all-start = ((bf16[8,8,2,128,128]{4,3,2,1,0:T(8,128)(2,1)}), bf16[8,8,2,128,128]{4,3,2,1,0:T(8,128)(2,1)}, u32[]{:S(2)}, u32[]{:S(2)}) async-start(bf16[8,8,2,128,128]{4,3,2,1,0:T(8,128)(2,1)} %bitcast.55), calls=%async_computation | async-start | bytes 8388608 | tf_op jit(solution)/shard_map/all_to_all | solution.py:172
  30.1 0.1 copy.21
  30.2 0.1 add.137
  30.3 2.0 %sort.35 = (s32[64]{0:T(128)}, s32[64]{0:T(128)S(1)}) sort(s32[64]{0:T(128)S(1)} %add.137, s32[64]{0:T(128)S(1)} %iota.27), dimensions={0}, to_apply=%region_1.2 | sort | flops 384 | bytes 1024 | tf_op jit(solution)/shard_map/jit(argsort)/sort | solution.py:173
  32.4 0.3 fusion.4
  32.7 47.0 %all-to-all-done = bf16[8,8,2,128,128]{4,3,2,1,0:T(8,128)(2,1)} async-done(((bf16[8,8,2,128,128]{4,3,2,1,0:T(8,128)(2,1)}), bf16[8,8,2,128,128]{4,3,2,1,0:T(8,128)(2,1)}, u32[]{:S(2)}, u32[]{:S(2)}) %all-to-all-start) | async-done | bytes 4194336 | tf_op jit(solution)/shard_map/all_to_all | solution.py:172
  79.7 5.2 %gather_fusion.4 = bf16[64,2,128,128]{3,2,1,0:T(8,128)(2,1)} fusion(bf16[64,2,128,128]{3,2,1,0:T(8,128)(2,1)} %bitcast.8, s32[1024]{0:T(1024)S(1)} %pad_clamp_fusion), kind=kCustom, calls=%fused_computation.4 | custom fusion | bytes 8388864 | tf_op jit(solution)/shard_map/jit(_take)/gather | solution.py:174
  84.9 4.9 %select_bitcast_fusion = bf16[2,128,64,128]{1,3,0,2:T(8,128)(2,1)} fusion(bf16[64,2,128,128]{3,2,1,0:T(8,128)(2,1)} %gather_fusion.4, pred[64]{0:T(512)(128)(4,1)S(1)} %compare_and_fusion.1), kind=kLoop, calls=%fused_computation.5 | loop fusion | flops 2097152 | bytes 8388672 | tf_op jit(solution)/shard_map/jit(_take)/select_n | solution.py:174
  89.8 6.4 %copy.32 = bf16[2,128,64,128]{3,1,0,2:T(8,128)(2,1)} copy(bf16[2,128,64,128]{1,3,0,2:T(8,128)(2,1)} %select_bitcast_fusion) | data formatting | bytes 8388608 | tf_op jit(solution)/shard_map/dot_general | solution.py:183
  96.2 33.9 %all-gather.2.cloned.1.call-done = bf16[8192,768]{1,0:T(8,128)(2,1)} async-done(((bf16[256,768]{1,0:T(8,128)(2,1)}), bf16[8192,768]{1,0:T(8,128)(2,1)}) %all-gather.2.cloned.1.call-update) | async-done | bytes 12582928 | tf_op jit(solution)/shard_map/all_gather | solution.py:182
  130.1 8.8 %fusion.2 = bf16[256,768]{1,0:T(8,128)(2,1)S(1)} fusion(bf16[256,64,128]{2,0,1:T(8,128)(2,1)} %bitcast.56, bf16[64,128,768]{2,1,0:T(8,128)(2,1)} %bitcast.59, pred[256]{0:T(512)(128)(4,1)S(1)} %broadcast_bitcast_fusion), kind=kOutput, calls=%fused_computation.11 | convolution fusion | flops 3221815296 | bytes 17170688 | tf_op jit(solution)/shard_map/dot_general | solution.py:183
  139.0 0.5 negate_convert_fusion
  139.5 1.9 %reshape_reshape.4.part_ref = bf16[8,4,144,128]{3,2,1,0:T(8,128)(2,1)} reshape(bf16[768,768]{1,0:T(8,128)(2,1)S(1)} %negate_convert_fusion) | data formatting | bytes 2359296 | tf_op jit(solution)/shard_map/reshape;reshape | solution.py:139
  141.4 30.5 %shard_map.77 = f32[144,128]{1,0:T(8,128)} custom-call(bf16[8,4,144,128]{3,2,1,0:T(8,128)(2,1)} %reshape_reshape.4.part_ref), custom_call_target="tpu_custom_call" | custom-call | tf_op jit(solution)/shard_map/pallas_call | solution.py:120
  171.9 0.9 reshape.167
  172.8 0.6 add_bitcast_fusion
  (41 shorter events, 0.9 us)
Async XLA Ops:
  7.2 2.2 %copy-start = (bf16[1,768,768]{2,1,0:T(8,128)(2,1)S(1)}, bf16[1,768,768]{2,1,0:T(8,128)(2,1)}, u32[]{:S(2)}) copy-start(bf16[1,768,768]{2,1,0:T(8,128)(2,1)} %param.11) | copy-start | bytes 3538948
  7.2 9.5 %copy-start.1 = (s32[128]{0:T(128)S(1)}, s32[128]{0:T(128)}, u32[]{:S(2)}) copy-start(s32[128]{0:T(128)} %param.7) | copy-start | bytes 1540
  7.2 10.6 %copy-start.4 = (s32[8,64]{1,0:T(8,128)S(1)}, s32[8,64]{1,0:T(8,128)}, u32[]{:S(2)}) copy-start(s32[8,64]{1,0:T(8,128)} %param.8) | copy-start | bytes 6148
  7.2 10.9 %copy-start.2 = (bf16[2048,512]{1,0:T(8,128)(2,1)S(1)}, bf16[2048,512]{1,0:T(8,128)(2,1)}, u32[]{:S(2)}) copy-start(bf16[2048,512]{1,0:T(8,128)(2,1)} %param.6) | copy-start | bytes 6291460
  7.2 122.9 %all-gather.2.cloned.1.call-start = ((), (), s32[]{:S(2)}) async-start(), calls=%async_computation.1 | async-start | bytes 12976128 | tf_op jit(solution)/shard_map/all_gather | solution.py:182
  25.4 54.3 %all-to-all-start = ((bf16[8,8,2,128,128]{4,3,2,1,0:T(8,128)(2,1)}), bf16[8,8,2,128,128]{4,3,2,1,0:T(8,128)(2,1)}, u32[]{:S(2)}, u32[]{:S(2)}) async-start(bf16[8,8,2,128,128]{4,3,2,1,0:T(8,128)(2,1)} %bitcast.55), calls=%async_computation | async-start | bytes 8388608 | tf_op jit(solution)/shard_map/all_to_all | solution.py:172
  130.1 8.8 %copy-start.3 = (bf16[256,768]{1,0:T(8,128)(2,1)S(1)}, bf16[256,768]{1,0:T(8,128)(2,1)}, u32[]{:S(2)}) copy-start(bf16[256,768]{1,0:T(8,128)(2,1)} %fusion.3) | copy-start | bytes 1179652
  138.9 34.5 %copy-start.5 = (bf16[256,768]{1,0:T(8,128)(2,1)}, bf16[256,768]{1,0:T(8,128)(2,1)S(1)}, u32[]{:S(2)}) copy-start(bf16[256,768]{1,0:T(8,128)(2,1)S(1)} %fusion.2) | copy-start | bytes 1179652
Sparse Core Ops, SparseCore 0:
  11.8 118.3 all-gather.1

commit v19 on v17

--- a/solution.py
+++ b/solution.py
@@ -41,13 +41,13 @@
         greet_col(k, 0)
     pl.semaphore_wait(barrier, inner + outer - 2)
 
-    own = pltpu.make_async_copy(part_ref.at[:, col], first.at[0], local_sem)
+    own = pltpu.make_async_copy(part_ref.at[col], first.at[0], local_sem)
     own.start()
 
     def stage_one(k):
         dest = lax.rem(col + k, inner)
         return pltpu.make_async_remote_copy(
-            src_ref=part_ref.at[:, dest],
+            src_ref=part_ref.at[dest],
             dst_ref=first.at[k],
             send_sem=send1.at[k],
             recv_sem=recv1.at[k],
@@ -77,7 +77,9 @@
 
     for k in range(1, inner):
         add_first(k, 0)
-    mid_out[...] = mid[...].astype(mid_out.dtype)
+    rows = mid_out.shape[1]
+    for o in range(outer):
+        mid_out[o] = mid[o * rows : (o + 1) * rows].astype(mid_out.dtype)
 
     def stage_two(k):
         dest = lax.rem(row + k, outer)
@@ -103,7 +105,7 @@
     for k in range(1, outer):
         finish_two(k, 0)
 
-    out_ref[...] = mid[row]
+    out_ref[...] = mid[pl.ds(pl.multiple_of(row * rows, 8), rows)]
 
     def add_second(k, carry):
         out_ref[...] += second[k].astype(jnp.float32)
@@ -123,8 +125,8 @@
         in_specs=[pl.BlockSpec(memory_space=pl.ANY)],
         out_specs=pl.BlockSpec(memory_space=pltpu.VMEM),
         scratch_shapes=[
-            pltpu.VMEM((inner, outer, rows, cols), part.dtype),
-            pltpu.VMEM((outer, rows, cols), jnp.float32),
+            pltpu.VMEM((inner, outer * rows, cols), part.dtype),
+            pltpu.VMEM((outer * rows, cols), jnp.float32),
             pltpu.VMEM((outer, rows, cols), part.dtype),
             pltpu.VMEM((outer, rows, cols), part.dtype),
             (
@@ -136,7 +138,7 @@
             pltpu.SemaphoreType.DMA,
         ],
         compiler_params=pltpu.CompilerParams(collective_id=0, has_side_effects=True),
-    )(part.reshape(outer, inner, rows, cols))
+    )(part.reshape(inner, outer * rows, cols))
 
 
 def per_device(anc_rows, row_home, block_lists, front_blocks, panel, pivot_inverse):
@@ -188,9 +190,13 @@
     ).reshape(rb_local * BLK, P_SIZE)
     cross = jnp.where(alive_rows[:, None], -product, jnp.zeros_like(product)).astype(jnp.bfloat16)
     pivot_rows = P_SIZE // pan_count
-    part = (-lax.dot_general(scaled, cross, contract, preferred_element_type=jnp.float32)).astype(
-        jnp.bfloat16
-    )
+    outer = pan_count // PAN_INNER
+    grid_order = jnp.transpose(
+        scaled.reshape(-1, outer, PAN_INNER, pivot_rows), (0, 2, 1, 3)
+    ).reshape(scaled.shape)
+    part = (
+        -lax.dot_general(grid_order, cross, contract, preferred_element_type=jnp.float32)
+    ).astype(jnp.bfloat16)
     shared = scatter_sum(part.reshape(pan_count, pivot_rows, P_SIZE), pan_count)
     own_columns = lax.dynamic_slice_in_dim(inverse_pivot, pan_idx * pivot_rows, pivot_rows, 1)
     triangle = lax.dot_general(

time: 180 us -> 180 us (level)
  no operation moved by 1% of the time
where the time goes in v19:
time: 180 us; the launch traced here: 179 us
  waiting for transfers between devices  80.7 us (45%)
  Pallas kernels  30.5 us (17%)
  local copies, waits for them, and re-layouts  25.3 us (14%)
  between operations  14.2 us (8%)
  matrix products  12.8 us (7%)
  other arithmetic  11.1 us (6%)
  starting transfers between devices  4.75 us (3%)
    all_to_all x1, waiting for transfers between devices, per_device(): lax.all_to_all(outgoing, 'grp', split_axis=0, concat_axis=0, tiled=True)  46.8 us
    all_gather x1, waiting for transfers between devices, per_device(): full = lax.all_gather(scaled, 'pan', axis=0, tiled=True)  33.9 us
    pallas_call x1, Pallas kernels, scatter_sum(): pl.pallas_call(functools.partial(_scatter_sum_kernel, inner, outer), out_...  30.5 us
    dot_general x1, matrix products, per_device(): lax.dot_general(sigma, full.reshape(front_len, BLK, P_SIZE), (((0, 2), (0...  8.75 us
    dot_general x1, local copies, waits for them, and re-layouts, per_device(): lax.dot_general(sigma, full.reshape(front_len, BLK, P_SIZE), (((0, 2), (0...  6.42 us
    gather x1, local copies, waits for them, and re-layouts, per_device(): jnp.take(received.reshape(groups * per_src, rb_local, BLK, BLK), order, a...  5.2 us
    select_n x2, other arithmetic, per_device(): jnp.take(received.reshape(groups * per_src, rb_local, BLK, BLK), order, a...  4.91 us
    all_to_all x1, starting transfers between devices, per_device(): lax.all_to_all(outgoing, 'grp', split_axis=0, concat_axis=0, tiled=True)  4.71 us
  transfers between devices with their start and end apart: 2, of which 2 were waited for; matrix products, arithmetic and copies ran while one was open for 18% of the time, Pallas kernels for 0%

profile of v19, /device:TPU:70, one launch (start us, length us, event | category | flops | bytes accessed | tf_op | source)
XLA Modules:
  0.0 179.4 jit_solution(12290887827812964631)
XLA Ops:
  7.3 1.4 dynamic_slice.16
  8.7 0.7 add_compare_fusion
  9.4 2.2 %fusion.3 = bf16[256,768]{1,0:T(8,128)(2,1)} fusion(bf16[1,768,768]{2,1,0:T(8,128)(2,1)S(1)} %copy-done, bf16[1,256,768]{2,1,0:T(8,128)(2,1)} %param.10, pred[256]{0:T(512)(128)(4,1)S(1)} %broadcast_bitcast_fusion), kind=kOutput, calls=%fused_computation.12 | convolution fusion | flops 302383104 | bytes 1966336 | tf_op jit(solution)/shard_map/dot_general | solution.py:182
  11.7 1.4 gather_fusion
  13.0 1.6 sort.34
  14.7 0.1 copy.22
  14.8 0.1 add.142
  15.0 0.2 dynamic-slice_reduce_fusion
  15.2 0.8 copy.25
  16.0 0.6 gather_fusion.1
  16.6 0.1 reshape.190
  16.7 0.8 gather_fusion.2
  17.6 0.1 fusion.11
  18.0 0.1 reshape.196
  18.1 2.1 %reshape.213 = bf16[16,128,4,128]{3,2,1,0:T(4,128)(2,1)} reshape(bf16[2048,512]{1,0:T(8,128)(2,1)S(1)} %copy-done.2) | data formatting | bytes 4194304 | tf_op jit(solution)/shard_map/reshape | solution.py:172
  20.2 2.1 %copy.29 = bf16[16,128,4,128]{3,1,2,0:T(8,128)(2,1)S(1)} copy(bf16[16,128,4,128]{3,2,1,0:T(4,128)(2,1)} %reshape.213) | data formatting | bytes 4194304 | tf_op jit(solution)/shard_map/reshape | solution.py:172
  22.4 3.1 %gather_fusion.3 = bf16[128,128,128]{2,1,0:T(8,128)(2,1)} fusion(bf16[16,128,4,128]{3,1,2,0:T(8,128)(2,1)S(1)} %copy.29, s32[128]{0:T(128)S(1)} %reshape.196), kind=kCustom, calls=%fused_computation.3 | custom fusion | bytes 8389632 | tf_op jit(solution)/shard_map/gather | solution.py:173
  25.4 4.7 %all-to-all-start = ((bf16[8,8,2,128,128]{4,3,2,1,0:T(8,128)(2,1)}), bf16[8,8,2,128,128]{4,3,2,1,0:T(8,128)(2,1)}, u32[]{:S(2)}, u32[]{:S(2)}) async-start(bf16[8,8,2,128,128]{4,3,2,1,0:T(8,128)(2,1)} %bitcast.60), calls=%async_computation | async-start | bytes 8388608 | tf_op jit(solution)/shard_map/all_to_all | solution.py:174
  30.2 0.2 copy.32
  30.4 0.1 copy.23
  30.5 0.1 add.137
  30.6 2.0 %sort.35 = (s32[64]{0:T(128)}, s32[64]{0:T(128)S(1)}) sort(s32[64]{0:T(128)S(1)} %add.137, s32[64]{0:T(128)S(1)} %iota.27), dimensions={0}, to_apply=%region_1.2 | sort | flops 384 | bytes 1024 | tf_op jit(solution)/shard_map/jit(argsort)/sort | solution.py:175
  32.7 0.3 fusion.4
  33.0 46.8 %all-to-all-done = bf16[8,8,2,128,128]{4,3,2,1,0:T(8,128)(2,1)} async-done(((bf16[8,8,2,128,128]{4,3,2,1,0:T(8,128)(2,1)}), bf16[8,8,2,128,128]{4,3,2,1,0:T(8,128)(2,1)}, u32[]{:S(2)}, u32[]{:S(2)}) %all-to-all-start) | async-done | bytes 4194336 | tf_op jit(solution)/shard_map/all_to_all | solution.py:174
  79.8 5.2 %gather_fusion.4 = bf16[64,2,128,128]{3,2,1,0:T(8,128)(2,1)} fusion(bf16[64,2,128,128]{3,2,1,0:T(8,128)(2,1)} %bitcast.8, s32[1024]{0:T(1024)S(1)} %pad_clamp_fusion), kind=kCustom, calls=%fused_computation.4 | custom fusion | bytes 8388864 | tf_op jit(solution)/shard_map/jit(_take)/gather | solution.py:176
  85.0 4.9 %select_bitcast_fusion = bf16[2,128,64,128]{1,3,0,2:T(8,128)(2,1)} fusion(bf16[64,2,128,128]{3,2,1,0:T(8,128)(2,1)} %gather_fusion.4, pred[64]{0:T(512)(128)(4,1)S(1)} %compare_and_fusion.1), kind=kLoop, calls=%fused_computation.5 | loop fusion | flops 2097152 | bytes 8388672 | tf_op jit(solution)/shard_map/jit(_take)/select_n | solution.py:176
  89.9 6.4 %copy.36 = bf16[2,128,64,128]{3,1,0,2:T(8,128)(2,1)} copy(bf16[2,128,64,128]{1,3,0,2:T(8,128)(2,1)} %select_bitcast_fusion) | data formatting | bytes 8388608 | tf_op jit(solution)/shard_map/dot_general | solution.py:185
  96.4 33.9 %all-gather.2.cloned.1.call-done = bf16[8192,768]{1,0:T(8,128)(2,1)} async-done(((bf16[256,768]{1,0:T(8,128)(2,1)}), bf16[8192,768]{1,0:T(8,128)(2,1)}) %all-gather.2.cloned.1.call-update) | async-done | bytes 12582928 | tf_op jit(solution)/shard_map/all_gather | solution.py:184
  130.2 8.7 %fusion.2 = bf16[256,768]{1,0:T(8,128)(2,1)S(1)} fusion(bf16[256,64,128]{2,0,1:T(8,128)(2,1)} %bitcast.62, bf16[64,128,768]{2,1,0:T(8,128)(2,1)} %bitcast.68, pred[256]{0:T(512)(128)(4,1)S(1)} %broadcast_bitcast_fusion), kind=kOutput, calls=%fused_computation.11 | convolution fusion | flops 3221815296 | bytes 17170688 | tf_op jit(solution)/shard_map/dot_general | solution.py:185
  139.0 1.5 negate_convert_fusion
  140.5 30.5 %shard_map.77 = f32[24,768]{1,0:T(8,128)} custom-call(bf16[4,192,768]{2,1,0:T(8,128)(2,1)} %bitcast.61), custom_call_target="tpu_custom_call" | custom-call | tf_op jit(solution)/shard_map/pallas_call | solution.py:122
  171.0 1.5 add_bitcast_fusion
  (41 shorter events, 0.9 us)
Async XLA Ops:
  7.2 2.2 %copy-start = (bf16[1,768,768]{2,1,0:T(8,128)(2,1)S(1)}, bf16[1,768,768]{2,1,0:T(8,128)(2,1)}, u32[]{:S(2)}) copy-start(bf16[1,768,768]{2,1,0:T(8,128)(2,1)} %param.11) | copy-start | bytes 3538948
  7.2 9.5 %copy-start.1 = (s32[128]{0:T(128)S(1)}, s32[128]{0:T(128)}, u32[]{:S(2)}) copy-start(s32[128]{0:T(128)} %param.7) | copy-start | bytes 1540
  7.2 10.6 %copy-start.5 = (s32[8,64]{1,0:T(8,128)S(1)}, s32[8,64]{1,0:T(8,128)}, u32[]{:S(2)}) copy-start(s32[8,64]{1,0:T(8,128)} %param.8) | copy-start | bytes 6148
  7.2 10.9 %copy-start.2 = (bf16[2048,512]{1,0:T(8,128)(2,1)S(1)}, bf16[2048,512]{1,0:T(8,128)(2,1)}, u32[]{:S(2)}) copy-start(bf16[2048,512]{1,0:T(8,128)(2,1)} %param.6) | copy-start | bytes 6291460
  7.2 123.0 %all-gather.2.cloned.1.call-start = ((), (), s32[]{:S(2)}) async-start(), calls=%async_computation.1 | async-start | bytes 12976128 | tf_op jit(solution)/shard_map/all_gather | solution.py:184
  25.4 4.7 %copy-start.3 = (bf16[256,768]{1,0:T(8,128)(2,1)S(1)}, bf16[256,768]{1,0:T(8,128)(2,1)}, u32[]{:S(2)}) copy-start(bf16[256,768]{1,0:T(8,128)(2,1)} %fusion.3) | copy-start | bytes 1179652
  25.4 54.4 %all-to-all-start = ((bf16[8,8,2,128,128]{4,3,2,1,0:T(8,128)(2,1)}), bf16[8,8,2,128,128]{4,3,2,1,0:T(8,128)(2,1)}, u32[]{:S(2)}, u32[]{:S(2)}) async-start(bf16[8,8,2,128,128]{4,3,2,1,0:T(8,128)(2,1)} %bitcast.60), calls=%async_computation | async-start | bytes 8388608 | tf_op jit(solution)/shard_map/all_to_all | solution.py:174
  139.0 33.6 %copy-start.4 = (bf16[256,768]{1,0:T(8,128)(2,1)}, bf16[256,768]{1,0:T(8,128)(2,1)S(1)}, u32[]{:S(2)}) copy-start(bf16[256,768]{1,0:T(8,128)(2,1)S(1)} %fusion.2) | copy-start | bytes 1179652
Sparse Core Ops, SparseCore 0:
  11.8 118.4 all-gather.1
